TPU v7x, 512 devices: a whole 4x8x8 slice. The times are simulated.
512 devices in a mesh: seq: 64 (over y, z_lo, x), blk: 8 (over z_hi, core).
Axes of the slice: x: 4, y: 8, z: 8 (z_hi: 4, z_lo: 2; z = z_hi * 2 + z_lo), core: 2. Of those that a mesh axis runs over, the one named last changes fastest.
Arguments:
- base_ids: int32 [32768], P('seq'), may hold values from 0 to 3
- span_start: int32 [4096], replicated, may hold values from 0 to 32760
- span_length: int32 [4096], replicated, may hold values from 1 to 8
- embedding: bfloat16 [5, 2048], P(None, 'blk'), may hold values from -6 to 6
- conv_kernel: bfloat16 [2, 9, 2048], P(None, None, 'blk'), may hold values from -2 to 2
- mix_weight: bfloat16 [2, 2048, 2048], P(None, 'blk'), may hold values from -0.125 to 0.125
- saved_input: bfloat16 [32768, 2048], P('seq', 'blk'), may hold values from -6 to 6
- cotangent: bfloat16 [32768, 2048], P('seq', 'blk'), may hold values from -6 to 6
Outputs:
- input_grad: bfloat16 [32768, 2048], P('seq', 'blk')
- weight_grad: float32 [2, 2048, 2048], P(None, ('blk', 'seq'))
- kernel_grad: float32 [2, 9, 2048], P(None, None, 'blk')
- embed_grad: float32 [5, 2048], P(None, 'blk')
Inputs may be any that keep to these rules, and one draw needn't show every extreme that they name: Span j masks the positions span_start[j] to span_start[j] + span_length[j] - 1, all inside the window; spans may share positions or touch.
All inputs are finite; a program needn't handle non-finite values.
Results may differ from a plain program's by a relative error of at most 0.007.
Values may be sent and summed in bfloat16 or wider, within the bound.
No kernel may reach another device: no remote copies, remote signals or barrier semaphores. Data moves between devices by JAX's collectives and lax.ppermute only.
A program may use at most 64 MiB of HBM per device.

v0:
```python
import math

import jax
import jax.numpy as jnp
from jax import lax
from jax.sharding import PartitionSpec as P

BASE_DILATION = 4


mask_token = 4
gelu_scale = 0.7978845608028654
gelu_cubic = 0.044715


def extended(cells, sides, width):
    for axis, dim in sides:
        count = lax.axis_size(axis)
        ends = count - 1
        head = lax.slice_in_dim(cells, 0, width, axis=dim)
        tail = lax.slice_in_dim(cells, cells.shape[dim] - width, cells.shape[dim], axis=dim)
        cells = jnp.concatenate(
            [
                lax.ppermute(tail, axis, [(i, (i + 1) % count) for i in range(ends)]),
                cells,
                lax.ppermute(head, axis, [((i + 1) % count, i) for i in range(ends)]),
            ],
            axis=dim,
        )
    return cells


def gelu_pair(pre_act):
    inner_arg = gelu_scale * (pre_act + gelu_cubic * pre_act * pre_act * pre_act)
    tangent = jnp.tanh(inner_arg)
    activation = 0.5 * pre_act * (1.0 + tangent)
    derivative = 0.5 * (1.0 + tangent) + 0.5 * pre_act * (1.0 - tangent * tangent) * gelu_scale * (
        1.0 + 3.0 * gelu_cubic * pre_act * pre_act
    )
    return (activation, derivative)


def tap_sum(padded, kernel, tap_spacing, row_count, flipped):
    tap_count = kernel.shape[0]
    running = jnp.zeros((row_count, padded.shape[1]), jnp.float32)
    for tap_index in range(tap_count):
        source = tap_count - 1 - tap_index if flipped else tap_index
        window = padded[source * tap_spacing : source * tap_spacing + row_count].astype(jnp.float32)
        running = running + kernel[tap_index].astype(jnp.float32) * window
    return running


def tap_products(grad_pre, padded, tap_spacing, tap_count):
    row_count = grad_pre.shape[0]
    grad_wide = grad_pre.astype(jnp.float32)
    output_rows = []
    for tap_index in range(tap_count):
        window = padded[tap_index * tap_spacing : tap_index * tap_spacing + row_count].astype(
            jnp.float32
        )
        output_rows.append(jnp.sum(grad_wide * window, axis=0))
    return jnp.stack(output_rows)


def covered_at(positions, span_start, span_length):
    span_end = span_start + span_length
    within = (positions[:, None] >= span_start[None, :]) & (positions[:, None] < span_end[None, :])
    return jnp.any(within, axis=1)


def lookup(hot_rows, table_rows):
    return jnp.einsum("vt,vc->tc", hot_rows, table_rows, preferred_element_type=jnp.float32).astype(
        jnp.bfloat16
    )


def on_device(
    base_ids, span_start, span_length, embedding, conv_kernel, mix_weight, saved_input, cotangent
):
    row_count = saved_input.shape[0]
    block_count = conv_kernel.shape[0]
    tap_count = conv_kernel.shape[1]
    taps_per_side = tap_count // 2
    vocab_rows = embedding.shape[0]
    total_rows = row_count * lax.axis_size("seq")
    grad_scale = 1.0 / math.sqrt(total_rows)
    first_row = lax.axis_index("seq") * row_count
    positions = first_row + jnp.arange(row_count, dtype=jnp.int32)
    covered = covered_at(positions, span_start, span_length)
    masked_ids = jnp.where(covered, mask_token, base_ids)
    vocab_ids = jnp.arange(vocab_rows, dtype=jnp.int32)
    one_hot = (vocab_ids[:, None] == masked_ids[None, :]).astype(jnp.bfloat16)
    initial_reach = taps_per_side * BASE_DILATION
    first_input = lookup(one_hot, embedding)
    first_padded = extended(first_input, (("seq", 0),), initial_reach)
    upstream = jnp.where(covered[:, None], cotangent, jnp.zeros_like(cotangent))
    weight_parts = [None] * block_count
    kernel_parts = [None] * block_count
    for block_number in range(block_count - 1, -1, -1):
        tap_spacing = BASE_DILATION * 2**block_number
        reach_rows = taps_per_side * tap_spacing
        if block_number == 0:
            padded_in = first_padded
        else:
            padded_in = extended(saved_input, (("seq", 0),), reach_rows)
        kernel = conv_kernel[block_number]
        weight_rows = mix_weight[block_number]
        pre_act = tap_sum(padded_in, kernel, tap_spacing, row_count, False)
        activation, derivative = gelu_pair(pre_act)
        act_half = activation.astype(jnp.bfloat16)
        column_piece = lax.all_gather(upstream, "blk", axis=1, tiled=True)
        grad_held = lax.dot_general(
            column_piece, weight_rows, (((1,), (1,)), ((), ())), preferred_element_type=jnp.float32
        )
        block_part = lax.dot_general(
            act_half, column_piece, (((0,), (0,)), ((), ())), preferred_element_type=jnp.float32
        )
        weight_part = block_part
        grad_pre = (grad_held * derivative).astype(jnp.bfloat16)
        kernel_parts[block_number] = (
            tap_products(grad_pre, padded_in, tap_spacing, tap_count) * grad_scale
        )
        padded_grad = extended(grad_pre, (("seq", 0),), reach_rows)
        upstream = (
            upstream.astype(jnp.float32)
            + tap_sum(padded_grad, kernel, tap_spacing, row_count, True)
        ).astype(jnp.bfloat16)
        weight_part = weight_part * grad_scale
        weight_parts[block_number] = lax.psum_scatter(
            weight_part, "seq", scatter_dimension=0, tiled=True
        )
    weight_grad = jnp.stack(weight_parts)
    embed_part = jnp.dot(one_hot, upstream, preferred_element_type=jnp.float32) * grad_scale
    kernel_grad, embed_grad = lax.psum((jnp.stack(kernel_parts), embed_part), "seq")
    return (upstream, weight_grad, kernel_grad, embed_grad)


def solution(mesh):
    placed = (
        P("seq"),
        P(),
        P(),
        P(None, "blk"),
        P(None, None, "blk"),
        P(None, "blk", None),
        P("seq", "blk"),
        P("seq", "blk"),
    )
    return jax.shard_map(
        on_device,
        mesh=mesh,
        in_specs=placed,
        out_specs=(
            P("seq", "blk"),
            P(None, ("blk", "seq"), None),
            P(None, None, "blk"),
            P(None, "blk"),
        ),
        check_vma=False,
    )
```

profile of v0, /device:TPU:2, one launch (start us, length us, event | category | flops | bytes accessed | tf_op | source)
XLA Modules:
  0.0 753.6 jit_solution(7351594547886416479)
XLA Ops:
  8.0 3.0 and_reduce_fusion
  11.0 1.8 broadcast_select_fusion
  13.6 3.4 collective-permute-start
  17.0 5.7 collective-permute-start.1
  23.6 1.0 constant_dynamic-update-slice_fusion
  24.6 1.3 fusion.13
  25.9 35.2 %all-gather.3.cloned.1.call-done = bf16[512,2048]{1,0:T(8,128)(2,1)} async-done(((bf16[512,256]{1,0:T(8,128)(2,1)}), bf16[512,2048]{1,0:T(8,128)(2,1)}) %all-gather.3.cloned.1.call-update) | async-done | bytes 2097168 | tf_op jit(solution)/shard_map/all_gather | solution.py:111
  61.1 3.9 fusion.47
  65.1 3.4 collective-permute-start.3
  68.4 2.5 collective-permute-start.2
  70.9 3.2 collective-permute-done.2
  74.1 1.1 fusion.38
  75.6 2.5 collective-permute-start.5
  78.1 3.4 collective-permute-start.4
  81.5 2.2 convolution_multiply_fusion
  83.6 36.3 %all-gather.5.cloned.1.call-done = bf16[512,2048]{1,0:T(8,128)(2,1)} async-done(((bf16[512,256]{1,0:T(8,128)(2,1)}), bf16[512,2048]{1,0:T(8,128)(2,1)}) %all-gather.5.cloned.1.call-update) | async-done | bytes 2097168 | tf_op jit(solution)/shard_map/all_gather | solution.py:111
  119.9 4.2 convolution_multiply_fusion.1
  124.1 1.4 dynamic-slice
  126.4 3.4 fusion.63
  129.8 3.4 collective-permute-start.7
  133.2 2.5 collective-permute-start.6
  135.8 2.9 collective-permute-done.6
  139.3 299.4 %all-reduce.2 = (f32[2,9,256]{2,0,1:T(2,128)}, f32[5,256]{1,0:T(8,128)}) all-reduce(f32[2,9,256]{2,0,1:T(2,128)S(1)} %pad_maximum_fusion.7, f32[5,256]{1,0:T(8,128)S(1)} %convolution_multiply_fusion.4), channel_id=1, replica_groups=mesh['seq'=64,'blk'=8] {'seq'}, use_global_device_ids=true, to_apply=%region_21.22 | all-reduce | flops 5888 | bytes 47104 | tf_op jit(solution)/shard_map/psum | solution.py:134
  438.7 306.9 %all-reduce.6.cloned.1.call-done = (f32[256,2048]{1,0:T(8,128)}, f32[256,2048]{1,0:T(8,128)}) async-done(((f32[256,2048]{1,0:T(8,128)}, f32[256,2048]{1,0:T(8,128)}), (f32[256,2048]{1,0:T(8,128)}, f32[256,2048]{1,0:T(8,128)})) %all-reduce.6.cloned.1.call-update) | async-done | bytes 4194320
  (68 shorter events, 5.2 us)
Async XLA Ops:
  7.2 68.1 %copy-start = (bf16[5,256]{1,0:T(8,128)(2,1)S(1)}, bf16[5,256]{1,0:T(8,128)(2,1)}, u32[]{:S(2)}) copy-start(bf16[5,256]{1,0:T(8,128)(2,1)} %param.11) | copy-start | bytes 7684
  7.2 54.0 %all-gather.3.cloned.1.call-start = ((), (), s32[]{:S(2)}) async-start(), calls=%async_computation | async-start | bytes 2359296 | tf_op jit(solution)/shard_map/all_gather | solution.py:111
  12.8 48.4 %copy-start.3 = (bf16[512,256]{1,0:T(8,128)(2,1)S(1)}, bf16[512,256]{1,0:T(8,128)(2,1)}, u32[]{:S(2)}) copy-start(bf16[512,256]{1,0:T(8,128)(2,1)} %param.14) | copy-start | bytes 786436
  12.8 107.1 %all-gather.5.cloned.1.call-start = ((), (), s32[]{:S(2)}) async-start(), calls=%async_computation.1 | async-start | bytes 2359296 | tf_op jit(solution)/shard_map/all_gather | solution.py:111
  13.6 10.0 %collective-permute-start = (bf16[32,256]{1,0:T(8,128)(2,1)S(1)}, bf16[32,256]{1,0:T(8,128)(2,1)S(1)}, u32[]{:S(2)}, u32[]{:S(2)}) collective-permute-start(bf16[32,256]{1,0:T(8,128)(2,1)S(1)} %get-tuple-element.42), channel_id=1, source_target_pairs={{0,8},{8,16},{16,24},{24,32},{32,40},{40,48},{48,56},{56,64},{64,7... | collective-permute-start | bytes 49160 | tf_op jit(solution)/shard_map/ppermute | solution.py:24
  17.0 7.6 %collective-permute-start.1 = (bf16[32,256]{1,0:T(8,128)(2,1)S(1)}, bf16[32,256]{1,0:T(8,128)(2,1)S(1)}, u32[]{:S(2)}, u32[]{:S(2)}) collective-permute-start(bf16[32,256]{1,0:T(8,128)(2,1)S(1)} %get-tuple-element.43), channel_id=1, source_target_pairs={{8,0},{16,8},{24,16},{32,24},{40,32},{48,40},{56,48},{64,56},{72,6... | collective-permute-start | bytes 49160 | tf_op jit(solution)/shard_map/ppermute | solution.py:26
  25.9 49.3 %copy-start.6 = (s32[512]{0:T(512)S(1)}, s32[512]{0:T(512)}, u32[]{:S(2)}) copy-start(s32[512]{0:T(512)} %param.8) | copy-start | bytes 6148
  61.1 12.9 %copy-start.4 = (bf16[512,256]{1,0:T(8,128)(2,1)S(1)}, bf16[512,256]{1,0:T(8,128)(2,1)}, u32[]{:S(2)}) copy-start(bf16[512,256]{1,0:T(8,128)(2,1)} %param.15) | copy-start | bytes 786436
  61.1 20.3 %copy-start.2 = (bf16[512,2048]{1,0:T(8,128)(2,1)S(1)}, bf16[512,2048]{1,0:T(8,128)(2,1)}, u32[]{:S(2)}) copy-start(bf16[512,2048]{1,0:T(8,128)(2,1)} %all-gather.3.cloned.1.call-done) | copy-start | bytes 6291460
  65.1 5.8 collective-permute-start.3
  68.4 5.6 collective-permute-start.2
  75.2 670.3 %all-reduce.6.cloned.1.call-start = ((), (), s32[]{:S(2)}) async-start(), calls=%async_computation.2 | async-start | bytes 8388608
  75.6 8.0 %collective-permute-start.5 = (bf16[16,256]{1,0:T(8,128)(2,1)S(1)}, bf16[16,256]{1,0:T(8,128)(2,1)S(1)}, u32[]{:S(2)}, u32[]{:S(2)}) collective-permute-start(bf16[16,256]{1,0:T(8,128)(2,1)S(1)} %get-tuple-element.37), channel_id=1, source_target_pairs={{8,0},{16,8},{24,16},{32,24},{40,32},{48,40},{56,48},{64,56},{72,6... | collective-permute-start | bytes 24584 | tf_op jit(solution)/shard_map/ppermute | solution.py:26
  78.1 5.6 collective-permute-start.4
  124.1 2.1 copy-start.8
  124.1 2.1 copy-start.7
  124.1 2.2 copy-start.9
  126.4 12.4 %copy-start.1 = (bf16[512,256]{1,0:T(8,128)(2,1)S(1)}, bf16[512,256]{1,0:T(8,128)(2,1)}, u32[]{:S(2)}) copy-start(bf16[512,256]{1,0:T(8,128)(2,1)} %fusion.38) | copy-start | bytes 786436
  129.8 6.0 collective-permute-start.7
  133.2 5.5 collective-permute-start.6
  139.1 607.9 %copy-start.5 = (bf16[512,256]{1,0:T(8,128)(2,1)}, bf16[512,256]{1,0:T(8,128)(2,1)S(1)}, u32[]{:S(2)}) copy-start(bf16[512,256]{1,0:T(8,128)(2,1)S(1)} %fusion.54) | copy-start | bytes 786436
Sparse Core Ops, SparseCore 0:
  12.9 48.1 all-gather.2
  75.3 44.5 all-gather.4
  124.2 621.2 all-reduce.5
where the time goes:
time: 754 us
  waiting for transfers between devices  384 us (51%)
  blocking collectives  299 us (40%)
  starting transfers between devices  26.7 us (4%)
  between operations  14.8 us (2%)
  matrix products  14.1 us (2%)
  other arithmetic  9.96 us (1%)
    unnamed x4, waiting for transfers between devices  307 us
    psum x1, blocking collectives, on_device(): lax.psum((jnp.stack(kernel_parts), embed_part), 'seq')  299 us
    all_gather x2, waiting for transfers between devices, on_device(): column_piece = lax.all_gather(upstream, 'blk', axis=1, tiled=True)  71.5 us
  transfers between devices with their start and end apart: 11, of which 5 were waited for; matrix products, arithmetic and copies ran while one was open for 2% of the time, Pallas kernels for 0%

commit v1 on v0

--- a/solution.py
+++ b/solution.py
@@ -3,10 +3,14 @@
 import jax
 import jax.numpy as jnp
 from jax import lax
-from jax.sharding import PartitionSpec as P
+from jax.sharding import Mesh, PartitionSpec as P
 
 BASE_DILATION = 4
 
+SEQ = ("y", "zl", "x")
+BLK = ("zh", "core")
+NEAR = ("zl", "x")
+FAR = ("y",)
 
 mask_token = 4
 gelu_scale = 0.7978845608028654
@@ -74,6 +78,25 @@
     )
 
 
+def scatter_sum(part):
+    near, far = lax.axis_size(NEAR), lax.axis_size(FAR)
+    rows, width = part.shape
+    own = rows // (near * far)
+    pieces = part.astype(jnp.bfloat16).reshape(far, near, own, width)
+    pieces = pieces.transpose(1, 0, 2, 3).reshape(near, far * own, width)
+    pieces = lax.all_to_all(pieces, NEAR, 0, 0)
+    half = jnp.sum(pieces.astype(jnp.float32), axis=0).astype(jnp.bfloat16)
+    pieces = lax.all_to_all(half.reshape(far, own, width), FAR, 0, 0)
+    return jnp.sum(pieces.astype(jnp.float32), axis=0)
+
+
+def whole_sum(part):
+    for axes in (NEAR, FAR):
+        copies = jnp.broadcast_to(part[None], (lax.axis_size(axes),) + part.shape)
+        part = jnp.sum(lax.all_to_all(copies, axes, 0, 0), axis=0)
+    return part
+
+
 def on_device(
     base_ids, span_start, span_length, embedding, conv_kernel, mix_weight, saved_input, cotangent
 ):
@@ -82,9 +105,9 @@
     tap_count = conv_kernel.shape[1]
     taps_per_side = tap_count // 2
     vocab_rows = embedding.shape[0]
-    total_rows = row_count * lax.axis_size("seq")
+    total_rows = row_count * lax.axis_size(SEQ)
     grad_scale = 1.0 / math.sqrt(total_rows)
-    first_row = lax.axis_index("seq") * row_count
+    first_row = lax.axis_index(SEQ) * row_count
     positions = first_row + jnp.arange(row_count, dtype=jnp.int32)
     covered = covered_at(positions, span_start, span_length)
     masked_ids = jnp.where(covered, mask_token, base_ids)
@@ -92,7 +115,7 @@
     one_hot = (vocab_ids[:, None] == masked_ids[None, :]).astype(jnp.bfloat16)
     initial_reach = taps_per_side * BASE_DILATION
     first_input = lookup(one_hot, embedding)
-    first_padded = extended(first_input, (("seq", 0),), initial_reach)
+    first_padded = extended(first_input, ((SEQ, 0),), initial_reach)
     upstream = jnp.where(covered[:, None], cotangent, jnp.zeros_like(cotangent))
     weight_parts = [None] * block_count
     kernel_parts = [None] * block_count
@@ -102,59 +125,60 @@
         if block_number == 0:
             padded_in = first_padded
         else:
-            padded_in = extended(saved_input, (("seq", 0),), reach_rows)
+            padded_in = extended(saved_input, ((SEQ, 0),), reach_rows)
         kernel = conv_kernel[block_number]
         weight_rows = mix_weight[block_number]
         pre_act = tap_sum(padded_in, kernel, tap_spacing, row_count, False)
         activation, derivative = gelu_pair(pre_act)
         act_half = activation.astype(jnp.bfloat16)
-        column_piece = lax.all_gather(upstream, "blk", axis=1, tiled=True)
+        column_piece = lax.all_gather(upstream, BLK, axis=1, tiled=True)
         grad_held = lax.dot_general(
             column_piece, weight_rows, (((1,), (1,)), ((), ())), preferred_element_type=jnp.float32
         )
         block_part = lax.dot_general(
             act_half, column_piece, (((0,), (0,)), ((), ())), preferred_element_type=jnp.float32
         )
-        weight_part = block_part
         grad_pre = (grad_held * derivative).astype(jnp.bfloat16)
         kernel_parts[block_number] = (
             tap_products(grad_pre, padded_in, tap_spacing, tap_count) * grad_scale
         )
-        padded_grad = extended(grad_pre, (("seq", 0),), reach_rows)
+        padded_grad = extended(grad_pre, ((SEQ, 0),), reach_rows)
         upstream = (
             upstream.astype(jnp.float32)
             + tap_sum(padded_grad, kernel, tap_spacing, row_count, True)
         ).astype(jnp.bfloat16)
-        weight_part = weight_part * grad_scale
-        weight_parts[block_number] = lax.psum_scatter(
-            weight_part, "seq", scatter_dimension=0, tiled=True
-        )
+        weight_parts[block_number] = scatter_sum(block_part) * grad_scale
     weight_grad = jnp.stack(weight_parts)
     embed_part = jnp.dot(one_hot, upstream, preferred_element_type=jnp.float32) * grad_scale
-    kernel_grad, embed_grad = lax.psum((jnp.stack(kernel_parts), embed_part), "seq")
+    small = jnp.concatenate(kernel_parts + [embed_part, jnp.zeros((1, embed_part.shape[1]))])
+    small = whole_sum(small)
+    split = block_count * tap_count
+    kernel_grad = small[:split].reshape(block_count, tap_count, -1)
+    embed_grad = small[split : split + vocab_rows]
     return (upstream, weight_grad, kernel_grad, embed_grad)
 
 
 def solution(mesh):
+    fine = Mesh(mesh.devices.reshape(8, 2, 4, 4, 2), SEQ + BLK)
     placed = (
-        P("seq"),
+        P(SEQ),
         P(),
         P(),
-        P(None, "blk"),
-        P(None, None, "blk"),
-        P(None, "blk", None),
-        P("seq", "blk"),
-        P("seq", "blk"),
+        P(None, BLK),
+        P(None, None, BLK),
+        P(None, BLK, None),
+        P(SEQ, BLK),
+        P(SEQ, BLK),
     )
     return jax.shard_map(
         on_device,
-        mesh=mesh,
+        mesh=fine,
         in_specs=placed,
         out_specs=(
-            P("seq", "blk"),
-            P(None, ("blk", "seq"), None),
-            P(None, None, "blk"),
-            P(None, "blk"),
+            P(SEQ, BLK),
+            P(None, BLK + SEQ, None),
+            P(None, None, BLK),
+            P(None, BLK),
         ),
         check_vma=False,
     )

time: 754 us -> 204 us (0.27)
  the two profiles are of different devices: /device:TPU:2 before, /device:TPU:64 now
where the time goes in v1:
time: 204 us; the launch traced here: 203 us
  waiting for transfers between devices  86.7 us (42%)
  starting transfers between devices  66.8 us (33%)
  between operations  14.4 us (7%)
  matrix products  12.2 us (6%)
  other arithmetic  11.5 us (6%)
  local copies, waits for them, and re-layouts  11.2 us (5%)
    all_gather x2, waiting for transfers between devices, on_device(): column_piece = lax.all_gather(upstream, BLK, axis=1, tiled=True)  32 us
    all_to_all x2, waiting for transfers between devices, scatter_sum(): pieces = lax.all_to_all(pieces, NEAR, 0, 0)  26.2 us
    ppermute x4, starting transfers between devices, extended(): lax.ppermute(head, axis, [((i + 1) % count, i) for i in range(ends)])  23.4 us
    all_to_all x2, starting transfers between devices, scatter_sum(): pieces = lax.all_to_all(half.reshape(far, own, width), FAR, 0, 0)  12.7 us
    ppermute x4, waiting for transfers between devices, extended(): lax.ppermute(tail, axis, [(i, (i + 1) % count) for i in range(ends)])  11.5 us
    all_to_all x2, starting transfers between devices, whole_sum(): part = jnp.sum(lax.all_to_all(copies, axes, 0, 0), axis=0)  11.3 us
    ppermute x4, starting transfers between devices, extended(): lax.ppermute(tail, axis, [(i, (i + 1) % count) for i in range(ends)])  10.4 us
    all_to_all x2, waiting for transfers between devices, whole_sum(): part = jnp.sum(lax.all_to_all(copies, axes, 0, 0), axis=0)  9.25 us
  transfers between devices with their start and end apart: 16, of which 7 were waited for; matrix products, arithmetic and copies ran while one was open for 11% of the time, Pallas kernels for 0%

profile of v1, /device:TPU:64, one launch (start us, length us, event | category | flops | bytes accessed | tf_op | source)
XLA Modules:
  0.0 202.7 jit_solution(17671131964420875736)
XLA Ops:
  8.0 3.0 %and_reduce_fusion = pred[512]{0:T(512)(128)(4,1)S(1)} fusion(s32[4096]{0:T(1024)S(1)} %add.151, s32[4096]{0:T(1024)} %param.9, s32[512]{0:T(512)S(1)} %iota_add_fusion), kind=kLoop, calls=%fused_computation | loop fusion | flops 8388096 | bytes 35328 | tf_op jit(solution)/shard_map/reduce_or | solution.py:72
  13.6 3.4 %collective-permute-start = (bf16[32,256]{1,0:T(8,128)(2,1)S(1)}, bf16[32,256]{1,0:T(8,128)(2,1)S(1)}, u32[]{:S(2)}, u32[]{:S(2)}) collective-permute-start(bf16[32,256]{1,0:T(8,128)(2,1)S(1)} %get-tuple-element.62), channel_id=1, source_target_pairs={{0,8},{8,16},{16,24},{24,32},{32,40},{40,48},{48,56},{56,64},{64,7... | collective-permute-start | bytes 49160 | tf_op jit(solution)/shard_map/ppermute | solution.py:28
  17.0 4.6 %collective-permute-start.1 = (bf16[32,256]{1,0:T(8,128)(2,1)S(1)}, bf16[32,256]{1,0:T(8,128)(2,1)S(1)}, u32[]{:S(2)}, u32[]{:S(2)}) collective-permute-start(bf16[32,256]{1,0:T(8,128)(2,1)S(1)} %get-tuple-element.63), channel_id=1, source_target_pairs={{8,0},{16,8},{24,16},{32,24},{40,32},{48,40},{56,48},{64,56},{72,6... | collective-permute-start | bytes 49160 | tf_op jit(solution)/shard_map/ppermute | solution.py:30
  23.5 2.1 %fusion.13 = f32[512,256]{1,0:T(8,128)} fusion(bf16[512,256]{1,0:T(8,128)(2,1)} %param.14, f32[256]{0:T(256)S(1)} %bitcast.67, f32[256]{0:T(256)S(1)} %bitcast.69, f32[256]{0:T(256)S(1)} %bitcast.71, f32[256]{0:T(256)S(1)} %bitcast.73, f32[256]{0:T(256)S(1)} %bitcast.75, f32[256]{0:T(256)S(1)} %bitcast.77, f32[256]{0:T(256)S(1)} %bitcast.79, ...), kind=kLoop, calls=%fused_computation.62 | loop fusion | flops 3407872 | bytes 2892800 | tf_op jit(solution)/shard_map/add | solution.py:53
  25.6 32.0 %all-gather.3.cloned.1.call-done = bf16[512,2048]{1,0:T(8,128)(2,1)} async-done(((bf16[512,256]{1,0:T(8,128)(2,1)}), bf16[512,2048]{1,0:T(8,128)(2,1)}) %all-gather.3.cloned.1.call-update) | async-done | bytes 2097168 | tf_op jit(solution)/shard_map/all_gather | solution.py:134
  57.5 3.5 %fusion.47 = (f32[256]{0:T(256)S(1)}, f32[256]{0:T(256)S(1)}, f32[256]{0:T(256)S(1)}, f32[256]{0:T(256)S(1)}, f32[256]{0:T(256)S(1)}, /*index=5*/f32[256]{0:T(25...) fusion(bf16[544,256]{1,0:T(8,128)(2,1)S(1)} %constant_dynamic-update-slice_fusion.2, ...), kind=kOutput, calls=%fused_computation.96 | convolution fusion | flops 543028992 | bytes 6300672 | tf_op jit(solution)/shard_map/dot_general | solution.py:135
  61.0 7.3 %collective-permute-start.2 = (bf16[32,256]{1,0:T(8,128)(2,1)S(1)}, bf16[32,256]{1,0:T(8,128)(2,1)S(1)}, u32[]{:S(2)}, u32[]{:S(2)}) collective-permute-start(bf16[32,256]{1,0:T(8,128)(2,1)S(1)} %get-tuple-element.58), channel_id=1, source_target_pairs={{8,0},{16,8},{24,16},{32,24},{40,32},{48,40},{56,48},{64,56},{72,6... | collective-permute-start | bytes 49160 | tf_op jit(solution)/shard_map/ppermute | solution.py:30
  70.3 5.8 %collective-permute-done.3 = bf16[32,256]{1,0:T(8,128)(2,1)S(1)} collective-permute-done((bf16[32,256]{1,0:T(8,128)(2,1)S(1)}, bf16[32,256]{1,0:T(8,128)(2,1)S(1)}, u32[]{:S(2)}, u32[]{:S(2)}) %collective-permute-start.3) | collective-permute-done | bytes 16416 | tf_op jit(solution)/shard_map/ppermute | solution.py:28
  81.7 3.5 %all-to-all-start.2 = ((bf16[8,32,2048]{2,1,0:T(8,128)(2,1)}), bf16[8,32,2048]{2,1,0:T(8,128)(2,1)S(1)}, u32[]{:S(2)}, u32[]{:S(2)}) async-start(bf16[8,32,2048]{2,1,0:T(8,128)(2,1)} %copy.43), calls=%async_computation.2 | async-start | bytes 2097152 | tf_op jit(solution)/shard_map/all_to_all | solution.py:87
  85.6 3.1 %collective-permute-start.4 = (bf16[16,256]{1,0:T(8,128)(2,1)S(1)}, bf16[16,256]{1,0:T(8,128)(2,1)S(1)}, u32[]{:S(2)}, u32[]{:S(2)}) collective-permute-start(bf16[16,256]{1,0:T(8,128)(2,1)S(1)} %get-tuple-element.56), channel_id=1, source_target_pairs={{0,8},{8,16},{16,24},{24,32},{32,40},{40,48},{48,56},{56,64},{64,7... | collective-permute-start | bytes 24584 | tf_op jit(solution)/shard_map/ppermute | solution.py:28
  88.7 4.8 %collective-permute-start.5 = (bf16[16,256]{1,0:T(8,128)(2,1)S(1)}, bf16[16,256]{1,0:T(8,128)(2,1)S(1)}, u32[]{:S(2)}, u32[]{:S(2)}) collective-permute-start(bf16[16,256]{1,0:T(8,128)(2,1)S(1)} %get-tuple-element.57), channel_id=1, source_target_pairs={{8,0},{16,8},{24,16},{32,24},{40,32},{48,40},{56,48},{64,56},{72,6... | collective-permute-start | bytes 24584 | tf_op jit(solution)/shard_map/ppermute | solution.py:30
  93.7 13.6 %all-to-all-done.2 = bf16[8,32,2048]{2,1,0:T(8,128)(2,1)S(1)} async-done(((bf16[8,32,2048]{2,1,0:T(8,128)(2,1)}), bf16[8,32,2048]{2,1,0:T(8,128)(2,1)S(1)}, u32[]{:S(2)}, u32[]{:S(2)}) %all-to-all-start.2) | async-done | bytes 1048608 | tf_op jit(solution)/shard_map/all_to_all | solution.py:87
  108.1 9.4 %all-to-all-start.3 = ((bf16[8,4,2048]{2,1,0:T(4,128)(2,1)}), bf16[8,4,2048]{2,1,0:T(4,128)(2,1)S(1)}, u32[]{:S(2)}, u32[]{:S(2)}) async-start(bf16[8,4,2048]{2,1,0:T(4,128)(2,1)} %reshape.224), calls=%async_computation.3 | async-start | bytes 262144 | tf_op jit(solution)/shard_map/all_to_all | solution.py:89
  117.5 3.6 %fusion.63 = (f32[256]{0:T(256)S(1)}, f32[256]{0:T(256)S(1)}, f32[256]{0:T(256)S(1)}, f32[256]{0:T(256)S(1)}, f32[256]{0:T(256)S(1)}, /*index=5*/f32[256]{0:T(25...) fusion(bf16[16,256]{1,0:T(8,128)(2,1)S(1)} %collective-permute-done.5, ...), kind=kOutput, calls=%fused_computation.112 | convolution fusion | flops 551548672 | bytes 3704832 | tf_op jit(solution)/shard_map/dot_general | solution.py:135
  121.2 6.7 %collective-permute-start.6 = (bf16[16,256]{1,0:T(8,128)(2,1)S(1)}, bf16[16,256]{1,0:T(8,128)(2,1)S(1)}, u32[]{:S(2)}, u32[]{:S(2)}) collective-permute-start(bf16[16,256]{1,0:T(8,128)(2,1)S(1)} %get-tuple-element.54), channel_id=1, source_target_pairs={{8,0},{16,8},{24,16},{32,24},{40,32},{48,40},{56,48},{64,56},{72,6... | collective-permute-start | bytes 24584 | tf_op jit(solution)/shard_map/ppermute | solution.py:30
  129.9 5.7 %collective-permute-done.7 = bf16[16,256]{1,0:T(8,128)(2,1)S(1)} collective-permute-done((bf16[16,256]{1,0:T(8,128)(2,1)S(1)}, bf16[16,256]{1,0:T(8,128)(2,1)S(1)}, u32[]{:S(2)}, u32[]{:S(2)}) %collective-permute-start.7) | collective-permute-done | bytes 8224 | tf_op jit(solution)/shard_map/ppermute | solution.py:28
  137.0 3.5 %all-to-all-start.4 = ((f32[8,24,256]{2,1,0:T(8,128)}), f32[8,24,256]{2,1,0:T(8,128)S(1)}, u32[]{:S(2)}, u32[]{:S(2)}) async-start(f32[8,24,256]{2,1,0:T(8,128)} %broadcast_in_dim.24), calls=%async_computation.4 | async-start | bytes 393216 | tf_op jit(solution)/shard_map/all_to_all | solution.py:96
  140.5 2.8 %convolution_convert_fusion.1 = bf16[256,2048]{1,0:T(8,128)(2,1)S(1)} fusion(bf16[512,2048]{1,0:T(8,128)(2,1)} %all-gather.5.cloned.1.call-done, bf16[512,256]{1,0:T(8,128)(2,1)S(1)} %convolution_convert_fusion.2, bf16[16,256]{1,0:T(8,128)(2,1)S(1)} %collective-permute-done.5, bf16[16,256]{1,0:T(8,128)(2,1)S(1)} %collective-permute-done.4, ...), kind=kOutput, calls=%fused_computation.2 | convolution fusion | flops 545128448 | bytes 3433472 | tf_op jit(solution)/shard_map/dot_general | solution.py:138
  145.9 5.5 %all-to-all-start = ((bf16[8,32,2048]{2,1,0:T(8,128)(2,1)}), bf16[8,32,2048]{2,1,0:T(8,128)(2,1)S(1)}, u32[]{:S(2)}, u32[]{:S(2)}) async-start(bf16[8,32,2048]{2,1,0:T(8,128)(2,1)} %copy.40), calls=%async_computation | async-start | bytes 2097152 | tf_op jit(solution)/shard_map/all_to_all | solution.py:87
  151.4 12.7 %all-to-all-done = bf16[8,32,2048]{2,1,0:T(8,128)(2,1)S(1)} async-done(((bf16[8,32,2048]{2,1,0:T(8,128)(2,1)}), bf16[8,32,2048]{2,1,0:T(8,128)(2,1)S(1)}, u32[]{:S(2)}, u32[]{:S(2)}) %all-to-all-start) | async-done | bytes 1048608 | tf_op jit(solution)/shard_map/all_to_all | solution.py:87
  164.7 7.7 %all-to-all-start.5 = ((f32[8,24,256]{2,1,0:T(8,128)}), f32[8,24,256]{2,1,0:T(8,128)S(1)}, u32[]{:S(2)}, u32[]{:S(2)}) async-start(f32[8,24,256]{2,1,0:T(8,128)} %broadcast_in_dim.25), calls=%async_computation.5 | async-start | bytes 393216 | tf_op jit(solution)/shard_map/all_to_all | solution.py:96
  173.4 9.2 %all-to-all-done.5 = f32[8,24,256]{2,1,0:T(8,128)S(1)} async-done(((f32[8,24,256]{2,1,0:T(8,128)}), f32[8,24,256]{2,1,0:T(8,128)S(1)}, u32[]{:S(2)}, u32[]{:S(2)}) %all-to-all-start.5) | async-done | bytes 196640 | tf_op jit(solution)/shard_map/all_to_all | solution.py:96
  182.7 3.4 %all-to-all-start.1 = ((bf16[8,4,2048]{2,1,0:T(4,128)(2,1)}), bf16[8,4,2048]{2,1,0:T(4,128)(2,1)S(1)}, u32[]{:S(2)}, u32[]{:S(2)}) async-start(bf16[8,4,2048]{2,1,0:T(4,128)(2,1)} %reshape.221), calls=%async_computation.1 | async-start | bytes 262144 | tf_op jit(solution)/shard_map/all_to_all | solution.py:89
  187.3 7.7 %all-to-all-done.1 = bf16[8,4,2048]{2,1,0:T(4,128)(2,1)S(1)} async-done(((bf16[8,4,2048]{2,1,0:T(4,128)(2,1)}), bf16[8,4,2048]{2,1,0:T(4,128)(2,1)S(1)}, u32[]{:S(2)}, u32[]{:S(2)}) %all-to-all-start.1) | async-done | bytes 131104 | tf_op jit(solution)/shard_map/all_to_all | solution.py:89
  (73 shorter events, 23.8 us)
Async XLA Ops:
  7.2 78.1 %copy-start = (bf16[5,256]{1,0:T(8,128)(2,1)S(1)}, bf16[5,256]{1,0:T(8,128)(2,1)}, u32[]{:S(2)}) copy-start(bf16[5,256]{1,0:T(8,128)(2,1)} %param.11) | copy-start | bytes 7684
  7.2 50.3 %all-gather.3.cloned.1.call-start = ((), (), s32[]{:S(2)}) async-start(), calls=%async_computation.6 | async-start | bytes 2359296 | tf_op jit(solution)/shard_map/all_gather | solution.py:134
  12.8 44.7 %copy-start.3 = (bf16[512,256]{1,0:T(8,128)(2,1)S(1)}, bf16[512,256]{1,0:T(8,128)(2,1)}, u32[]{:S(2)}) copy-start(bf16[512,256]{1,0:T(8,128)(2,1)} %param.14) | copy-start | bytes 786436
  12.8 104.7 %all-gather.5.cloned.1.call-start = ((), (), s32[]{:S(2)}) async-start(), calls=%async_computation.7 | async-start | bytes 2359296 | tf_op jit(solution)/shard_map/all_gather | solution.py:134
  13.6 8.8 %collective-permute-start = (bf16[32,256]{1,0:T(8,128)(2,1)S(1)}, bf16[32,256]{1,0:T(8,128)(2,1)S(1)}, u32[]{:S(2)}, u32[]{:S(2)}) collective-permute-start(bf16[32,256]{1,0:T(8,128)(2,1)S(1)} %get-tuple-element.62), channel_id=1, source_target_pairs={{0,8},{8,16},{16,24},{24,32},{32,40},{40,48},{48,56},{56,64},{64,7... | collective-permute-start | bytes 49160 | tf_op jit(solution)/shard_map/ppermute | solution.py:28
  17.0 6.4 %collective-permute-start.1 = (bf16[32,256]{1,0:T(8,128)(2,1)S(1)}, bf16[32,256]{1,0:T(8,128)(2,1)S(1)}, u32[]{:S(2)}, u32[]{:S(2)}) collective-permute-start(bf16[32,256]{1,0:T(8,128)(2,1)S(1)} %get-tuple-element.63), channel_id=1, source_target_pairs={{8,0},{16,8},{24,16},{32,24},{40,32},{48,40},{56,48},{64,56},{72,6... | collective-permute-start | bytes 49160 | tf_op jit(solution)/shard_map/ppermute | solution.py:30
  25.6 50.5 %copy-start.4 = (bf16[512,256]{1,0:T(8,128)(2,1)S(1)}, bf16[512,256]{1,0:T(8,128)(2,1)}, u32[]{:S(2)}) copy-start(bf16[512,256]{1,0:T(8,128)(2,1)} %param.15) | copy-start | bytes 786436
  57.5 19.7 %copy-start.2 = (bf16[512,2048]{1,0:T(8,128)(2,1)S(1)}, bf16[512,2048]{1,0:T(8,128)(2,1)}, u32[]{:S(2)}) copy-start(bf16[512,2048]{1,0:T(8,128)(2,1)} %all-gather.3.cloned.1.call-done) | copy-start | bytes 6291460
  61.0 9.3 %collective-permute-start.2 = (bf16[32,256]{1,0:T(8,128)(2,1)S(1)}, bf16[32,256]{1,0:T(8,128)(2,1)S(1)}, u32[]{:S(2)}, u32[]{:S(2)}) collective-permute-start(bf16[32,256]{1,0:T(8,128)(2,1)S(1)} %get-tuple-element.58), channel_id=1, source_target_pairs={{8,0},{16,8},{24,16},{32,24},{40,32},{48,40},{56,48},{64,56},{72,6... | collective-permute-start | bytes 49160 | tf_op jit(solution)/shard_map/ppermute | solution.py:30
  68.4 7.7 %collective-permute-start.3 = (bf16[32,256]{1,0:T(8,128)(2,1)S(1)}, bf16[32,256]{1,0:T(8,128)(2,1)S(1)}, u32[]{:S(2)}, u32[]{:S(2)}) collective-permute-start(bf16[32,256]{1,0:T(8,128)(2,1)S(1)} %get-tuple-element.59), channel_id=1, source_target_pairs={{0,8},{8,16},{16,24},{24,32},{32,40},{40,48},{48,56},{56,64},{64,7... | collective-permute-start | bytes 49160 | tf_op jit(solution)/shard_map/ppermute | solution.py:28
  80.2 5.1 %copy-start.6 = (s32[512]{0:T(512)S(1)}, s32[512]{0:T(512)}, u32[]{:S(2)}) copy-start(s32[512]{0:T(512)} %param.8) | copy-start | bytes 6148
  81.7 25.5 %all-to-all-start.2 = ((bf16[8,32,2048]{2,1,0:T(8,128)(2,1)}), bf16[8,32,2048]{2,1,0:T(8,128)(2,1)S(1)}, u32[]{:S(2)}, u32[]{:S(2)}) async-start(bf16[8,32,2048]{2,1,0:T(8,128)(2,1)} %copy.43), calls=%async_computation.2 | async-start | bytes 2097152 | tf_op jit(solution)/shard_map/all_to_all | solution.py:87
  85.6 31.9 %collective-permute-start.4 = (bf16[16,256]{1,0:T(8,128)(2,1)S(1)}, bf16[16,256]{1,0:T(8,128)(2,1)S(1)}, u32[]{:S(2)}, u32[]{:S(2)}) collective-permute-start(bf16[16,256]{1,0:T(8,128)(2,1)S(1)} %get-tuple-element.56), channel_id=1, source_target_pairs={{0,8},{8,16},{16,24},{24,32},{32,40},{40,48},{48,56},{56,64},{64,7... | collective-permute-start | bytes 24584 | tf_op jit(solution)/shard_map/ppermute | solution.py:28
  88.7 28.7 %collective-permute-start.5 = (bf16[16,256]{1,0:T(8,128)(2,1)S(1)}, bf16[16,256]{1,0:T(8,128)(2,1)S(1)}, u32[]{:S(2)}, u32[]{:S(2)}) collective-permute-start(bf16[16,256]{1,0:T(8,128)(2,1)S(1)} %get-tuple-element.57), channel_id=1, source_target_pairs={{8,0},{16,8},{24,16},{32,24},{40,32},{48,40},{56,48},{64,56},{72,6... | collective-permute-start | bytes 24584 | tf_op jit(solution)/shard_map/ppermute | solution.py:30
  108.1 28.1 %all-to-all-start.3 = ((bf16[8,4,2048]{2,1,0:T(4,128)(2,1)}), bf16[8,4,2048]{2,1,0:T(4,128)(2,1)S(1)}, u32[]{:S(2)}, u32[]{:S(2)}) async-start(bf16[8,4,2048]{2,1,0:T(4,128)(2,1)} %reshape.224), calls=%async_computation.3 | async-start | bytes 262144 | tf_op jit(solution)/shard_map/all_to_all | solution.py:89
  117.5 18.1 %copy-start.1 = (bf16[512,256]{1,0:T(8,128)(2,1)S(1)}, bf16[512,256]{1,0:T(8,128)(2,1)}, u32[]{:S(2)}) copy-start(bf16[512,256]{1,0:T(8,128)(2,1)} %fusion.38) | copy-start | bytes 786436
  121.2 8.7 %collective-permute-start.6 = (bf16[16,256]{1,0:T(8,128)(2,1)S(1)}, bf16[16,256]{1,0:T(8,128)(2,1)S(1)}, u32[]{:S(2)}, u32[]{:S(2)}) collective-permute-start(bf16[16,256]{1,0:T(8,128)(2,1)S(1)} %get-tuple-element.54), channel_id=1, source_target_pairs={{8,0},{16,8},{24,16},{32,24},{40,32},{48,40},{56,48},{64,56},{72,6... | collective-permute-start | bytes 24584 | tf_op jit(solution)/shard_map/ppermute | solution.py:30
  127.9 7.7 %collective-permute-start.7 = (bf16[16,256]{1,0:T(8,128)(2,1)S(1)}, bf16[16,256]{1,0:T(8,128)(2,1)S(1)}, u32[]{:S(2)}, u32[]{:S(2)}) collective-permute-start(bf16[16,256]{1,0:T(8,128)(2,1)S(1)} %get-tuple-element.55), channel_id=1, source_target_pairs={{0,8},{8,16},{16,24},{24,32},{32,40},{40,48},{48,56},{56,64},{64,7... | collective-permute-start | bytes 24584 | tf_op jit(solution)/shard_map/ppermute | solution.py:28
  136.0 7.2 %copy-start.5 = (bf16[512,256]{1,0:T(8,128)(2,1)}, bf16[512,256]{1,0:T(8,128)(2,1)S(1)}, u32[]{:S(2)}) copy-start(bf16[512,256]{1,0:T(8,128)(2,1)S(1)} %fusion.54) | copy-start | bytes 786436
  137.0 8.9 %all-to-all-start.4 = ((f32[8,24,256]{2,1,0:T(8,128)}), f32[8,24,256]{2,1,0:T(8,128)S(1)}, u32[]{:S(2)}, u32[]{:S(2)}) async-start(f32[8,24,256]{2,1,0:T(8,128)} %broadcast_in_dim.24), calls=%async_computation.4 | async-start | bytes 393216 | tf_op jit(solution)/shard_map/all_to_all | solution.py:96
  145.9 18.1 %all-to-all-start = ((bf16[8,32,2048]{2,1,0:T(8,128)(2,1)}), bf16[8,32,2048]{2,1,0:T(8,128)(2,1)S(1)}, u32[]{:S(2)}, u32[]{:S(2)}) async-start(bf16[8,32,2048]{2,1,0:T(8,128)(2,1)} %copy.40), calls=%async_computation | async-start | bytes 2097152 | tf_op jit(solution)/shard_map/all_to_all | solution.py:87
  164.7 18.0 %all-to-all-start.5 = ((f32[8,24,256]{2,1,0:T(8,128)}), f32[8,24,256]{2,1,0:T(8,128)S(1)}, u32[]{:S(2)}, u32[]{:S(2)}) async-start(f32[8,24,256]{2,1,0:T(8,128)} %broadcast_in_dim.25), calls=%async_computation.5 | async-start | bytes 393216 | tf_op jit(solution)/shard_map/all_to_all | solution.py:96
  182.7 12.4 %all-to-all-start.1 = ((bf16[8,4,2048]{2,1,0:T(4,128)(2,1)}), bf16[8,4,2048]{2,1,0:T(4,128)(2,1)S(1)}, u32[]{:S(2)}, u32[]{:S(2)}) async-start(bf16[8,4,2048]{2,1,0:T(4,128)(2,1)} %reshape.221), calls=%async_computation.1 | async-start | bytes 262144 | tf_op jit(solution)/shard_map/all_to_all | solution.py:89
Sparse Core Ops, SparseCore 0:
  12.9 44.5 all-gather.2
  77.4 37.2 all-gather.4

commit v2 on v1

v2 whole, which is shorter than its diff:
```python
import functools
import math

import jax
import jax.numpy as jnp
from jax import lax
from jax.experimental import pallas as pl
from jax.experimental.pallas import tpu as pltpu
from jax.sharding import Mesh, PartitionSpec as P

BASE_DILATION = 4

SEQ = ("y", "zl", "x")
BLK = ("zh", "core")
NEAR = ("zl", "x")
FAR = ("y",)

mask_token = 4
gelu_scale = 0.7978845608028654
gelu_cubic = 0.044715
LANES = 256
SMALL_ROWS = 16
ID_ROWS = 16


def gelu_pair(pre_act):
    inner_arg = gelu_scale * (pre_act + gelu_cubic * pre_act * pre_act * pre_act)
    tangent = jnp.tanh(inner_arg)
    activation = 0.5 * pre_act * (1.0 + tangent)
    derivative = 0.5 * (1.0 + tangent) + 0.5 * pre_act * (1.0 - tangent * tangent) * gelu_scale * (
        1.0 + 3.0 * gelu_cubic * pre_act * pre_act
    )
    return (activation, derivative)


def tap_sum(padded, kernel, tap_spacing, row_count, flipped):
    tap_count = kernel.shape[0]
    running = jnp.zeros((row_count, padded.shape[1]), jnp.float32)
    for tap_index in range(tap_count):
        source = tap_count - 1 - tap_index if flipped else tap_index
        window = padded[source * tap_spacing : source * tap_spacing + row_count].astype(jnp.float32)
        running = running + kernel[tap_index].astype(jnp.float32) * window
    return running


def tap_products(grad_pre, padded, tap_spacing, tap_count):
    row_count = grad_pre.shape[0]
    grad_wide = grad_pre.astype(jnp.float32)
    output_rows = []
    for tap_index in range(tap_count):
        window = padded[tap_index * tap_spacing : tap_index * tap_spacing + row_count].astype(
            jnp.float32
        )
        output_rows.append(jnp.sum(grad_wide * window, axis=0))
    return jnp.stack(output_rows)


def covered_at(positions, span_start, span_length):
    span_end = span_start + span_length
    within = (positions[:, None] >= span_start[None, :]) & (positions[:, None] < span_end[None, :])
    return jnp.any(within, axis=1)


def seq_shift(cells, step):
    count = lax.axis_size(SEQ)
    if step > 0:
        return lax.ppermute(cells, SEQ, [(i, i + 1) for i in range(count - 1)])
    return lax.ppermute(cells, SEQ, [(i + 1, i) for i in range(count - 1)])


def ring_copies(slab):
    count = lax.axis_size("zh")
    moved = [slab]
    for step in (1, 3, 2):
        moved.append(lax.ppermute(slab, "zh", [(i, (i + step) % count) for i in range(count)]))
    return moved


def core_swap(cells):
    return lax.ppermute(cells, "core", [(0, 1), (1, 0)])


def block_order():
    ring = lax.axis_size("zh")
    here, core = lax.axis_index("zh"), lax.axis_index("core")
    steps = jnp.array([0, 1, 3, 2], jnp.int32)
    chips = (here - steps) % ring
    return jnp.concatenate([chips * 2 + core, chips * 2 + 1 - core])


def ordered_weights(weight_rows, order):
    blocks = weight_rows.reshape(LANES, -1, LANES).transpose(1, 2, 0)
    return jnp.take(blocks, order, axis=0)


def product_over_blocks(mine, other, weights):
    half = mine.shape[0]
    total = None
    for index in range(2 * half):
        piece = mine[index] if index < half else other[index - half]
        term = jnp.dot(piece, weights[index], preferred_element_type=jnp.float32)
        total = term if total is None else total + term
    return total


def upper_kernel(mine, other, weights, slope, base, taps, grad_out, up_out, wide):
    rows = base.shape[0]
    reach = (slope.shape[0] - rows) // 2
    grad = product_over_blocks(mine, other, weights) * slope[...]
    grad = grad.astype(jnp.bfloat16)
    grad_out[...] = grad[:rows]
    grad = grad.astype(jnp.float32)
    wide[reach : reach + rows] = grad[:rows]
    wide[:reach] = grad[rows : rows + reach]
    wide[reach + rows :] = grad[rows + reach :]
    running = base[...]
    count = taps.shape[0]
    spacing = reach // (count // 2)
    for index in range(count):
        start = (count - 1 - index) * spacing
        running = running + taps[index : index + 1] * wide[start : start + rows]
    up_out[...] = running.astype(jnp.bfloat16)


def lower_kernel(mine, other, weights, slope, hot, up_row, table, taps, grad_out, small_out):
    grad = (product_over_blocks(mine, other, weights) * slope[...]).astype(jnp.bfloat16)
    grad_out[...] = grad
    count = taps.shape[0]
    picked = jnp.dot(hot[...], grad, preferred_element_type=jnp.float32)
    middle = count // 2
    embed = jnp.dot(
        hot[middle * 8 : middle * 8 + 8], up_row[...], preferred_element_type=jnp.float32
    )
    small_out[...] = jnp.zeros_like(small_out)
    for index in range(count):
        piece = picked[index * 8 : index * 8 + 8]
        small_out[index : index + 1] = jnp.sum(piece * table[...], axis=0, keepdims=True)
        embed = embed + piece * taps[index : index + 1]
    small_out[count : count + 5] = embed[:5]


def outer_kernel(act, mine, other, small, out):
    rows = act.shape[1]
    half = mine.shape[0]
    for index in range(2 * half):
        piece = mine[index, :rows] if index < half else other[index - half, :rows]
        out[:, index * LANES : (index + 1) * LANES] = jnp.dot(
            act[...], piece, preferred_element_type=jnp.float32
        ).astype(jnp.bfloat16)
    extra = small[...].astype(jnp.bfloat16)
    extra = jnp.concatenate([extra, jnp.zeros_like(extra)], axis=0)
    group = 2 * small.shape[0]
    for index in range(act.shape[0] // group):
        out[index * group : (index + 1) * group, 2 * half * LANES :] = extra


def call(kernel, outs, scratch, *operands):
    return pl.pallas_call(
        kernel,
        out_shape=outs,
        scratch_shapes=scratch,
        compiler_params=pltpu.CompilerParams(vmem_limit_bytes=32 << 20),
    )(*operands)


def scatter_first(outer):
    near = lax.axis_size(NEAR)
    pieces = outer.reshape(near, outer.shape[0] // near, outer.shape[1])
    return lax.all_to_all(pieces, NEAR, 0, 0)


def scatter_second(pieces, scale):
    far = lax.axis_size(FAR)
    total = jnp.sum(pieces.astype(jnp.float32), axis=0)
    rows = total.shape[0]
    own = rows // far
    width = total.shape[1] - LANES
    main = total[:, :width].astype(jnp.bfloat16).reshape(far, own, width)
    small = total[:SMALL_ROWS, width:].astype(jnp.bfloat16).reshape(1, own, -1)
    small = jnp.broadcast_to(small, (far,) + small.shape[1:])
    pieces = lax.all_to_all(jnp.concatenate([main, small], axis=2), FAR, 0, 0)
    total = jnp.sum(pieces.astype(jnp.float32), axis=0) * scale
    return total[:, :width], total[:, width:].reshape(SMALL_ROWS, LANES)


def on_device(
    base_ids, span_start, span_length, embedding, conv_kernel, mix_weight, saved_input, cotangent
):
    rows = saved_input.shape[0]
    tap_count = conv_kernel.shape[1]
    side = tap_count // 2
    vocab_rows = embedding.shape[0]
    total_rows = rows * lax.axis_size(SEQ)
    grad_scale = 1.0 / math.sqrt(total_rows)
    low_gap, high_gap = BASE_DILATION, 2 * BASE_DILATION
    low_reach, high_reach = side * low_gap, side * high_gap
    bf16, f32 = jnp.bfloat16, jnp.float32

    gathered = ring_copies(cotangent)

    def edge(lo, hi, cut):
        ids = jnp.broadcast_to(base_ids[cut].astype(bf16)[:, None], (ID_ROWS, LANES))
        return jnp.concatenate([saved_input[lo], cotangent[hi], ids])

    wide_edge, thin_edge = 2 * high_reach, high_reach
    to_next = edge(
        slice(rows - wide_edge, rows), slice(rows - thin_edge, rows), slice(rows - ID_ROWS, rows)
    )
    to_prev = edge(slice(0, wide_edge), slice(0, thin_edge), slice(0, ID_ROWS))
    before = seq_shift(to_next, 1)
    after = seq_shift(to_prev, -1)

    edges = jnp.concatenate(
        [before[wide_edge : wide_edge + thin_edge], after[wide_edge : wide_edge + thin_edge]]
    )
    edges_gathered = ring_copies(edges)
    mine = jnp.stack(
        [jnp.concatenate([a, b], axis=0) for a, b in zip(gathered, edges_gathered)]
    )
    other = core_swap(mine)

    first_row = lax.axis_index(SEQ) * rows
    positions = first_row - high_reach + jnp.arange(rows + 2 * high_reach, dtype=jnp.int32)
    covered = covered_at(positions, span_start, span_length)
    inner = covered[high_reach : high_reach + rows]

    def edge_last(cells):
        return jnp.concatenate(
            [cells[high_reach : high_reach + rows], cells[:high_reach], cells[high_reach + rows :]]
        )

    order = block_order()
    upper_weights = ordered_weights(mix_weight[1], order)
    lower_weights = ordered_weights(mix_weight[0], order)
    kernel_wide = conv_kernel.astype(f32)

    channel = jnp.arange(LANES, dtype=jnp.int32)
    near, far = lax.axis_size(NEAR), lax.axis_size(FAR)
    own = LANES // (near * far)
    place = (channel // own % near) * (far * own) + channel // (own * near) * own + channel % own
    shuffle = (place[None, :] == channel[:, None]).astype(bf16)

    saved_wide = jnp.concatenate([before[:wide_edge], saved_input, after[:wide_edge]])
    pre_upper = tap_sum(saved_wide, conv_kernel[1], high_gap, rows + 2 * high_reach, False)
    act_upper, slope_upper = gelu_pair(pre_upper)
    slope_upper = edge_last(jnp.where(covered[:, None], slope_upper, 0.0))
    act_upper = jnp.where(
        inner[:, None], act_upper[high_reach : high_reach + rows].astype(bf16), jnp.zeros((), bf16)
    )
    act_upper = jnp.einsum("pc,tc->pt", shuffle, act_upper, preferred_element_type=f32).astype(bf16)
    masked = jnp.where(inner[:, None], cotangent, jnp.zeros_like(cotangent)).astype(f32)

    near_positions = positions[high_reach - low_reach : high_reach + rows + low_reach]
    near_covered = covered[high_reach - low_reach : high_reach + rows + low_reach]
    ids = jnp.concatenate(
        [
            before[wide_edge + thin_edge :, 0].astype(jnp.int32),
            base_ids,
            after[wide_edge + thin_edge :, 0].astype(jnp.int32),
        ]
    )
    ids = jnp.where(near_covered, mask_token, ids)
    ids = jnp.where((near_positions >= 0) & (near_positions < total_rows), ids, 7)
    hot = (jnp.arange(8, dtype=jnp.int32)[:, None] == ids[None, :]).astype(bf16)
    hot = jnp.where(jnp.arange(8)[:, None] < vocab_rows, hot, jnp.zeros((), bf16))
    table = jnp.concatenate([embedding, jnp.zeros((8 - vocab_rows, LANES), bf16)])
    first_wide = jnp.einsum("vt,vc->tc", hot, table, preferred_element_type=f32).astype(bf16)
    pre_lower = tap_sum(first_wide, conv_kernel[0], low_gap, rows, False)
    act_lower, slope_lower = gelu_pair(pre_lower)
    act_lower = jnp.einsum(
        "pc,tc->pt", shuffle, act_lower.astype(bf16), preferred_element_type=f32
    ).astype(bf16)
    hot_taps = jnp.concatenate(
        [hot[:, index * low_gap : index * low_gap + rows] for index in range(tap_count)]
    )

    (
        slope_upper,
        act_upper,
        slope_lower,
        act_lower,
        upper_weights,
        lower_weights,
        masked,
        hot_taps,
        mine,
    ) = lax.optimization_barrier(
        (
            slope_upper,
            act_upper,
            slope_lower,
            act_lower,
            upper_weights,
            lower_weights,
            masked,
            hot_taps,
            mine,
        )
    )

    slab = jax.ShapeDtypeStruct((rows, LANES), bf16)
    small_shape = jax.ShapeDtypeStruct((SMALL_ROWS, LANES), f32)
    outer_shape = jax.ShapeDtypeStruct((LANES, 9 * LANES), bf16)
    grad_upper, up_mid = call(
        upper_kernel,
        (slab, slab),
        [pltpu.VMEM((rows + 2 * high_reach, LANES), f32)],
        mine, other, upper_weights, slope_upper, masked, kernel_wide[1],
    )

    mid_gathered = jnp.stack(ring_copies(up_mid))
    mid_other = core_swap(mid_gathered)

    upper_taps = tap_products(
        grad_upper, saved_wide[high_reach : rows + 3 * high_reach], high_gap, tap_count
    )
    upper_small = jnp.concatenate([upper_taps, jnp.zeros((SMALL_ROWS - tap_count, LANES), f32)])
    upper_outer = call(outer_kernel, outer_shape, [], act_upper, mine, other, upper_small)
    upper_grad, upper_small = scatter_second(scatter_first(upper_outer), grad_scale)

    grad_lower, lower_small = call(
        lower_kernel,
        (slab, small_shape),
        [],
        mid_gathered, mid_other, lower_weights, slope_lower, hot_taps, up_mid,
        table.astype(f32), kernel_wide[0],
    )
    lower_outer = call(
        outer_kernel, outer_shape, [], act_lower, mid_gathered, mid_other, lower_small
    )
    lower_grad, lower_small = scatter_second(scatter_first(lower_outer), grad_scale)

    padded = jnp.concatenate(
        [
            seq_shift(grad_lower[rows - low_reach :], 1),
            grad_lower,
            seq_shift(grad_lower[:low_reach], -1),
        ]
    )
    input_grad = (
        up_mid.astype(f32) + tap_sum(padded, conv_kernel[0], low_gap, rows, True)
    ).astype(bf16)

    blocks = jnp.stack([lower_grad, upper_grad]).reshape(2, own, -1, LANES)
    spots = jnp.argsort(order)
    weight_grad = jnp.take(blocks, spots, axis=2).reshape(2, own, -1)
    kernel_grad = jnp.stack([lower_small[:tap_count], upper_small[:tap_count]])
    embed_grad = lower_small[tap_count : tap_count + vocab_rows]
    return (input_grad, weight_grad, kernel_grad, embed_grad)


def solution(mesh):
    fine = Mesh(mesh.devices.reshape(8, 2, 4, 4, 2), SEQ + BLK)
    placed = (
        P(SEQ),
        P(),
        P(),
        P(None, BLK),
        P(None, None, BLK),
        P(None, BLK, None),
        P(SEQ, BLK),
        P(SEQ, BLK),
    )
    return jax.shard_map(
        on_device,
        mesh=fine,
        in_specs=placed,
        out_specs=(
            P(SEQ, BLK),
            P(None, BLK + SEQ, None),
            P(None, None, BLK),
            P(None, BLK),
        ),
        check_vma=False,
    )
```

time: 204 us -> 199 us (0.975)
  waiting for transfers between devices: 86.7 us -> 54.5 us
  starting transfers between devices: 66.8 us -> 84.3 us
  other arithmetic: 11.5 us -> 27.7 us
  between operations: 14.4 us -> 1.47 us
  local copies, waits for them, and re-layouts: 11.2 us -> 21.3 us
  matrix products: 12.2 us -> 2.47 us
  Pallas kernels: 0 us -> 5.53 us
    all_gather x2 -> x0, waiting for transfers between devices: 32 us -> none  [on_device(): column_piece = lax.all_gather(upstream, BLK, axis=1, tiled=True)]
    all_to_all x6 -> x4, waiting for transfers between devices: 43.2 us -> 16.4 us  [the longest x2 16.4 us: scatter_second(): pieces = lax.all_to_all(jnp.concatenate([main, small], axis=2), FAR, 0, 0)]
    ppermute x8 -> x15, waiting for transfers between devices: 11.5 us -> 38.2 us  [the longest x9 30.3 us: ring_copies(): lax.ppermute(slab, 'zh', [(i, (i + step) % count) for i in range(count)])]
    ppermute x8 -> x15, starting transfers between devices: 33.8 us -> 60 us  [the longest x9 41.7 us: ring_copies(): lax.ppermute(slab, 'zh', [(i, (i + step) % count) for i in range(count)])]
    dot_general x6 -> x3, matrix products: 12.2 us -> 2.47 us  [the longest x1 1.09 us: on_device(): jnp.einsum('pc,tc->pt', shuffle, act_lower.astype(bf16), preferred_elemen...]
    slice x5 -> x23, local copies, waits for them, and re-layouts: 1.36 us -> 10.3 us  [the longest x2 2.2 us: on_device(): lower_weights = ordered_weights(mix_weight[0], order)]
    all_to_all x6 -> x4, starting transfers between devices: 33 us -> 24.2 us  [the longest x2 13.8 us: scatter_first(): return lax.all_to_all(pieces, NEAR, 0, 0)]
    pallas_call x0 -> x4, Pallas kernels: none -> 5.53 us  [call(): pl.pallas_call(kernel, out_shape=outs, scratch_shapes=scratch, compiler_p...]
  transfers between devices with their start and end apart: 16 -> 19, of which waited for: 7 -> 7; matrix products, arithmetic and copies ran while one was open for 11% -> 20% of each run, Pallas kernels for 0% -> 1%
where the time goes in v2:
time: 199 us; the launch traced here: 197 us
  starting transfers between devices  84.3 us (42%)
  waiting for transfers between devices  54.5 us (27%)
  other arithmetic  27.7 us (14%)
  local copies, waits for them, and re-layouts  21.3 us (11%)
  Pallas kernels  5.53 us (3%)
  matrix products  2.47 us (1%)
    ppermute x9, starting transfers between devices, ring_copies(): lax.ppermute(slab, 'zh', [(i, (i + step) % count) for i in range(count)])  41.7 us
    ppermute x9, waiting for transfers between devices, ring_copies(): lax.ppermute(slab, 'zh', [(i, (i + step) % count) for i in range(count)])  30.3 us
    all_to_all x2, waiting for transfers between devices, scatter_second(): pieces = lax.all_to_all(jnp.concatenate([main, small], axis=2), FAR, 0, 0)  16.4 us
    all_to_all x2, starting transfers between devices, scatter_first(): return lax.all_to_all(pieces, NEAR, 0, 0)  13.8 us
    all_to_all x2, starting transfers between devices, scatter_second(): pieces = lax.all_to_all(jnp.concatenate([main, small], axis=2), FAR, 0, 0)  10.5 us
    ppermute x2, starting transfers between devices, seq_shift(): return lax.ppermute(cells, SEQ, [(i + 1, i) for i in range(count - 1)])  9.22 us
    ppermute x2, waiting for transfers between devices, seq_shift(): return lax.ppermute(cells, SEQ, [(i, i + 1) for i in range(count - 1)])  7.83 us
    pallas_call x4, Pallas kernels, call(): pl.pallas_call(kernel, out_shape=outs, scratch_shapes=scratch, compiler_p...  5.53 us
  transfers between devices with their start and end apart: 19, of which 7 were waited for; matrix products, arithmetic and copies ran while one was open for 20% of the time, Pallas kernels for 1%

profile of v2, /device:TPU:64, one launch (start us, length us, event | category | flops | bytes accessed | tf_op | source)
XLA Modules:
  0.0 197.3 jit_solution(4242232365956426066)
XLA Ops:
  0.6 6.1 %collective-permute-start.2 = (bf16[512,256]{1,0:T(8,128)(2,1)}, bf16[512,256]{1,0:T(8,128)(2,1)}, u32[]{:S(2)}, u32[]{:S(2)}) collective-permute-start(bf16[512,256]{1,0:T(8,128)(2,1)} %param.18), channel_id=1, source_target_pairs={{0,2},{2,4},{4,6},{6,0},{1,3},{3,5},{5,7},{7,1},{8,10},{10,12},{12... | collective-permute-start | bytes 786440 | tf_op jit(solution)/shard_map/ppermute | solution.py:75
  6.7 5.9 %collective-permute-start.4 = (bf16[512,256]{1,0:T(8,128)(2,1)}, bf16[512,256]{1,0:T(8,128)(2,1)}, u32[]{:S(2)}, u32[]{:S(2)}) collective-permute-start(bf16[512,256]{1,0:T(8,128)(2,1)} %param.18), channel_id=1, source_target_pairs={{0,6},{2,0},{4,2},{6,4},{1,7},{3,1},{5,3},{7,5},{8,14},{10,8},{12,... | collective-permute-start | bytes 786440 | tf_op jit(solution)/shard_map/ppermute | solution.py:75
  12.6 6.0 %collective-permute-start.6 = (bf16[512,256]{1,0:T(8,128)(2,1)}, bf16[512,256]{1,0:T(8,128)(2,1)}, u32[]{:S(2)}, u32[]{:S(2)}) collective-permute-start(bf16[512,256]{1,0:T(8,128)(2,1)} %param.18), channel_id=1, source_target_pairs={{0,4},{2,6},{4,0},{6,2},{1,5},{3,7},{5,1},{7,3},{8,12},{10,14},{12... | collective-permute-start | bytes 786440 | tf_op jit(solution)/shard_map/ppermute | solution.py:75
  21.7 4.6 %collective-permute-start.1 = (bf16[112,256]{1,0:T(8,128)(2,1)}, bf16[112,256]{1,0:T(8,128)(2,1)}, u32[]{:S(2)}, u32[]{:S(2)}) collective-permute-start(bf16[112,256]{1,0:T(8,128)(2,1)} %maximum_maximum_fusion.1), channel_id=1, source_target_pairs={{8,0},{16,8},{24,16},{32,24},{40,32},{48,40},{56,48},{64,56},{72,6... | collective-permute-start | bytes 172040 | tf_op jit(solution)/shard_map/ppermute | solution.py:68
  32.6 3.3 %and_reduce_fusion = pred[576]{0:T(1024)(128)(4,1)S(1)} fusion(s32[4096]{0:T(1024)S(1)} %add.199, s32[4096]{0:T(1024)} %param.12, s32[576]{0:T(1024)S(1)} %iota_add_fusion), kind=kLoop, calls=%fused_computation.3 | loop fusion | flops 9436608 | bytes 35648 | tf_op jit(solution)/shard_map/reduce_or | solution.py:61
  44.6 3.1 %collective-permute-start.3 = (bf16[64,256]{1,0:T(8,128)(2,1)S(1)}, bf16[64,256]{1,0:T(8,128)(2,1)S(1)}, u32[]{:S(2)}, u32[]{:S(2)}) collective-permute-start(bf16[64,256]{1,0:T(8,128)(2,1)S(1)} %pad_maximum_fusion.9), channel_id=1, source_target_pairs={{0,2},{2,4},{4,6},{6,0},{1,3},{3,5},{5,7},{7,1},{8,10},{10,12},{12... | collective-permute-start | bytes 98312 | tf_op jit(solution)/shard_map/ppermute | solution.py:75
  47.7 4.9 %collective-permute-start.5 = (bf16[64,256]{1,0:T(8,128)(2,1)S(1)}, bf16[64,256]{1,0:T(8,128)(2,1)S(1)}, u32[]{:S(2)}, u32[]{:S(2)}) collective-permute-start(bf16[64,256]{1,0:T(8,128)(2,1)S(1)} %pad_maximum_fusion.9), channel_id=1, source_target_pairs={{0,6},{2,0},{4,2},{6,4},{1,7},{3,1},{5,3},{7,5},{8,14},{10,8},{12,... | collective-permute-start | bytes 98312 | tf_op jit(solution)/shard_map/ppermute | solution.py:75
  57.8 3.7 %collective-permute-start.7 = (bf16[64,256]{1,0:T(8,128)(2,1)S(1)}, bf16[64,256]{1,0:T(8,128)(2,1)S(1)}, u32[]{:S(2)}, u32[]{:S(2)}) collective-permute-start(bf16[64,256]{1,0:T(8,128)(2,1)S(1)} %pad_maximum_fusion.9), channel_id=1, source_target_pairs={{0,4},{2,6},{4,0},{6,2},{1,5},{3,7},{5,1},{7,3},{8,12},{10,14},{12... | collective-permute-start | bytes 98312 | tf_op jit(solution)/shard_map/ppermute | solution.py:75
  63.6 4.0 %collective-permute-done.7 = bf16[64,256]{1,0:T(8,128)(2,1)S(1)} collective-permute-done((bf16[64,256]{1,0:T(8,128)(2,1)S(1)}, bf16[64,256]{1,0:T(8,128)(2,1)S(1)}, u32[]{:S(2)}, u32[]{:S(2)}) %collective-permute-start.7) | collective-permute-done | bytes 32800 | tf_op jit(solution)/shard_map/ppermute | solution.py:75
  68.7 1.9 collective-permute-start.8
  81.7 7.9 %all-to-all-start.2 = ((bf16[8,32,2304]{2,1,0:T(8,128)(2,1)}), bf16[8,32,2304]{2,1,0:T(8,128)(2,1)}, u32[]{:S(2)}, u32[]{:S(2)}) async-start(bf16[8,32,2304]{2,1,0:T(8,128)(2,1)} %bitcast.43), calls=%async_computation.2 | async-start | bytes 2359296 | tf_op jit(solution)/shard_map/all_to_all | solution.py:169
  91.5 6.0 %collective-permute-start.10 = (bf16[512,256]{1,0:T(8,128)(2,1)S(1)}, bf16[512,256]{1,0:T(8,128)(2,1)S(1)}, u32[]{:S(2)}, u32[]{:S(2)}) collective-permute-start(bf16[512,256]{1,0:T(8,128)(2,1)S(1)} %copy-done.1), channel_id=1, source_target_pairs={{0,6},{2,0},{4,2},{6,4},{1,7},{3,1},{5,3},{7,5},{8,14},{10,8},{12,... | collective-permute-start | bytes 786440 | tf_op jit(solution)/shard_map/ppermute | solution.py:75
  97.5 4.1 %collective-permute-start.11 = (bf16[512,256]{1,0:T(8,128)(2,1)S(1)}, bf16[512,256]{1,0:T(8,128)(2,1)S(1)}, u32[]{:S(2)}, u32[]{:S(2)}) collective-permute-start(bf16[512,256]{1,0:T(8,128)(2,1)S(1)} %copy-done.1), channel_id=1, source_target_pairs={{0,4},{2,6},{4,0},{6,2},{1,5},{3,7},{5,1},{7,3},{8,12},{10,14},{12... | collective-permute-start | bytes 786440 | tf_op jit(solution)/shard_map/ppermute | solution.py:75
  101.8 18.5 %collective-permute-done.10 = bf16[512,256]{1,0:T(8,128)(2,1)S(1)} collective-permute-done((bf16[512,256]{1,0:T(8,128)(2,1)S(1)}, bf16[512,256]{1,0:T(8,128)(2,1)S(1)}, u32[]{:S(2)}, u32[]{:S(2)}) %collective-permute-start.10) | collective-permute-done | bytes 262176 | tf_op jit(solution)/shard_map/ppermute | solution.py:75
  120.3 7.6 %collective-permute-done.11 = bf16[512,256]{1,0:T(8,128)(2,1)S(1)} collective-permute-done((bf16[512,256]{1,0:T(8,128)(2,1)S(1)}, bf16[512,256]{1,0:T(8,128)(2,1)S(1)}, u32[]{:S(2)}, u32[]{:S(2)}) %collective-permute-start.11) | collective-permute-done | bytes 262176 | tf_op jit(solution)/shard_map/ppermute | solution.py:75
  130.0 2.1 %reduce.1 = bf16[32,2304]{1,0:T(8,128)(2,1)} reduce(bf16[8,32,2304]{2,1,0:T(8,128)(2,1)} %all-to-all-done.2, bf16[]{:T(256)} %constant.144.clone.1), dimensions={0}, to_apply=%region_13.15.clone | reduce | flops 516096 | bytes 1327106 | tf_op jit(solution)/shard_map/reduce_sum | solution.py:174
  137.7 7.1 %all-to-all-start.3 = ((bf16[8,4,3072]{2,1,0:T(4,128)(2,1)}), bf16[8,4,3072]{2,1,0:T(4,128)(2,1)}, u32[]{:S(2)}, u32[]{:S(2)}) async-start(bf16[8,4,3072]{2,1,0:T(4,128)(2,1)} %pad_maximum_fusion.7), calls=%async_computation.3 | async-start | bytes 393216 | tf_op jit(solution)/shard_map/all_to_all | solution.py:181
  149.3 6.7 %all-to-all-done.3 = bf16[8,4,3072]{2,1,0:T(4,128)(2,1)} async-done(((bf16[8,4,3072]{2,1,0:T(4,128)(2,1)}), bf16[8,4,3072]{2,1,0:T(4,128)(2,1)}, u32[]{:S(2)}, u32[]{:S(2)}) %all-to-all-start.3) | async-done | bytes 196640 | tf_op jit(solution)/shard_map/all_to_all | solution.py:181
  156.1 5.9 %all-to-all-start = ((bf16[8,32,2304]{2,1,0:T(8,128)(2,1)}), bf16[8,32,2304]{2,1,0:T(8,128)(2,1)S(1)}, u32[]{:S(2)}, u32[]{:S(2)}) async-start(bf16[8,32,2304]{2,1,0:T(8,128)(2,1)} %bitcast.32), calls=%async_computation | async-start | bytes 2359296 | tf_op jit(solution)/shard_map/all_to_all | solution.py:169
  161.9 3.4 %collective-permute-start.14 = (bf16[16,256]{1,0:T(8,128)(2,1)S(1)}, bf16[16,256]{1,0:T(8,128)(2,1)S(1)}, u32[]{:S(2)}, u32[]{:S(2)}) collective-permute-start(bf16[16,256]{1,0:T(8,128)(2,1)S(1)} %get-tuple-element.89), channel_id=1, source_target_pairs={{0,8},{8,16},{16,24},{24,32},{32,40},{40,48},{48,56},{56,64},{64,7... | collective-permute-start | bytes 24584 | tf_op jit(solution)/shard_map/ppermute | solution.py:67
  165.4 4.6 %collective-permute-start.13 = (bf16[16,256]{1,0:T(8,128)(2,1)S(1)}, bf16[16,256]{1,0:T(8,128)(2,1)S(1)}, u32[]{:S(2)}, u32[]{:S(2)}) collective-permute-start(bf16[16,256]{1,0:T(8,128)(2,1)S(1)} %get-tuple-element.88), channel_id=1, source_target_pairs={{8,0},{16,8},{24,16},{32,24},{40,32},{48,40},{56,48},{64,56},{72,6... | collective-permute-start | bytes 24584 | tf_op jit(solution)/shard_map/ppermute | solution.py:68
  170.0 7.8 %collective-permute-done.14 = bf16[16,256]{1,0:T(8,128)(2,1)S(1)} collective-permute-done((bf16[16,256]{1,0:T(8,128)(2,1)S(1)}, bf16[16,256]{1,0:T(8,128)(2,1)S(1)}, u32[]{:S(2)}, u32[]{:S(2)}) %collective-permute-start.14) | collective-permute-done | bytes 8224 | tf_op jit(solution)/shard_map/ppermute | solution.py:67
  181.3 3.4 %all-to-all-start.1 = ((bf16[8,4,3072]{2,1,0:T(4,128)(2,1)}), bf16[8,4,3072]{2,1,0:T(4,128)(2,1)S(1)}, u32[]{:S(2)}, u32[]{:S(2)}) async-start(bf16[8,4,3072]{2,1,0:T(4,128)(2,1)} %pad_maximum_fusion.6), calls=%async_computation.1 | async-start | bytes 393216 | tf_op jit(solution)/shard_map/all_to_all | solution.py:181
  184.8 9.6 %all-to-all-done.1 = bf16[8,4,3072]{2,1,0:T(4,128)(2,1)S(1)} async-done(((bf16[8,4,3072]{2,1,0:T(4,128)(2,1)}), bf16[8,4,3072]{2,1,0:T(4,128)(2,1)S(1)}, u32[]{:S(2)}, u32[]{:S(2)}) %all-to-all-start.1) | async-done | bytes 196640 | tf_op jit(solution)/shard_map/all_to_all | solution.py:181
  (189 shorter events, 57.6 us)
Async XLA Ops:
  0.6 60.9 %collective-permute-start.2 = (bf16[512,256]{1,0:T(8,128)(2,1)}, bf16[512,256]{1,0:T(8,128)(2,1)}, u32[]{:S(2)}, u32[]{:S(2)}) collective-permute-start(bf16[512,256]{1,0:T(8,128)(2,1)} %param.18), channel_id=1, source_target_pairs={{0,2},{2,4},{4,6},{6,0},{1,3},{3,5},{5,7},{7,1},{8,10},{10,12},{12... | collective-permute-start | bytes 786440 | tf_op jit(solution)/shard_map/ppermute | solution.py:75
  6.7 55.8 %collective-permute-start.4 = (bf16[512,256]{1,0:T(8,128)(2,1)}, bf16[512,256]{1,0:T(8,128)(2,1)}, u32[]{:S(2)}, u32[]{:S(2)}) collective-permute-start(bf16[512,256]{1,0:T(8,128)(2,1)} %param.18), channel_id=1, source_target_pairs={{0,6},{2,0},{4,2},{6,4},{1,7},{3,1},{5,3},{7,5},{8,14},{10,8},{12,... | collective-permute-start | bytes 786440 | tf_op jit(solution)/shard_map/ppermute | solution.py:75
  12.6 54.9 %collective-permute-start.6 = (bf16[512,256]{1,0:T(8,128)(2,1)}, bf16[512,256]{1,0:T(8,128)(2,1)}, u32[]{:S(2)}, u32[]{:S(2)}) collective-permute-start(bf16[512,256]{1,0:T(8,128)(2,1)} %param.18), channel_id=1, source_target_pairs={{0,4},{2,6},{4,0},{6,2},{1,5},{3,7},{5,1},{7,3},{8,12},{10,14},{12... | collective-permute-start | bytes 786440 | tf_op jit(solution)/shard_map/ppermute | solution.py:75
  21.7 22.2 %collective-permute-start.1 = (bf16[112,256]{1,0:T(8,128)(2,1)}, bf16[112,256]{1,0:T(8,128)(2,1)}, u32[]{:S(2)}, u32[]{:S(2)}) collective-permute-start(bf16[112,256]{1,0:T(8,128)(2,1)} %maximum_maximum_fusion.1), channel_id=1, source_target_pairs={{8,0},{16,8},{24,16},{32,24},{40,32},{48,40},{56,48},{64,56},{72,6... | collective-permute-start | bytes 172040 | tf_op jit(solution)/shard_map/ppermute | solution.py:68
  27.2 16.0 %collective-permute-start = (bf16[112,256]{1,0:T(8,128)(2,1)}, bf16[112,256]{1,0:T(8,128)(2,1)}, u32[]{:S(2)}, u32[]{:S(2)}) collective-permute-start(bf16[112,256]{1,0:T(8,128)(2,1)} %maximum_maximum_fusion), channel_id=1, source_target_pairs={{0,8},{8,16},{16,24},{24,32},{32,40},{40,48},{48,56},{56,64},{64,7... | collective-permute-start | bytes 172040 | tf_op jit(solution)/shard_map/ppermute | solution.py:67
  31.1 40.0 %copy-start.11 = (f32[1,1,256]{2,0,1:T(1,128)}, f32[1,1,256]{2,0,1:T(1,128)S(1)}, u32[]{:S(2)}) copy-start(f32[1,1,256]{2,0,1:T(1,128)S(1)} %get-tuple-element.105) | copy-start | bytes 3076
  31.1 40.0 %copy-start.13 = (f32[1,1,256]{2,0,1:T(1,128)}, f32[1,1,256]{2,0,1:T(1,128)S(1)}, u32[]{:S(2)}) copy-start(f32[1,1,256]{2,0,1:T(1,128)S(1)} %get-tuple-element.115) | copy-start | bytes 3076
  42.8 13.6 %copy-start.16 = (f32[1,1,256]{2,0,1:T(1,128)S(1)}, f32[1,1,256]{2,0,1:T(1,128)}, u32[]{:S(2)}) copy-start(f32[1,1,256]{2,0,1:T(1,128)} %get-tuple-element.106) | copy-start | bytes 3076
  44.6 13.2 %collective-permute-start.3 = (bf16[64,256]{1,0:T(8,128)(2,1)S(1)}, bf16[64,256]{1,0:T(8,128)(2,1)S(1)}, u32[]{:S(2)}, u32[]{:S(2)}) collective-permute-start(bf16[64,256]{1,0:T(8,128)(2,1)S(1)} %pad_maximum_fusion.9), channel_id=1, source_target_pairs={{0,2},{2,4},{4,6},{6,0},{1,3},{3,5},{5,7},{7,1},{8,10},{10,12},{12... | collective-permute-start | bytes 98312 | tf_op jit(solution)/shard_map/ppermute | solution.py:75
  47.7 14.9 %collective-permute-start.5 = (bf16[64,256]{1,0:T(8,128)(2,1)S(1)}, bf16[64,256]{1,0:T(8,128)(2,1)S(1)}, u32[]{:S(2)}, u32[]{:S(2)}) collective-permute-start(bf16[64,256]{1,0:T(8,128)(2,1)S(1)} %pad_maximum_fusion.9), channel_id=1, source_target_pairs={{0,6},{2,0},{4,2},{6,4},{1,7},{3,1},{5,3},{7,5},{8,14},{10,8},{12,... | collective-permute-start | bytes 98312 | tf_op jit(solution)/shard_map/ppermute | solution.py:75
  57.8 9.7 %collective-permute-start.7 = (bf16[64,256]{1,0:T(8,128)(2,1)S(1)}, bf16[64,256]{1,0:T(8,128)(2,1)S(1)}, u32[]{:S(2)}, u32[]{:S(2)}) collective-permute-start(bf16[64,256]{1,0:T(8,128)(2,1)S(1)} %pad_maximum_fusion.9), channel_id=1, source_target_pairs={{0,4},{2,6},{4,0},{6,2},{1,5},{3,7},{5,1},{7,3},{8,12},{10,14},{12... | collective-permute-start | bytes 98312 | tf_op jit(solution)/shard_map/ppermute | solution.py:75
  68.7 6.1 %collective-permute-start.8 = (bf16[4,576,256]{2,1,0:T(8,128)(2,1)S(1)}, bf16[4,576,256]{2,1,0:T(8,128)(2,1)S(1)}, u32[]{:S(2)}, u32[]{:S(2)}) collective-permute-start(bf16[4,576,256]{2,1,0:T(8,128)(2,1)S(1)} %pad_maximum_fusion.mine), channel_id=1, source_target_pairs={{0,1},{1,0},{2,3},{3,2},{4,5},{5,4},{6,7},{7,6},{8,9},{9,8},{10,11... | collective-permute-start | bytes 3538952 | tf_op jit(solution)/shard_map/ppermute | solution.py:80
  81.7 48.3 %all-to-all-start.2 = ((bf16[8,32,2304]{2,1,0:T(8,128)(2,1)}), bf16[8,32,2304]{2,1,0:T(8,128)(2,1)}, u32[]{:S(2)}, u32[]{:S(2)}) async-start(bf16[8,32,2304]{2,1,0:T(8,128)(2,1)} %bitcast.43), calls=%async_computation.2 | async-start | bytes 2359296 | tf_op jit(solution)/shard_map/all_to_all | solution.py:169
  89.6 12.2 %collective-permute-start.9 = (bf16[512,256]{1,0:T(8,128)(2,1)S(1)}, bf16[512,256]{1,0:T(8,128)(2,1)S(1)}, u32[]{:S(2)}, u32[]{:S(2)}) collective-permute-start(bf16[512,256]{1,0:T(8,128)(2,1)S(1)} %copy-done.1), channel_id=1, source_target_pairs={{0,2},{2,4},{4,6},{6,0},{1,3},{3,5},{5,7},{7,1},{8,10},{10,12},{12... | collective-permute-start | bytes 786440 | tf_op jit(solution)/shard_map/ppermute | solution.py:75
  91.5 28.9 %collective-permute-start.10 = (bf16[512,256]{1,0:T(8,128)(2,1)S(1)}, bf16[512,256]{1,0:T(8,128)(2,1)S(1)}, u32[]{:S(2)}, u32[]{:S(2)}) collective-permute-start(bf16[512,256]{1,0:T(8,128)(2,1)S(1)} %copy-done.1), channel_id=1, source_target_pairs={{0,6},{2,0},{4,2},{6,4},{1,7},{3,1},{5,3},{7,5},{8,14},{10,8},{12,... | collective-permute-start | bytes 786440 | tf_op jit(solution)/shard_map/ppermute | solution.py:75
  97.5 30.4 %collective-permute-start.11 = (bf16[512,256]{1,0:T(8,128)(2,1)S(1)}, bf16[512,256]{1,0:T(8,128)(2,1)S(1)}, u32[]{:S(2)}, u32[]{:S(2)}) collective-permute-start(bf16[512,256]{1,0:T(8,128)(2,1)S(1)} %copy-done.1), channel_id=1, source_target_pairs={{0,4},{2,6},{4,0},{6,2},{1,5},{3,7},{5,1},{7,3},{8,12},{10,14},{12... | collective-permute-start | bytes 786440 | tf_op jit(solution)/shard_map/ppermute | solution.py:75
  128.0 16.8 %collective-permute-start.12 = (bf16[4,512,256]{2,1,0:T(8,128)(2,1)S(1)}, bf16[4,512,256]{2,1,0:T(8,128)(2,1)S(1)}, u32[]{:S(2)}, u32[]{:S(2)}) collective-permute-start(bf16[4,512,256]{2,1,0:T(8,128)(2,1)S(1)} %pad_maximum_fusion.1.mine), channel_id=1, source_target_pairs={{0,1},{1,0},{2,3},{3,2},{4,5},{5,4},{6,7},{7,6},{8,9},{9,8},{10,11... | collective-permute-start | bytes 3145736 | tf_op jit(solution)/shard_map/ppermute | solution.py:80
  137.7 18.3 %all-to-all-start.3 = ((bf16[8,4,3072]{2,1,0:T(4,128)(2,1)}), bf16[8,4,3072]{2,1,0:T(4,128)(2,1)}, u32[]{:S(2)}, u32[]{:S(2)}) async-start(bf16[8,4,3072]{2,1,0:T(4,128)(2,1)} %pad_maximum_fusion.7), calls=%async_computation.3 | async-start | bytes 393216 | tf_op jit(solution)/shard_map/all_to_all | solution.py:181
  156.1 21.8 %copy-start.12 = (f32[1,1,256]{2,0,1:T(1,128)S(1)}, f32[1,1,256]{2,0,1:T(1,128)}, u32[]{:S(2)}) copy-start(f32[1,1,256]{2,0,1:T(1,128)} %copy-done.11) | copy-start | bytes 3076
  156.1 21.8 %copy-start.14 = (f32[1,1,256]{2,0,1:T(1,128)S(1)}, f32[1,1,256]{2,0,1:T(1,128)}, u32[]{:S(2)}) copy-start(f32[1,1,256]{2,0,1:T(1,128)} %copy-done.13) | copy-start | bytes 3076
  156.1 24.1 %all-to-all-start = ((bf16[8,32,2304]{2,1,0:T(8,128)(2,1)}), bf16[8,32,2304]{2,1,0:T(8,128)(2,1)S(1)}, u32[]{:S(2)}, u32[]{:S(2)}) async-start(bf16[8,32,2304]{2,1,0:T(8,128)(2,1)} %bitcast.32), calls=%async_computation | async-start | bytes 2359296 | tf_op jit(solution)/shard_map/all_to_all | solution.py:169
  161.9 15.9 %collective-permute-start.14 = (bf16[16,256]{1,0:T(8,128)(2,1)S(1)}, bf16[16,256]{1,0:T(8,128)(2,1)S(1)}, u32[]{:S(2)}, u32[]{:S(2)}) collective-permute-start(bf16[16,256]{1,0:T(8,128)(2,1)S(1)} %get-tuple-element.89), channel_id=1, source_target_pairs={{0,8},{8,16},{16,24},{24,32},{32,40},{40,48},{48,56},{56,64},{64,7... | collective-permute-start | bytes 24584 | tf_op jit(solution)/shard_map/ppermute | solution.py:67
  165.4 12.5 %collective-permute-start.13 = (bf16[16,256]{1,0:T(8,128)(2,1)S(1)}, bf16[16,256]{1,0:T(8,128)(2,1)S(1)}, u32[]{:S(2)}, u32[]{:S(2)}) collective-permute-start(bf16[16,256]{1,0:T(8,128)(2,1)S(1)} %get-tuple-element.88), channel_id=1, source_target_pairs={{8,0},{16,8},{24,16},{32,24},{40,32},{48,40},{56,48},{64,56},{72,6... | collective-permute-start | bytes 24584 | tf_op jit(solution)/shard_map/ppermute | solution.py:68
  181.3 13.1 %all-to-all-start.1 = ((bf16[8,4,3072]{2,1,0:T(4,128)(2,1)}), bf16[8,4,3072]{2,1,0:T(4,128)(2,1)S(1)}, u32[]{:S(2)}, u32[]{:S(2)}) async-start(bf16[8,4,3072]{2,1,0:T(4,128)(2,1)} %pad_maximum_fusion.6), calls=%async_computation.1 | async-start | bytes 393216 | tf_op jit(solution)/shard_map/all_to_all | solution.py:181
  (25 other events, 176.1 us)

commit v3 on v1

v3 whole, which is shorter than its diff:
```python
import math

import jax
import jax.numpy as jnp
from jax import lax
from jax.experimental import pallas as pl
from jax.experimental.pallas import tpu as pltpu
from jax.sharding import Mesh, PartitionSpec as P

BASE_DILATION = 4

SEQ = ("y", "zl", "x")
BLK = ("zh", "core")
NEAR = ("zl", "x")
STEPS = (0, 1, 3, 2)

mask_token = 4
gelu_scale = 0.7978845608028654
gelu_cubic = 0.044715
LANES = 256
BF16 = jnp.bfloat16
F32 = jnp.float32

ROWS = 512
TAPS = 9
VOCAB = 5
LOW_GAP, HIGH_GAP = BASE_DILATION, 2 * BASE_DILATION
LOW_REACH, HIGH_REACH = 4 * LOW_GAP, 4 * HIGH_GAP
EDGE = HIGH_REACH
MESSAGE = EDGE + 16
CHUNK = 64
PAIRED = (((1,), (1,)), ((), ()))


def gelu_pair(pre_act):
    square = pre_act * pre_act
    tangent = jnp.tanh(gelu_scale * (pre_act + gelu_cubic * square * pre_act))
    half = 0.5 * (1.0 + tangent)
    derivative = half + 0.5 * pre_act * (1.0 - tangent * tangent) * gelu_scale * (
        1.0 + 3.0 * gelu_cubic * square
    )
    return (pre_act * half, derivative)


def call(kernel, outs, scratch, in_specs, *operands):
    extra = {} if in_specs is None else {"in_specs": in_specs, "grid": (1,)}
    return pl.pallas_call(
        kernel,
        out_shape=outs,
        scratch_shapes=scratch,
        compiler_params=pltpu.CompilerParams(vmem_limit_bytes=40 << 20),
        **extra,
    )(*operands)


def shape(dims, kind):
    return jax.ShapeDtypeStruct(dims, kind)


def pack_kernel(saved_head, saved_tail, ids, next_out, prev_out):
    for out, rows, row in ((next_out, saved_tail, 3), (prev_out, saved_head, 0)):
        out[:EDGE] = rows[...]
        line = jnp.broadcast_to(ids[row : row + 1].astype(F32), (MESSAGE - EDGE, 128))
        out[EDGE:] = jnp.concatenate([line, line], axis=1).astype(BF16)


def prep_kernel(
    place, before, after, saved, cot, ids, start, length, embedding, conv,
    slope_up, act_up, slope_low, act_low, masked, hot_out,
    cover, idw, wide, first, table, act_all,
):
    base = place[0] * ROWS - CHUNK
    total = place[1]

    def cover_chunk(index, carry):
        row0 = pl.multiple_of(index * CHUNK, CHUNK)
        here = lax.broadcasted_iota(jnp.int32, (CHUNK, 128), 0) + (base + row0)
        hit = jnp.zeros((CHUNK, 128), jnp.int32)
        for group in range(start.shape[0]):
            gap = here - start[group : group + 1]
            hit = jnp.where((gap >= 0) & (gap < length[group : group + 1]), 1, hit)
        seen = jnp.max(hit, axis=1, keepdims=True).astype(F32)
        cover[pl.ds(row0, CHUNK), :] = jnp.broadcast_to(seen, (CHUNK, 128))
        return carry

    lax.fori_loop(0, ROWS // CHUNK + 2, cover_chunk, 0)

    def column(row):
        return jnp.transpose(jnp.broadcast_to(row.astype(F32), (128, 128)))

    idw[:LOW_REACH] = column(before[EDGE : EDGE + 1, :128])[128 - LOW_REACH :]
    for piece in range(ROWS // 128):
        idw[LOW_REACH + 128 * piece : LOW_REACH + 128 * (piece + 1)] = column(ids[piece : piece + 1])
    idw[LOW_REACH + ROWS :] = column(after[EDGE : EDGE + 1, :128])[:LOW_REACH]
    spread = ROWS + 2 * LOW_REACH
    spot = lax.broadcasted_iota(jnp.int32, (spread, 128), 0) + (base + CHUNK - LOW_REACH)
    lane = lax.broadcasted_iota(jnp.int32, (1, 128), 1)
    tokens = jnp.where(
        cover[CHUNK - LOW_REACH : CHUNK - LOW_REACH + spread] > 0.0,
        float(mask_token),
        idw[...],
    )
    tokens = jnp.where((spot >= 0) & (spot < total), tokens, 7.0)
    idw[...] = tokens
    table[...] = jnp.zeros_like(table)
    table[:VOCAB] = embedding[...].astype(F32)
    hot = jnp.where(tokens == lane.astype(F32), 1.0, 0.0).astype(BF16)
    first[...] = jnp.dot(hot, table[...].astype(BF16), preferred_element_type=F32)

    channel = lax.broadcasted_iota(jnp.int32, (LANES, LANES), 1)
    target = lax.broadcasted_iota(jnp.int32, (LANES, LANES), 0)
    tail = ((channel >> 5) << 2) | (channel & 3)
    low_place = (((channel >> 2) & 7) << 5) | tail
    up_place = (((channel >> 2) & 3) << 6) | (((channel >> 4) & 1) << 5) | tail
    low_shuffle = jnp.where(low_place == target, 1.0, 0.0).astype(BF16)
    up_shuffle = jnp.where(up_place == target, 1.0, 0.0).astype(BF16)

    taps_low = [conv[0, index : index + 1].astype(F32) for index in range(TAPS)]
    for chunk in range(ROWS // CHUNK):
        row0 = chunk * CHUNK
        pre = None
        for index in range(TAPS):
            begin = row0 + index * LOW_GAP
            term = taps_low[index] * first[begin : begin + CHUNK]
            pre = term if pre is None else pre + term
        act, slope = gelu_pair(pre)
        slope_low[row0 : row0 + CHUNK] = slope
        act_all[row0 : row0 + CHUNK] = act.astype(BF16)
    act_low[...] = lax.dot_general(
        low_shuffle, act_all[:ROWS], PAIRED, preferred_element_type=F32
    ).astype(BF16)

    picked = idw[:ROWS]
    for index in range(1, TAPS):
        picked = jnp.where((lane >> 3) == index, idw[index * LOW_GAP : index * LOW_GAP + ROWS], picked)
    kind = lane & 7
    live = (kind < VOCAB) & (lane < 8 * TAPS)
    hot = jnp.where((picked == kind.astype(F32)) & live, 1.0, 0.0)
    hot_out[...] = jnp.transpose(hot).astype(BF16)

    wide[:HIGH_REACH] = before[:HIGH_REACH].astype(F32)
    wide[HIGH_REACH : HIGH_REACH + ROWS] = saved[...].astype(F32)
    wide[HIGH_REACH + ROWS :] = after[:HIGH_REACH].astype(F32)
    taps_up = [conv[1, index : index + 1].astype(F32) for index in range(TAPS)]
    for chunk in range(ROWS // CHUNK):
        row0 = chunk * CHUNK
        pre = None
        for index in range(TAPS):
            begin = row0 + index * HIGH_GAP
            term = taps_up[index] * wide[begin : begin + CHUNK]
            pre = term if pre is None else pre + term
        act, slope = gelu_pair(pre)
        seen = cover[CHUNK + row0 : 2 * CHUNK + row0] > 0.0
        seen = jnp.concatenate([seen, seen], axis=1)
        slope_up[row0 : row0 + CHUNK] = jnp.where(seen, slope, 0.0)
        act_all[row0 : row0 + CHUNK] = jnp.where(seen, act, 0.0).astype(BF16)
        masked[row0 : row0 + CHUNK] = jnp.where(
            seen, cot[row0 : row0 + CHUNK].astype(F32), 0.0
        ).astype(BF16)
    act_up[...] = lax.dot_general(
        up_shuffle, act_all[:ROWS], PAIRED, preferred_element_type=F32
    ).astype(BF16)


def chip_block(place, step):
    return (place[2] - step) & 3


def weight_columns(weights, place, step, core):
    block = chip_block(place, step) * 2 + core
    return weights[0, :, pl.ds(pl.multiple_of(block * LANES, LANES), LANES)]


def product_over_blocks(place, mine, pairs, weights):
    total = None
    for index, step in enumerate(STEPS):
        term = lax.dot_general(
            mine[index][...], weight_columns(weights, place, step, place[3]), PAIRED,
            preferred_element_type=F32,
        )
        total = term if total is None else total + term
    for index, step in enumerate(STEPS):
        total = total + lax.dot_general(
            pairs[index // 2][index % 2], weight_columns(weights, place, step, 1 - place[3]),
            PAIRED, preferred_element_type=F32,
        )
    return total


def upper_kernel(place, m0, m1, m2, m3, p0, p1, weights, slope, grad_out, head_out, tail_out):
    grad = product_over_blocks(place, (m0, m1, m2, m3), (p0, p1), weights) * slope[...]
    grad = grad.astype(BF16)
    grad_out[...] = grad
    head_out[...] = grad[:HIGH_REACH]
    tail_out[...] = grad[ROWS - HIGH_REACH :]


def outer_product(act, mine, pairs, out):
    for index in range(2 * len(STEPS)):
        half = index % len(STEPS)
        piece = mine[half][...] if index < len(STEPS) else pairs[half // 2][half % 2]
        out[:, index * LANES : (index + 1) * LANES] = jnp.dot(
            act[...], piece, preferred_element_type=F32
        ).astype(BF16)


def upper_outer_kernel(act, m0, m1, m2, m3, p0, p1, grad, before, saved, after, out, tap_out, wide):
    outer_product(act, (m0, m1, m2, m3), (p0, p1), out)
    wide[:HIGH_REACH] = before[:HIGH_REACH].astype(F32)
    wide[HIGH_REACH : HIGH_REACH + ROWS] = saved[...].astype(F32)
    wide[HIGH_REACH + ROWS :] = after[:HIGH_REACH].astype(F32)
    sums = [jnp.zeros((8, LANES), F32) for index in range(TAPS)]
    for chunk in range(ROWS // CHUNK):
        row0 = chunk * CHUNK
        grad_wide = grad[row0 : row0 + CHUNK].astype(F32)
        for index in range(TAPS):
            begin = row0 + index * HIGH_GAP
            term = grad_wide * wide[begin : begin + CHUNK]
            sums[index] = sums[index] + jnp.sum(term.reshape(CHUNK // 8, 8, LANES), axis=0)
    tap_out[...] = jnp.zeros_like(tap_out)
    for index in range(TAPS):
        tap_out[index : index + 1] = jnp.sum(sums[index], axis=0, keepdims=True)


def lower_kernel(
    place, act, m0, m1, m2, m3, p0, p1, weights, slope, hot, up_row, embedding, conv, upper_taps,
    out, grad_out, small, table,
):
    mine, pairs = (m0, m1, m2, m3), (p0, p1)
    grad = (product_over_blocks(place, mine, pairs, weights) * slope[...]).astype(BF16)
    grad_out[...] = grad
    outer_product(act, mine, pairs, out)
    picked = jnp.dot(hot[...], grad, preferred_element_type=F32)
    embed = jnp.dot(hot[32:48], up_row[...], preferred_element_type=F32)[:8]
    table[...] = jnp.zeros_like(table)
    table[:VOCAB] = embedding[...].astype(F32)
    small[...] = jnp.zeros_like(small)
    for index in range(TAPS):
        piece = picked[index * 8 : index * 8 + 8]
        small[index : index + 1] = jnp.sum(piece * table[...], axis=0, keepdims=True)
        embed = embed + piece * conv[0, index : index + 1].astype(F32)
    small[TAPS : TAPS + VOCAB] = embed[:VOCAB]
    small[TAPS + VOCAB : 2 * TAPS + VOCAB] = upper_taps[:TAPS]
    packed = small[...].astype(BF16)
    for index in range(LANES // 32):
        out[index * 32 : (index + 1) * 32, 8 * LANES :] = packed


def upper_half_kernel(place, pieces, keep, send, total):
    running = pieces[0].astype(F32)
    for index in range(1, pieces.shape[0]):
        running = running + pieces[index].astype(F32)
    total[...] = running
    keep[...] = total[pl.ds(pl.multiple_of(place[4] * 32, 32), 32), :]
    send[...] = total[pl.ds(pl.multiple_of((1 - place[4]) * 32, 32), 32), :].astype(BF16)


def middle_kernel(pieces, keep, received, out):
    running = pieces[0].astype(F32)
    for index in range(1, pieces.shape[0]):
        running = running + pieces[index].astype(F32)
    width = 8 * LANES
    upper = (keep[...] + received[...].astype(F32)).astype(BF16)
    small = running[:, width:].astype(BF16)
    lower = running[:, :width].astype(BF16)
    for far in range(8):
        out[far, :, :width] = lower[4 * far : 4 * far + 4]
        out[far, :, width : 2 * width] = upper[4 * far : 4 * far + 4]
        for group in range(6):
            begin = 2 * width + group * LANES
            out[far, :, begin : begin + LANES] = small[4 * group : 4 * group + 4]


def final_kernel(place, pieces, weight_out, kernel_out, embed_out, *, scale):
    running = pieces[0].astype(F32)
    for index in range(1, pieces.shape[0]):
        running = running + pieces[index].astype(F32)
    running = running * scale
    width = 8 * LANES
    for index in range(8):
        step = STEPS[index % 4]
        core = place[3] if index < 4 else 1 - place[3]
        spot = pl.multiple_of((chip_block(place, step) * 2 + core) * LANES, LANES)
        for layer in range(2):
            begin = layer * width + index * LANES
            weight_out[layer, :, pl.ds(spot, LANES)] = running[:, begin : begin + LANES]

    def small_row(row):
        begin = 2 * width + (row // 4) * LANES
        return running[row % 4 : row % 4 + 1, begin : begin + LANES]

    for index in range(TAPS):
        kernel_out[0, index : index + 1] = small_row(index)
        kernel_out[1, index : index + 1] = small_row(TAPS + VOCAB + index)
    for index in range(VOCAB):
        embed_out[index : index + 1] = small_row(TAPS + index)


def spread_kernel(base, grad, before, after, conv, out, wide, *, layer, gap):
    reach = gap * (TAPS // 2)
    wide[:reach] = before[...].astype(F32)
    wide[reach : reach + ROWS] = grad[...].astype(F32)
    wide[reach + ROWS :] = after[...].astype(F32)
    for chunk in range(ROWS // CHUNK):
        row0 = chunk * CHUNK
        running = base[row0 : row0 + CHUNK].astype(F32)
        for index in range(TAPS):
            begin = row0 + (TAPS - 1 - index) * gap
            tap = conv[layer, index : index + 1].astype(F32)
            running = running + tap * wide[begin : begin + CHUNK]
        out[row0 : row0 + CHUNK] = running.astype(BF16)


def spread(base, grad, before, after, conv, layer, gap):
    def kernel(*refs):
        spread_kernel(*refs, layer=layer, gap=gap)

    scratch = [pltpu.VMEM((ROWS + gap * (TAPS - 1), LANES), F32)]
    out = shape((ROWS, LANES), BF16)
    return call(kernel, out, scratch, None, base, grad, before, after, conv)


def seq_shift(cells, step):
    count = lax.axis_size(SEQ)
    if step > 0:
        return lax.ppermute(cells, SEQ, [(i, i + 1) for i in range(count - 1)])
    return lax.ppermute(cells, SEQ, [(i + 1, i) for i in range(count - 1)])


def ring_copies(slab):
    count = lax.axis_size("zh")
    moved = {0: slab}
    for step in (2, 1, 3):
        moved[step] = lax.ppermute(slab, "zh", [(i, (i + step) % count) for i in range(count)])
    return [moved[step] for step in STEPS]


def core_swap(cells):
    return lax.ppermute(cells, "core", [(0, 1), (1, 0)])


def swapped_pairs(mine):
    return core_swap(jnp.stack(mine[:2])), core_swap(jnp.stack(mine[2:]))


def on_device(
    base_ids, span_start, span_length, embedding, conv_kernel, mix_weight, saved_input, cotangent
):
    total_rows = ROWS * lax.axis_size(SEQ)
    place = jnp.stack(
        [
            lax.axis_index(SEQ),
            jnp.int32(total_rows),
            lax.axis_index("zh"),
            lax.axis_index("core"),
            lax.axis_index("zl"),
        ]
    ).astype(jnp.int32)
    smem = pl.BlockSpec(memory_space=pltpu.SMEM)
    vmem = pl.BlockSpec(memory_space=pltpu.VMEM)
    ids = base_ids.reshape(ROWS // 128, 128)
    slab = shape((ROWS, LANES), BF16)
    slab_wide = shape((ROWS, LANES), F32)
    turned = shape((LANES, ROWS), BF16)

    message = shape((MESSAGE, LANES), BF16)
    last = ROWS // HIGH_REACH - 1
    to_next, to_prev = call(
        pack_kernel,
        (message, message),
        [],
        [
            pl.BlockSpec((HIGH_REACH, LANES), lambda step: (0, 0)),
            pl.BlockSpec((HIGH_REACH, LANES), lambda step: (last, 0)),
            vmem,
        ],
        saved_input, saved_input, ids,
    )
    before = seq_shift(to_next, 1)
    after = seq_shift(to_prev, -1)
    source, before, after = lax.optimization_barrier((cotangent, before, after))
    mine = ring_copies(source)

    slope_up, act_up, slope_low, act_low, masked, hot = call(
        prep_kernel,
        (slab_wide, turned, slab_wide, turned, slab, shape((128, ROWS), BF16)),
        [
            pltpu.VMEM((ROWS + 2 * CHUNK, 128), F32),
            pltpu.VMEM((ROWS + 2 * LOW_REACH, 128), F32),
            pltpu.VMEM((ROWS + 2 * HIGH_REACH, LANES), F32),
            pltpu.VMEM((ROWS + 2 * LOW_REACH, LANES), F32),
            pltpu.VMEM((128, LANES), F32),
            pltpu.VMEM((ROWS, LANES), BF16),
        ],
        [smem] + [vmem] * 9,
        place, before, after, saved_input, cotangent, ids,
        span_start.reshape(-1, 128), span_length.reshape(-1, 128), embedding, conv_kernel,
    )
    slope_up, mine[1], mine[2], mine[3] = lax.optimization_barrier(
        (slope_up, mine[1], mine[2], mine[3])
    )
    pairs = swapped_pairs(mine)

    weight_specs = [
        pl.BlockSpec((1, LANES, 8 * LANES), lambda step: (0, 0, 0)),
        pl.BlockSpec((1, LANES, 8 * LANES), lambda step: (1, 0, 0)),
    ]
    rim = shape((HIGH_REACH, LANES), BF16)
    grad_upper, head, tail = call(
        upper_kernel,
        (slab, rim, rim),
        [],
        [smem] + [vmem] * 6 + [weight_specs[1], vmem],
        place, *mine, *pairs, mix_weight, slope_up,
    )
    up_before = seq_shift(tail, 1)
    up_after = seq_shift(head, -1)
    up_mid = spread(masked, grad_upper, up_before, up_after, conv_kernel, 1, HIGH_GAP)
    mid = ring_copies(up_mid)
    mid_pairs = swapped_pairs(mid)

    upper_outer, upper_taps = call(
        upper_outer_kernel,
        (shape((LANES, 8 * LANES), BF16), shape((16, LANES), F32)),
        [pltpu.VMEM((ROWS + 2 * HIGH_REACH, LANES), F32)],
        None,
        act_up, *mine, *pairs, grad_upper, before, saved_input, after,
    )
    pieces = lax.all_to_all(upper_outer.reshape(4, 64, 8 * LANES), "x", 0, 0)
    keep, send = call(
        upper_half_kernel,
        (shape((32, 8 * LANES), F32), shape((32, 8 * LANES), BF16)),
        [pltpu.VMEM((64, 8 * LANES), F32)],
        [smem, vmem],
        place, pieces,
    )
    received = lax.ppermute(send, "zl", [(0, 1), (1, 0)])

    lower_outer, grad_lower = call(
        lower_kernel,
        (shape((LANES, 9 * LANES), BF16), slab),
        [pltpu.VMEM((32, LANES), F32), pltpu.VMEM((8, LANES), F32)],
        [smem] + [vmem] * 7 + [weight_specs[0]] + [vmem] * 6,
        place, act_low, *mid, *mid_pairs, mix_weight, slope_low, hot, up_mid, embedding,
        conv_kernel, upper_taps,
    )
    pieces = lax.all_to_all(lower_outer.reshape(8, 32, 9 * LANES), NEAR, 0, 0)
    low_before = seq_shift(grad_lower[ROWS - LOW_REACH :], 1)
    low_after = seq_shift(grad_lower[:LOW_REACH], -1)
    input_grad = spread(up_mid, grad_lower, low_before, low_after, conv_kernel, 0, LOW_GAP)
    middle = call(
        middle_kernel, shape((8, 4, 22 * LANES), BF16), [], None, pieces, keep, received
    )
    pieces = lax.all_to_all(middle, "y", 0, 0)

    def finish(*refs):
        final_kernel(*refs, scale=1.0 / math.sqrt(total_rows))

    weight_grad, kernel_grad, embed_grad = call(
        finish,
        (shape((2, 4, 8 * LANES), F32), shape((2, TAPS, LANES), F32), shape((VOCAB, LANES), F32)),
        [],
        [smem, vmem],
        place, pieces,
    )
    return (input_grad, weight_grad, kernel_grad, embed_grad)


def solution(mesh):
    fine = Mesh(mesh.devices.reshape(8, 2, 4, 4, 2), SEQ + BLK)
    placed = (
        P(SEQ),
        P(),
        P(),
        P(None, BLK),
        P(None, None, BLK),
        P(None, BLK, None),
        P(SEQ, BLK),
        P(SEQ, BLK),
    )
    return jax.shard_map(
        on_device,
        mesh=fine,
        in_specs=placed,
        out_specs=(
            P(SEQ, BLK),
            P(None, BLK + SEQ, None),
            P(None, None, BLK),
            P(None, BLK),
        ),
        check_vma=False,
    )
```

time: 204 us -> 160 us (0.78)
  the two profiles are of different devices: /device:TPU:64 before, /device:TPU:32 now
where the time goes in v3:
time: 160 us; the launch traced here: 159 us
  starting transfers between devices  90.3 us (56%)
  waiting for transfers between devices  39.4 us (25%)
  Pallas kernels  15.1 us (9%)
  local copies, waits for them, and re-layouts  11.2 us (7%)
  other arithmetic  2.18 us (1%)
    ppermute x6, starting transfers between devices, ring_copies(): lax.ppermute(slab, 'zh', [(i, (i + step) % count) for i in range(count)])  29.8 us
    ppermute x3, starting transfers between devices, seq_shift(): return lax.ppermute(cells, SEQ, [(i + 1, i) for i in range(count - 1)])  21.9 us
    pallas_call x10, Pallas kernels, call(): pl.pallas_call(kernel, out_shape=outs, scratch_shapes=scratch, compiler_p...  15.1 us
    ppermute x1, waiting for transfers between devices, on_device(): received = lax.ppermute(send, 'zl', [(0, 1), (1, 0)])  13.7 us
    ppermute x6, waiting for transfers between devices, ring_copies(): lax.ppermute(slab, 'zh', [(i, (i + step) % count) for i in range(count)])  12 us
    unnamed x60, local copies, waits for them, and re-layouts  11.1 us
    all_to_all x1, starting transfers between devices, on_device(): pieces = lax.all_to_all(middle, 'y', 0, 0)  9.4 us
    ppermute x4, starting transfers between devices, core_swap(): return lax.ppermute(cells, 'core', [(0, 1), (1, 0)])  8.79 us
  transfers between devices with their start and end apart: 20, of which 10 were waited for; matrix products, arithmetic and copies ran while one was open for 2% of the time, Pallas kernels for 7%

profile of v3, /device:TPU:32, one launch (start us, length us, event | category | flops | bytes accessed | tf_op | source)
XLA Modules:
  0.0 159.3 jit_solution(15726254617133188308)
XLA Ops:
  2.3 3.4 %collective-permute-start = (bf16[48,256]{1,0:T(8,128)(2,1)S(1)}, bf16[48,256]{1,0:T(8,128)(2,1)S(1)}, u32[]{:S(2)}, u32[]{:S(2)}) collective-permute-start(bf16[48,256]{1,0:T(8,128)(2,1)S(1)} %get-tuple-element.31), channel_id=1, source_target_pairs={{0,8},{8,16},{16,24},{24,32},{32,40},{40,48},{48,56},{56,64},{64,7... | collective-permute-start | bytes 73736 | tf_op jit(solution)/shard_map/ppermute | solution.py:326
  5.7 6.7 %collective-permute-start.1 = (bf16[48,256]{1,0:T(8,128)(2,1)S(1)}, bf16[48,256]{1,0:T(8,128)(2,1)S(1)}, u32[]{:S(2)}, u32[]{:S(2)}) collective-permute-start(bf16[48,256]{1,0:T(8,128)(2,1)S(1)} %get-tuple-element.32), channel_id=1, source_target_pairs={{8,0},{16,8},{24,16},{32,24},{40,32},{48,40},{56,48},{64,56},{72,6... | collective-permute-start | bytes 73736 | tf_op jit(solution)/shard_map/ppermute | solution.py:327
  13.8 10.9 %collective-permute-start.4 = (bf16[512,256]{1,0:T(8,128)(2,1)}, bf16[512,256]{1,0:T(8,128)(2,1)S(1)}, u32[]{:S(2)}, u32[]{:S(2)}) collective-permute-start(bf16[512,256]{1,0:T(8,128)(2,1)} %m0.1), channel_id=1, source_target_pairs={{0,4},{2,6},{4,0},{6,2},{1,5},{3,7},{5,1},{7,3},{8,12},{10,14},{12... | collective-permute-start | bytes 786440 | tf_op jit(solution)/shard_map/ppermute | solution.py:334
  24.8 1.9 %collective-permute-start.3 = (bf16[512,256]{1,0:T(8,128)(2,1)}, bf16[512,256]{1,0:T(8,128)(2,1)S(1)}, u32[]{:S(2)}, u32[]{:S(2)}) collective-permute-start(bf16[512,256]{1,0:T(8,128)(2,1)} %m0.1), channel_id=1, source_target_pairs={{0,6},{2,0},{4,2},{6,4},{1,7},{3,1},{5,3},{7,5},{8,14},{10,8},{12,... | collective-permute-start | bytes 786440 | tf_op jit(solution)/shard_map/ppermute | solution.py:334
  26.7 4.8 %collective-permute-start.2 = (bf16[512,256]{1,0:T(8,128)(2,1)}, bf16[512,256]{1,0:T(8,128)(2,1)S(1)}, u32[]{:S(2)}, u32[]{:S(2)}) collective-permute-start(bf16[512,256]{1,0:T(8,128)(2,1)} %m0.1), channel_id=1, source_target_pairs={{0,2},{2,4},{4,6},{6,0},{1,3},{3,5},{5,7},{7,1},{8,10},{10,12},{12... | collective-permute-start | bytes 786440 | tf_op jit(solution)/shard_map/ppermute | solution.py:334
  37.0 6.0 %shard_map.112 = (f32[512,256]{1,0:T(8,128)S(1)}, bf16[256,512]{1,0:T(8,128)(2,1)S(1)}, f32[512,256]{1,0:T(8,128)S(1)}, bf16[256,512]{1,0:T(8,128)(2,1)S(1)}, bf...) custom-call(s32[5]{0:T(128)S(1)} %stack.55.place.refs_0_, bf16[48,256]{1,0:T(8,128)(2,1)S(1)} %collective-permute-done.before, ...), custom_call_target="tpu_custom_call" | custom-call | tf_op jit(solution)/shard_map/pallas_call | solution.py:47
  43.1 3.0 %collective-permute-done.3.m2 = bf16[512,256]{1,0:T(8,128)(2,1)S(1)} collective-permute-done((bf16[512,256]{1,0:T(8,128)(2,1)}, bf16[512,256]{1,0:T(8,128)(2,1)S(1)}, u32[]{:S(2)}, u32[]{:S(2)}) %collective-permute-start.3) | collective-permute-done | bytes 262176 | tf_op jit(solution)/shard_map/ppermute | solution.py:334
  49.2 2.5 %collective-permute-start.6 = (bf16[2,512,256]{2,1,0:T(8,128)(2,1)S(1)}, bf16[2,512,256]{2,1,0:T(8,128)(2,1)S(1)}, u32[]{:S(2)}, u32[]{:S(2)}) collective-permute-start(bf16[2,512,256]{2,1,0:T(8,128)(2,1)S(1)} %pad_maximum_fusion.1), channel_id=1, source_target_pairs={{0,1},{1,0},{2,3},{3,2},{4,5},{5,4},{6,7},{7,6},{8,9},{9,8},{10,11... | collective-permute-start | bytes 1572872 | tf_op jit(solution)/shard_map/ppermute | solution.py:339
  56.5 10.3 %collective-permute-start.8 = (bf16[32,256]{1,0:T(8,128)(2,1)S(1)}, bf16[32,256]{1,0:T(8,128)(2,1)S(1)}, u32[]{:S(2)}, u32[]{:S(2)}) collective-permute-start(bf16[32,256]{1,0:T(8,128)(2,1)S(1)} %get-tuple-element.44), channel_id=1, source_target_pairs={{8,0},{16,8},{24,16},{32,24},{40,32},{48,40},{56,48},{64,56},{72,6... | collective-permute-start | bytes 49160 | tf_op jit(solution)/shard_map/ppermute | solution.py:327
  68.6 5.4 %collective-permute-start.11 = (bf16[512,256]{1,0:T(8,128)(2,1)S(1)}, bf16[512,256]{1,0:T(8,128)(2,1)}, u32[]{:S(2)}, u32[]{:S(2)}) collective-permute-start(bf16[512,256]{1,0:T(8,128)(2,1)S(1)} %shard_map.114.m0.up_row.refs_0_), channel_id=1, source_target_pairs={{0,4},{2,6},{4,0},{6,2},{1,5},{3,7},{5,1},{7,3},{8,12},{10,14},{12... | collective-permute-start | bytes 786440 | tf_op jit(solution)/shard_map/ppermute | solution.py:334
  74.0 2.4 %collective-permute-start.10 = (bf16[512,256]{1,0:T(8,128)(2,1)S(1)}, bf16[512,256]{1,0:T(8,128)(2,1)}, u32[]{:S(2)}, u32[]{:S(2)}) collective-permute-start(bf16[512,256]{1,0:T(8,128)(2,1)S(1)} %shard_map.114.m0.up_row.refs_0_), channel_id=1, source_target_pairs={{0,6},{2,0},{4,2},{6,4},{1,7},{3,1},{5,3},{7,5},{8,14},{10,8},{12,... | collective-permute-start | bytes 786440 | tf_op jit(solution)/shard_map/ppermute | solution.py:334
  76.4 4.3 %collective-permute-start.9 = (bf16[512,256]{1,0:T(8,128)(2,1)S(1)}, bf16[512,256]{1,0:T(8,128)(2,1)}, u32[]{:S(2)}, u32[]{:S(2)}) collective-permute-start(bf16[512,256]{1,0:T(8,128)(2,1)S(1)} %shard_map.114.m0.up_row.refs_0_), channel_id=1, source_target_pairs={{0,2},{2,4},{4,6},{6,0},{1,3},{3,5},{5,7},{7,1},{8,10},{10,12},{12... | collective-permute-start | bytes 786440 | tf_op jit(solution)/shard_map/ppermute | solution.py:334
  83.2 3.5 %all-to-all-start.1 = ((bf16[4,64,2048]{2,1,0:T(8,128)(2,1)}), bf16[4,64,2048]{2,1,0:T(8,128)(2,1)S(1)}, u32[]{:S(2)}, u32[]{:S(2)}) async-start(bf16[4,64,2048]{2,1,0:T(8,128)(2,1)} %bitcast.23), calls=%async_computation.1 | async-start | bytes 2097152 | tf_op jit(solution)/shard_map/all_to_all | solution.py:429
  86.7 3.5 %collective-permute-done.11.m3 = bf16[512,256]{1,0:T(8,128)(2,1)} collective-permute-done((bf16[512,256]{1,0:T(8,128)(2,1)S(1)}, bf16[512,256]{1,0:T(8,128)(2,1)}, u32[]{:S(2)}, u32[]{:S(2)}) %collective-permute-start.11) | collective-permute-done | bytes 262176 | tf_op jit(solution)/shard_map/ppermute | solution.py:334
  90.3 4.4 %collective-permute-done.10.m2 = bf16[512,256]{1,0:T(8,128)(2,1)} collective-permute-done((bf16[512,256]{1,0:T(8,128)(2,1)S(1)}, bf16[512,256]{1,0:T(8,128)(2,1)}, u32[]{:S(2)}, u32[]{:S(2)}) %collective-permute-start.10) | collective-permute-done | bytes 262176 | tf_op jit(solution)/shard_map/ppermute | solution.py:334
  95.7 1.9 %collective-permute-start.13 = (bf16[2,512,256]{2,1,0:T(8,128)(2,1)S(1)}, bf16[2,512,256]{2,1,0:T(8,128)(2,1)S(1)}, u32[]{:S(2)}, u32[]{:S(2)}) collective-permute-start(bf16[2,512,256]{2,1,0:T(8,128)(2,1)S(1)} %pad_maximum_fusion.3), channel_id=1, source_target_pairs={{0,1},{1,0},{2,3},{3,2},{4,5},{5,4},{6,7},{7,6},{8,9},{9,8},{10,11... | collective-permute-start | bytes 1572872 | tf_op jit(solution)/shard_map/ppermute | solution.py:339
  98.7 2.4 %collective-permute-start.12 = (bf16[2,512,256]{2,1,0:T(8,128)(2,1)S(1)}, bf16[2,512,256]{2,1,0:T(8,128)(2,1)S(1)}, u32[]{:S(2)}, u32[]{:S(2)}) collective-permute-start(bf16[2,512,256]{2,1,0:T(8,128)(2,1)S(1)} %pad_maximum_fusion.2), channel_id=1, source_target_pairs={{0,1},{1,0},{2,3},{3,2},{4,5},{5,4},{6,7},{7,6},{8,9},{9,8},{10,11... | collective-permute-start | bytes 1572872 | tf_op jit(solution)/shard_map/ppermute | solution.py:339
  102.6 2.6 %shard_map.116 = (bf16[256,2304]{1,0:T(8,128)(2,1)S(1)}, bf16[512,256]{1,0:T(8,128)(2,1)S(1)}) custom-call(s32[5]{0:T(128)S(1)} %copy-done.19, bf16[256,512]{1,0:T(8,128)(2,1)S(1)} %copy-done.13, bf16[512,256]{1,0:T(8,128)(2,1)S(1)} %shard_map.114.m0.up_row.refs_0_, bf16[512,256]{1,0:T(8,128)(2,1)} %collective-permute-done.9.m1, ...), custom_call_target="tpu_custom_call" | custom-call | tf_op jit(solution)/shard_map/pallas_call | solution.py:47
  107.0 5.8 %all-to-all-start = ((bf16[8,32,2304]{2,1,0:T(8,128)(2,1)}), bf16[8,32,2304]{2,1,0:T(8,128)(2,1)S(1)}, u32[]{:S(2)}, u32[]{:S(2)}) async-start(bf16[8,32,2304]{2,1,0:T(8,128)(2,1)} %bitcast.22), calls=%async_computation | async-start | bytes 2359296 | tf_op jit(solution)/shard_map/all_to_all | solution.py:447
  113.5 3.9 %collective-permute-start.16 = (bf16[32,2048]{1,0:T(8,128)(2,1)S(1)}, bf16[32,2048]{1,0:T(8,128)(2,1)S(1)}, u32[]{:S(2)}, u32[]{:S(2)}) collective-permute-start(bf16[32,2048]{1,0:T(8,128)(2,1)S(1)} %get-tuple-element.54), channel_id=1, source_target_pairs={{0,32},{32,0},{1,33},{33,1},{2,34},{34,2},{3,35},{35,3},{4,36},{36... | collective-permute-start | bytes 393224 | tf_op jit(solution)/shard_map/ppermute | solution.py:437
  117.4 13.7 %collective-permute-done.16.received = bf16[32,2048]{1,0:T(8,128)(2,1)S(1)} collective-permute-done((bf16[32,2048]{1,0:T(8,128)(2,1)S(1)}, bf16[32,2048]{1,0:T(8,128)(2,1)S(1)}, u32[]{:S(2)}, u32[]{:S(2)}) %collective-permute-start.16) | collective-permute-done | bytes 131104 | tf_op jit(solution)/shard_map/ppermute | solution.py:437
  132.1 9.4 %all-to-all-start.2 = ((bf16[8,4,5632]{2,1,0:T(4,128)(2,1)}), bf16[8,4,5632]{2,1,0:T(4,128)(2,1)S(1)}, u32[]{:S(2)}, u32[]{:S(2)}) async-start(bf16[8,4,5632]{2,1,0:T(4,128)(2,1)} %shard_map.119), calls=%async_computation.2 | async-start | bytes 720896 | tf_op jit(solution)/shard_map/all_to_all | solution.py:454
  141.5 4.9 %collective-permute-start.15 = (bf16[16,256]{1,0:T(8,128)(2,1)S(1)}, bf16[16,256]{1,0:T(8,128)(2,1)S(1)}, u32[]{:S(2)}, u32[]{:S(2)}) collective-permute-start(bf16[16,256]{1,0:T(8,128)(2,1)S(1)} %get-tuple-element.62), channel_id=1, source_target_pairs={{8,0},{16,8},{24,16},{32,24},{40,32},{48,40},{56,48},{64,56},{72,6... | collective-permute-start | bytes 24584 | tf_op jit(solution)/shard_map/ppermute | solution.py:327
  148.4 7.8 %collective-permute-done.14.refs_2_ = bf16[16,256]{1,0:T(8,128)(2,1)S(1)} collective-permute-done((bf16[16,256]{1,0:T(8,128)(2,1)S(1)}, bf16[16,256]{1,0:T(8,128)(2,1)S(1)}, u32[]{:S(2)}, u32[]{:S(2)}) %collective-permute-start.14) | collective-permute-done | bytes 8224 | tf_op jit(solution)/shard_map/ppermute | solution.py:326
  (92 shorter events, 32.6 us)
Async XLA Ops:
  2.3 10.1 %collective-permute-start = (bf16[48,256]{1,0:T(8,128)(2,1)S(1)}, bf16[48,256]{1,0:T(8,128)(2,1)S(1)}, u32[]{:S(2)}, u32[]{:S(2)}) collective-permute-start(bf16[48,256]{1,0:T(8,128)(2,1)S(1)} %get-tuple-element.31), channel_id=1, source_target_pairs={{0,8},{8,16},{16,24},{24,32},{32,40},{40,48},{48,56},{56,64},{64,7... | collective-permute-start | bytes 73736 | tf_op jit(solution)/shard_map/ppermute | solution.py:326
  5.7 8.2 %collective-permute-start.1 = (bf16[48,256]{1,0:T(8,128)(2,1)S(1)}, bf16[48,256]{1,0:T(8,128)(2,1)S(1)}, u32[]{:S(2)}, u32[]{:S(2)}) collective-permute-start(bf16[48,256]{1,0:T(8,128)(2,1)S(1)} %get-tuple-element.32), channel_id=1, source_target_pairs={{8,0},{16,8},{24,16},{32,24},{40,32},{48,40},{56,48},{64,56},{72,6... | collective-permute-start | bytes 73736 | tf_op jit(solution)/shard_map/ppermute | solution.py:327
  13.8 29.2 %collective-permute-start.4 = (bf16[512,256]{1,0:T(8,128)(2,1)}, bf16[512,256]{1,0:T(8,128)(2,1)S(1)}, u32[]{:S(2)}, u32[]{:S(2)}) collective-permute-start(bf16[512,256]{1,0:T(8,128)(2,1)} %m0.1), channel_id=1, source_target_pairs={{0,4},{2,6},{4,0},{6,2},{1,5},{3,7},{5,1},{7,3},{8,12},{10,14},{12... | collective-permute-start | bytes 786440 | tf_op jit(solution)/shard_map/ppermute | solution.py:334
  24.8 21.3 %collective-permute-start.3 = (bf16[512,256]{1,0:T(8,128)(2,1)}, bf16[512,256]{1,0:T(8,128)(2,1)S(1)}, u32[]{:S(2)}, u32[]{:S(2)}) collective-permute-start(bf16[512,256]{1,0:T(8,128)(2,1)} %m0.1), channel_id=1, source_target_pairs={{0,6},{2,0},{4,2},{6,4},{1,7},{3,1},{5,3},{7,5},{8,14},{10,8},{12,... | collective-permute-start | bytes 786440 | tf_op jit(solution)/shard_map/ppermute | solution.py:334
  26.7 20.4 %collective-permute-start.2 = (bf16[512,256]{1,0:T(8,128)(2,1)}, bf16[512,256]{1,0:T(8,128)(2,1)S(1)}, u32[]{:S(2)}, u32[]{:S(2)}) collective-permute-start(bf16[512,256]{1,0:T(8,128)(2,1)} %m0.1), channel_id=1, source_target_pairs={{0,2},{2,4},{4,6},{6,0},{1,3},{3,5},{5,7},{7,1},{8,10},{10,12},{12... | collective-permute-start | bytes 786440 | tf_op jit(solution)/shard_map/ppermute | solution.py:334
  32.3 20.9 %copy-start.18 = (s32[5]{0:T(128)}, s32[5]{0:T(128)S(1)}, u32[]{:S(2)}) copy-start(s32[5]{0:T(128)S(1)} %stack.55.place.refs_0_) | copy-start | bytes 64
  47.1 4.6 %collective-permute-start.5 = (bf16[2,512,256]{2,1,0:T(8,128)(2,1)S(1)}, bf16[2,512,256]{2,1,0:T(8,128)(2,1)S(1)}, u32[]{:S(2)}, u32[]{:S(2)}) collective-permute-start(bf16[2,512,256]{2,1,0:T(8,128)(2,1)S(1)} %pad_maximum_fusion), channel_id=1, source_target_pairs={{0,1},{1,0},{2,3},{3,2},{4,5},{5,4},{6,7},{7,6},{8,9},{9,8},{10,11... | collective-permute-start | bytes 1572872 | tf_op jit(solution)/shard_map/ppermute | solution.py:339
  49.1 31.6 %copy-start.3 = (bf16[512,256]{1,0:T(8,128)(2,1)S(1)}, bf16[512,256]{1,0:T(8,128)(2,1)}, u32[]{:S(2)}) copy-start(bf16[512,256]{1,0:T(8,128)(2,1)} %saved.3) | copy-start | bytes 786436
  49.2 31.6 %copy-start.15 = (bf16[48,256]{1,0:T(8,128)(2,1)S(1)}, bf16[48,256]{1,0:T(8,128)(2,1)}, u32[]{:S(2)}) copy-start(bf16[48,256]{1,0:T(8,128)(2,1)} %copy-done.14) | copy-start | bytes 73732
  49.2 31.6 %copy-start.17 = (bf16[48,256]{1,0:T(8,128)(2,1)S(1)}, bf16[48,256]{1,0:T(8,128)(2,1)}, u32[]{:S(2)}) copy-start(bf16[48,256]{1,0:T(8,128)(2,1)} %copy-done.16) | copy-start | bytes 73732
  49.2 4.1 %collective-permute-start.6 = (bf16[2,512,256]{2,1,0:T(8,128)(2,1)S(1)}, bf16[2,512,256]{2,1,0:T(8,128)(2,1)S(1)}, u32[]{:S(2)}, u32[]{:S(2)}) collective-permute-start(bf16[2,512,256]{2,1,0:T(8,128)(2,1)S(1)} %pad_maximum_fusion.1), channel_id=1, source_target_pairs={{0,1},{1,0},{2,3},{3,2},{4,5},{5,4},{6,7},{7,6},{8,9},{9,8},{10,11... | collective-permute-start | bytes 1572872 | tf_op jit(solution)/shard_map/ppermute | solution.py:339
  54.6 12.2 %collective-permute-start.7 = (bf16[32,256]{1,0:T(8,128)(2,1)S(1)}, bf16[32,256]{1,0:T(8,128)(2,1)S(1)}, u32[]{:S(2)}, u32[]{:S(2)}) collective-permute-start(bf16[32,256]{1,0:T(8,128)(2,1)S(1)} %get-tuple-element.43), channel_id=1, source_target_pairs={{0,8},{8,16},{16,24},{24,32},{32,40},{40,48},{48,56},{56,64},{64,7... | collective-permute-start | bytes 49160 | tf_op jit(solution)/shard_map/ppermute | solution.py:326
  56.5 11.7 %collective-permute-start.8 = (bf16[32,256]{1,0:T(8,128)(2,1)S(1)}, bf16[32,256]{1,0:T(8,128)(2,1)S(1)}, u32[]{:S(2)}, u32[]{:S(2)}) collective-permute-start(bf16[32,256]{1,0:T(8,128)(2,1)S(1)} %get-tuple-element.44), channel_id=1, source_target_pairs={{8,0},{16,8},{24,16},{32,24},{40,32},{48,40},{56,48},{64,56},{72,6... | collective-permute-start | bytes 49160 | tf_op jit(solution)/shard_map/ppermute | solution.py:327
  68.6 21.7 %collective-permute-start.11 = (bf16[512,256]{1,0:T(8,128)(2,1)S(1)}, bf16[512,256]{1,0:T(8,128)(2,1)}, u32[]{:S(2)}, u32[]{:S(2)}) collective-permute-start(bf16[512,256]{1,0:T(8,128)(2,1)S(1)} %shard_map.114.m0.up_row.refs_0_), channel_id=1, source_target_pairs={{0,4},{2,6},{4,0},{6,2},{1,5},{3,7},{5,1},{7,3},{8,12},{10,14},{12... | collective-permute-start | bytes 786440 | tf_op jit(solution)/shard_map/ppermute | solution.py:334
  74.0 20.7 %collective-permute-start.10 = (bf16[512,256]{1,0:T(8,128)(2,1)S(1)}, bf16[512,256]{1,0:T(8,128)(2,1)}, u32[]{:S(2)}, u32[]{:S(2)}) collective-permute-start(bf16[512,256]{1,0:T(8,128)(2,1)S(1)} %shard_map.114.m0.up_row.refs_0_), channel_id=1, source_target_pairs={{0,6},{2,0},{4,2},{6,4},{1,7},{3,1},{5,3},{7,5},{8,14},{10,8},{12,... | collective-permute-start | bytes 786440 | tf_op jit(solution)/shard_map/ppermute | solution.py:334
  76.4 21.2 %collective-permute-start.9 = (bf16[512,256]{1,0:T(8,128)(2,1)S(1)}, bf16[512,256]{1,0:T(8,128)(2,1)}, u32[]{:S(2)}, u32[]{:S(2)}) collective-permute-start(bf16[512,256]{1,0:T(8,128)(2,1)S(1)} %shard_map.114.m0.up_row.refs_0_), channel_id=1, source_target_pairs={{0,2},{2,4},{4,6},{6,0},{1,3},{3,5},{5,7},{7,1},{8,10},{10,12},{12... | collective-permute-start | bytes 786440 | tf_op jit(solution)/shard_map/ppermute | solution.py:334
  83.2 23.8 %all-to-all-start.1 = ((bf16[4,64,2048]{2,1,0:T(8,128)(2,1)}), bf16[4,64,2048]{2,1,0:T(8,128)(2,1)S(1)}, u32[]{:S(2)}, u32[]{:S(2)}) async-start(bf16[4,64,2048]{2,1,0:T(8,128)(2,1)} %bitcast.23), calls=%async_computation.1 | async-start | bytes 2097152 | tf_op jit(solution)/shard_map/all_to_all | solution.py:429
  95.7 5.4 %collective-permute-start.13 = (bf16[2,512,256]{2,1,0:T(8,128)(2,1)S(1)}, bf16[2,512,256]{2,1,0:T(8,128)(2,1)S(1)}, u32[]{:S(2)}, u32[]{:S(2)}) collective-permute-start(bf16[2,512,256]{2,1,0:T(8,128)(2,1)S(1)} %pad_maximum_fusion.3), channel_id=1, source_target_pairs={{0,1},{1,0},{2,3},{3,2},{4,5},{5,4},{6,7},{7,6},{8,9},{9,8},{10,11... | collective-permute-start | bytes 1572872 | tf_op jit(solution)/shard_map/ppermute | solution.py:339
  98.7 3.9 %collective-permute-start.12 = (bf16[2,512,256]{2,1,0:T(8,128)(2,1)S(1)}, bf16[2,512,256]{2,1,0:T(8,128)(2,1)S(1)}, u32[]{:S(2)}, u32[]{:S(2)}) collective-permute-start(bf16[2,512,256]{2,1,0:T(8,128)(2,1)S(1)} %pad_maximum_fusion.2), channel_id=1, source_target_pairs={{0,1},{1,0},{2,3},{3,2},{4,5},{5,4},{6,7},{7,6},{8,9},{9,8},{10,11... | collective-permute-start | bytes 1572872 | tf_op jit(solution)/shard_map/ppermute | solution.py:339
  107.0 24.2 %all-to-all-start = ((bf16[8,32,2304]{2,1,0:T(8,128)(2,1)}), bf16[8,32,2304]{2,1,0:T(8,128)(2,1)S(1)}, u32[]{:S(2)}, u32[]{:S(2)}) async-start(bf16[8,32,2304]{2,1,0:T(8,128)(2,1)} %bitcast.22), calls=%async_computation | async-start | bytes 2359296 | tf_op jit(solution)/shard_map/all_to_all | solution.py:447
  113.5 17.6 %collective-permute-start.16 = (bf16[32,2048]{1,0:T(8,128)(2,1)S(1)}, bf16[32,2048]{1,0:T(8,128)(2,1)S(1)}, u32[]{:S(2)}, u32[]{:S(2)}) collective-permute-start(bf16[32,2048]{1,0:T(8,128)(2,1)S(1)} %get-tuple-element.54), channel_id=1, source_target_pairs={{0,32},{32,0},{1,33},{33,1},{2,34},{34,2},{3,35},{35,3},{4,36},{36... | collective-permute-start | bytes 393224 | tf_op jit(solution)/shard_map/ppermute | solution.py:437
  132.1 25.4 %all-to-all-start.2 = ((bf16[8,4,5632]{2,1,0:T(4,128)(2,1)}), bf16[8,4,5632]{2,1,0:T(4,128)(2,1)S(1)}, u32[]{:S(2)}, u32[]{:S(2)}) async-start(bf16[8,4,5632]{2,1,0:T(4,128)(2,1)} %shard_map.119), calls=%async_computation.2 | async-start | bytes 720896 | tf_op jit(solution)/shard_map/all_to_all | solution.py:454
  141.5 6.9 %collective-permute-start.15 = (bf16[16,256]{1,0:T(8,128)(2,1)S(1)}, bf16[16,256]{1,0:T(8,128)(2,1)S(1)}, u32[]{:S(2)}, u32[]{:S(2)}) collective-permute-start(bf16[16,256]{1,0:T(8,128)(2,1)S(1)} %get-tuple-element.62), channel_id=1, source_target_pairs={{8,0},{16,8},{24,16},{32,24},{40,32},{48,40},{56,48},{64,56},{72,6... | collective-permute-start | bytes 24584 | tf_op jit(solution)/shard_map/ppermute | solution.py:327
  146.4 9.8 %collective-permute-start.14 = (bf16[16,256]{1,0:T(8,128)(2,1)S(1)}, bf16[16,256]{1,0:T(8,128)(2,1)S(1)}, u32[]{:S(2)}, u32[]{:S(2)}) collective-permute-start(bf16[16,256]{1,0:T(8,128)(2,1)S(1)} %get-tuple-element.63), channel_id=1, source_target_pairs={{0,8},{8,16},{16,24},{24,32},{32,40},{40,48},{48,56},{56,64},{64,7... | collective-permute-start | bytes 24584 | tf_op jit(solution)/shard_map/ppermute | solution.py:326
  (25 other events, 187.9 us)

commit v4 on v3

--- a/solution.py
+++ b/solution.py
@@ -42,24 +42,57 @@
     return (pre_act * half, derivative)
 
 
-def call(kernel, outs, scratch, in_specs, *operands):
+def call(kernel, outs, scratch, in_specs, *operands, out_specs=None):
     extra = {} if in_specs is None else {"in_specs": in_specs, "grid": (1,)}
+    if out_specs is not None:
+        extra["out_specs"] = out_specs
     return pl.pallas_call(
         kernel,
         out_shape=outs,
         scratch_shapes=scratch,
-        compiler_params=pltpu.CompilerParams(vmem_limit_bytes=40 << 20),
+        compiler_params=pltpu.CompilerParams(vmem_limit_bytes=16 << 20),
         **extra,
     )(*operands)
 
 
+def call_staged(kernel, outs, scratch, place, *operands):
+    count = len(operands)
+    lead = 0 if place is None else 1
+
+    def staged(*refs):
+        head, sources, rest = refs[:lead], refs[lead : lead + count], refs[lead + count :]
+        held, sems = rest[-count - 1 : -1], rest[-1]
+        loads = [
+            pltpu.make_async_copy(sources[index], held[index], sems.at[index])
+            for index in range(count)
+        ]
+        for load in loads:
+            load.start()
+        for load in loads:
+            load.wait()
+        kernel(*head, *held, *rest[: -count - 1])
+
+    smem = pl.BlockSpec(memory_space=pltpu.SMEM)
+    hbm = pl.BlockSpec(memory_space=pltpu.HBM)
+    operands = [pltpu.with_memory_space_constraint(cells, pltpu.HBM) for cells in operands]
+    return pl.pallas_call(
+        staged,
+        out_shape=outs,
+        in_specs=[smem] * lead + [hbm] * count,
+        scratch_shapes=list(scratch)
+        + [pltpu.VMEM(cells.shape, cells.dtype) for cells in operands]
+        + [pltpu.SemaphoreType.DMA((count,))],
+        compiler_params=pltpu.CompilerParams(vmem_limit_bytes=24 << 20),
+    )(*(() if place is None else (place,)), *operands)
+
+
 def shape(dims, kind):
     return jax.ShapeDtypeStruct(dims, kind)
 
 
-def pack_kernel(saved_head, saved_tail, ids, next_out, prev_out):
-    for out, rows, row in ((next_out, saved_tail, 3), (prev_out, saved_head, 0)):
-        out[:EDGE] = rows[...]
+def pack_kernel(saved, ids, next_out, prev_out):
+    for out, begin, row in ((next_out, ROWS - EDGE, 3), (prev_out, 0, 0)):
+        out[:EDGE] = saved[begin : begin + EDGE]
         line = jnp.broadcast_to(ids[row : row + 1].astype(F32), (MESSAGE - EDGE, 128))
         out[EDGE:] = jnp.concatenate([line, line], axis=1).astype(BF16)
 
@@ -195,17 +228,24 @@
     tail_out[...] = grad[ROWS - HIGH_REACH :]
 
 
-def outer_product(act, mine, pairs, out):
+def outer_product(act, mine, pairs, out, stage, sems):
+    copies = []
     for index in range(2 * len(STEPS)):
         half = index % len(STEPS)
         piece = mine[half][...] if index < len(STEPS) else pairs[half // 2][half % 2]
-        out[:, index * LANES : (index + 1) * LANES] = jnp.dot(
-            act[...], piece, preferred_element_type=F32
-        ).astype(BF16)
-
-
-def upper_outer_kernel(act, m0, m1, m2, m3, p0, p1, grad, before, saved, after, out, tap_out, wide):
-    outer_product(act, (m0, m1, m2, m3), (p0, p1), out)
+        lanes = slice(index * LANES, (index + 1) * LANES)
+        stage[:, lanes] = jnp.dot(act[...], piece, preferred_element_type=F32).astype(BF16)
+        copies.append(
+            pltpu.make_async_copy(stage.at[:, lanes], out.at[:, lanes], sems.at[index])
+        )
+        copies[-1].start()
+    return copies
+
+
+def upper_outer_kernel(
+    act, m0, m1, m2, m3, p0, p1, grad, before, saved, after, out, tap_out, wide, stage, sems
+):
+    copies = outer_product(act, (m0, m1, m2, m3), (p0, p1), out, stage, sems)
     wide[:HIGH_REACH] = before[:HIGH_REACH].astype(F32)
     wide[HIGH_REACH : HIGH_REACH + ROWS] = saved[...].astype(F32)
     wide[HIGH_REACH + ROWS :] = after[:HIGH_REACH].astype(F32)
@@ -220,16 +260,18 @@
     tap_out[...] = jnp.zeros_like(tap_out)
     for index in range(TAPS):
         tap_out[index : index + 1] = jnp.sum(sums[index], axis=0, keepdims=True)
+    for copy in copies:
+        copy.wait()
 
 
 def lower_kernel(
     place, act, m0, m1, m2, m3, p0, p1, weights, slope, hot, up_row, embedding, conv, upper_taps,
-    out, grad_out, small, table,
+    out, grad_out, small, table, stage, sems,
 ):
     mine, pairs = (m0, m1, m2, m3), (p0, p1)
     grad = (product_over_blocks(place, mine, pairs, weights) * slope[...]).astype(BF16)
     grad_out[...] = grad
-    outer_product(act, mine, pairs, out)
+    copies = outer_product(act, mine, pairs, out, stage, sems)
     picked = jnp.dot(hot[...], grad, preferred_element_type=F32)
     embed = jnp.dot(hot[32:48], up_row[...], preferred_element_type=F32)[:8]
     table[...] = jnp.zeros_like(table)
@@ -243,7 +285,13 @@
     small[TAPS + VOCAB : 2 * TAPS + VOCAB] = upper_taps[:TAPS]
     packed = small[...].astype(BF16)
     for index in range(LANES // 32):
-        out[index * 32 : (index + 1) * 32, 8 * LANES :] = packed
+        stage[index * 32 : (index + 1) * 32, 8 * LANES :] = packed
+    last = pltpu.make_async_copy(
+        stage.at[:, 8 * LANES :], out.at[:, 8 * LANES :], sems.at[8]
+    )
+    last.start()
+    for copy in copies + [last]:
+        copy.wait()
 
 
 def upper_half_kernel(place, pieces, keep, send, total):
@@ -290,8 +338,8 @@
         return running[row % 4 : row % 4 + 1, begin : begin + LANES]
 
     for index in range(TAPS):
-        kernel_out[0, index : index + 1] = small_row(index)
-        kernel_out[1, index : index + 1] = small_row(TAPS + VOCAB + index)
+        kernel_out[index, 0:1] = small_row(index)
+        kernel_out[index, 1:2] = small_row(TAPS + VOCAB + index)
     for index in range(VOCAB):
         embed_out[index : index + 1] = small_row(TAPS + index)
 
@@ -364,24 +412,14 @@
     turned = shape((LANES, ROWS), BF16)
 
     message = shape((MESSAGE, LANES), BF16)
-    last = ROWS // HIGH_REACH - 1
-    to_next, to_prev = call(
-        pack_kernel,
-        (message, message),
-        [],
-        [
-            pl.BlockSpec((HIGH_REACH, LANES), lambda step: (0, 0)),
-            pl.BlockSpec((HIGH_REACH, LANES), lambda step: (last, 0)),
-            vmem,
-        ],
-        saved_input, saved_input, ids,
+    to_next, to_prev = call_staged(
+        pack_kernel, (message, message), [], None, saved_input, ids
     )
     before = seq_shift(to_next, 1)
     after = seq_shift(to_prev, -1)
-    source, before, after = lax.optimization_barrier((cotangent, before, after))
-    mine = ring_copies(source)
-
-    slope_up, act_up, slope_low, act_low, masked, hot = call(
+    mine = ring_copies(cotangent)
+
+    slope_up, act_up, slope_low, act_low, masked, hot = call_staged(
         prep_kernel,
         (slab_wide, turned, slab_wide, turned, slab, shape((128, ROWS), BF16)),
         [
@@ -392,7 +430,6 @@
             pltpu.VMEM((128, LANES), F32),
             pltpu.VMEM((ROWS, LANES), BF16),
         ],
-        [smem] + [vmem] * 9,
         place, before, after, saved_input, cotangent, ids,
         span_start.reshape(-1, 128), span_length.reshape(-1, 128), embedding, conv_kernel,
     )
@@ -419,12 +456,17 @@
     mid = ring_copies(up_mid)
     mid_pairs = swapped_pairs(mid)
 
+    far_specs = (pl.BlockSpec(memory_space=pltpu.HBM), vmem)
     upper_outer, upper_taps = call(
         upper_outer_kernel,
-        (shape((LANES, 8 * LANES), BF16), shape((16, LANES), F32)),
-        [pltpu.VMEM((ROWS + 2 * HIGH_REACH, LANES), F32)],
-        None,
-        act_up, *mine, *pairs, grad_upper, before, saved_input, after,
+        (pltpu.HBM((LANES, 8 * LANES), BF16), shape((16, LANES), F32)),
+        [
+            pltpu.VMEM((ROWS + 2 * HIGH_REACH, LANES), F32),
+            pltpu.VMEM((LANES, 8 * LANES), BF16),
+            pltpu.SemaphoreType.DMA((8,)),
+        ],
+        [vmem] * 11,
+        act_up, *mine, *pairs, grad_upper, before, saved_input, after, out_specs=far_specs,
     )
     pieces = lax.all_to_all(upper_outer.reshape(4, 64, 8 * LANES), "x", 0, 0)
     keep, send = call(
@@ -438,11 +480,16 @@
 
     lower_outer, grad_lower = call(
         lower_kernel,
-        (shape((LANES, 9 * LANES), BF16), slab),
-        [pltpu.VMEM((32, LANES), F32), pltpu.VMEM((8, LANES), F32)],
+        (pltpu.HBM((LANES, 9 * LANES), BF16), slab),
+        [
+            pltpu.VMEM((32, LANES), F32),
+            pltpu.VMEM((8, LANES), F32),
+            pltpu.VMEM((LANES, 9 * LANES), BF16),
+            pltpu.SemaphoreType.DMA((9,)),
+        ],
         [smem] + [vmem] * 7 + [weight_specs[0]] + [vmem] * 6,
         place, act_low, *mid, *mid_pairs, mix_weight, slope_low, hot, up_mid, embedding,
-        conv_kernel, upper_taps,
+        conv_kernel, upper_taps, out_specs=far_specs,
     )
     pieces = lax.all_to_all(lower_outer.reshape(8, 32, 9 * LANES), NEAR, 0, 0)
     low_before = seq_shift(grad_lower[ROWS - LOW_REACH :], 1)
@@ -458,12 +505,12 @@
 
     weight_grad, kernel_grad, embed_grad = call(
         finish,
-        (shape((2, 4, 8 * LANES), F32), shape((2, TAPS, LANES), F32), shape((VOCAB, LANES), F32)),
+        (shape((2, 4, 8 * LANES), F32), shape((TAPS, 2, LANES), F32), shape((VOCAB, LANES), F32)),
         [],
         [smem, vmem],
         place, pieces,
     )
-    return (input_grad, weight_grad, kernel_grad, embed_grad)
+    return (input_grad, weight_grad, kernel_grad.transpose(1, 0, 2), embed_grad)
 
 
 def solution(mesh):

time: 160 us -> 154 us (0.963)
  waiting for transfers between devices: 39.4 us -> 29.9 us
  local copies, waits for them, and re-layouts: 11.2 us -> 3.38 us
  starting transfers between devices: 90.3 us -> 96.3 us
  Pallas kernels: 15.1 us -> 18.9 us
    ppermute x6, waiting for transfers between devices: 12 us -> 3.75 us  [ring_copies(): lax.ppermute(slab, 'zh', [(i, (i + step) % count) for i in range(count)])]
    pallas_call x0 -> x2, Pallas kernels: none -> 8.09 us  [call_staged(): pl.pallas_call(staged, out_shape=outs, in_specs=[smem] * lead + [hbm] * c...]
    unnamed x60 -> x41, local copies, waits for them, and re-layouts: 11.1 us -> 3.29 us
    all_to_all x1, starting transfers between devices: 3.51 us -> 8.81 us  [on_device(): pieces = lax.all_to_all(upper_outer.reshape(4, 64, 8 * LANES), 'x', 0, 0)]
    all_to_all x1, starting transfers between devices: 5.76 us -> 10.2 us  [on_device(): pieces = lax.all_to_all(lower_outer.reshape(8, 32, 9 * LANES), NEAR, 0, 0)]
    pallas_call x10 -> x8, Pallas kernels: 15.1 us -> 10.8 us  [call(): pl.pallas_call(kernel, out_shape=outs, scratch_shapes=scratch, compiler_p...]
    all_to_all x1, starting transfers between devices: 9.4 us -> 7.21 us  [on_device(): pieces = lax.all_to_all(middle, 'y', 0, 0)]
    ppermute x3, starting transfers between devices: 21.9 us -> 20.2 us  [seq_shift(): return lax.ppermute(cells, SEQ, [(i + 1, i) for i in range(count - 1)])]
  transfers between devices with their start and end apart: 20 -> 20, of which waited for: 10 -> 7; matrix products, arithmetic and copies ran while one was open for 2% -> 2% of each run, Pallas kernels for 7% -> 10%
where the time goes in v4:
time: 154 us; the launch traced here: 153 us
  starting transfers between devices  96.3 us (63%)
  waiting for transfers between devices  29.9 us (19%)
  Pallas kernels  18.9 us (12%)
  other arithmetic  3.5 us (2%)
  local copies, waits for them, and re-layouts  3.38 us (2%)
    ppermute x6, starting transfers between devices, ring_copies(): lax.ppermute(slab, 'zh', [(i, (i + step) % count) for i in range(count)])  30.5 us
    ppermute x3, starting transfers between devices, seq_shift(): return lax.ppermute(cells, SEQ, [(i + 1, i) for i in range(count - 1)])  20.2 us
    ppermute x1, waiting for transfers between devices, on_device(): received = lax.ppermute(send, 'zl', [(0, 1), (1, 0)])  13.5 us
    pallas_call x8, Pallas kernels, call(): pl.pallas_call(kernel, out_shape=outs, scratch_shapes=scratch, compiler_p...  10.8 us
    all_to_all x1, starting transfers between devices, on_device(): pieces = lax.all_to_all(lower_outer.reshape(8, 32, 9 * LANES), NEAR, 0, 0)  10.2 us
    all_to_all x1, starting transfers between devices, on_device(): pieces = lax.all_to_all(upper_outer.reshape(4, 64, 8 * LANES), 'x', 0, 0)  8.81 us
    ppermute x4, starting transfers between devices, core_swap(): return lax.ppermute(cells, 'core', [(0, 1), (1, 0)])  8.3 us
    pallas_call x2, Pallas kernels, call_staged(): pl.pallas_call(staged, out_shape=outs, in_specs=[smem] * lead + [hbm] * c...  8.09 us
  transfers between devices with their start and end apart: 20, of which 7 were waited for; matrix products, arithmetic and copies ran while one was open for 2% of the time, Pallas kernels for 10%

profile of v4, /device:TPU:32, one launch (start us, length us, event | category | flops | bytes accessed | tf_op | source)
XLA Modules:
  0.0 153.1 jit_solution(3420552466759311787)
XLA Ops:
  0.6 10.9 %collective-permute-start.4 = (bf16[512,256]{1,0:T(8,128)(2,1)}, bf16[512,256]{1,0:T(8,128)(2,1)S(1)}, u32[]{:S(2)}, u32[]{:S(2)}) collective-permute-start(bf16[512,256]{1,0:T(8,128)(2,1)} %m0.3), channel_id=1, source_target_pairs={{0,4},{2,6},{4,0},{6,2},{1,5},{3,7},{5,1},{7,3},{8,12},{10,14},{12... | collective-permute-start | bytes 786440 | tf_op jit(solution)/shard_map/ppermute | solution.py:382
  11.6 1.9 %collective-permute-start.3 = (bf16[512,256]{1,0:T(8,128)(2,1)}, bf16[512,256]{1,0:T(8,128)(2,1)S(1)}, u32[]{:S(2)}, u32[]{:S(2)}) collective-permute-start(bf16[512,256]{1,0:T(8,128)(2,1)} %m0.3), channel_id=1, source_target_pairs={{0,6},{2,0},{4,2},{6,4},{1,7},{3,1},{5,3},{7,5},{8,14},{10,8},{12,... | collective-permute-start | bytes 786440 | tf_op jit(solution)/shard_map/ppermute | solution.py:382
  13.5 4.8 %collective-permute-start.2 = (bf16[512,256]{1,0:T(8,128)(2,1)}, bf16[512,256]{1,0:T(8,128)(2,1)S(1)}, u32[]{:S(2)}, u32[]{:S(2)}) collective-permute-start(bf16[512,256]{1,0:T(8,128)(2,1)} %m0.3), channel_id=1, source_target_pairs={{0,2},{2,4},{4,6},{6,0},{1,3},{3,5},{5,7},{7,1},{8,10},{10,12},{12... | collective-permute-start | bytes 786440 | tf_op jit(solution)/shard_map/ppermute | solution.py:382
  19.3 3.4 %collective-permute-start = (bf16[48,256]{1,0:T(8,128)(2,1)S(1)}, bf16[48,256]{1,0:T(8,128)(2,1)S(1)}, u32[]{:S(2)}, u32[]{:S(2)}) collective-permute-start(bf16[48,256]{1,0:T(8,128)(2,1)S(1)} %get-tuple-element.28), channel_id=1, source_target_pairs={{0,8},{8,16},{16,24},{24,32},{32,40},{40,48},{48,56},{56,64},{64,7... | collective-permute-start | bytes 73736 | tf_op jit(solution)/shard_map/ppermute | solution.py:374
  22.7 6.7 %collective-permute-start.1 = (bf16[48,256]{1,0:T(8,128)(2,1)S(1)}, bf16[48,256]{1,0:T(8,128)(2,1)S(1)}, u32[]{:S(2)}, u32[]{:S(2)}) collective-permute-start(bf16[48,256]{1,0:T(8,128)(2,1)S(1)} %get-tuple-element.29), channel_id=1, source_target_pairs={{8,0},{16,8},{24,16},{32,24},{40,32},{48,40},{56,48},{64,56},{72,6... | collective-permute-start | bytes 73736 | tf_op jit(solution)/shard_map/ppermute | solution.py:375
  31.5 7.1 %shard_map.112 = (f32[512,256]{1,0:T(8,128)S(1)}, bf16[256,512]{1,0:T(8,128)(2,1)S(1)}, f32[512,256]{1,0:T(8,128)S(1)}, bf16[256,512]{1,0:T(8,128)(2,1)S(1)}, bf...) custom-call(s32[5]{0:T(128)S(1)} %stack.55.refs_0_.place, bf16[48,256]{1,0:T(8,128)(2,1)} %copy-done.10, ...), custom_call_target="tpu_custom_call" | custom-call | tf_op jit(solution)/shard_map/pallas_call | solution.py:78
  40.0 1.9 %collective-permute-start.5 = (bf16[2,512,256]{2,1,0:T(8,128)(2,1)S(1)}, bf16[2,512,256]{2,1,0:T(8,128)(2,1)S(1)}, u32[]{:S(2)}, u32[]{:S(2)}) collective-permute-start(bf16[2,512,256]{2,1,0:T(8,128)(2,1)S(1)} %pad_maximum_fusion), channel_id=1, source_target_pairs={{0,1},{1,0},{2,3},{3,2},{4,5},{5,4},{6,7},{7,6},{8,9},{9,8},{10,11... | collective-permute-start | bytes 1572872 | tf_op jit(solution)/shard_map/ppermute | solution.py:387
  42.0 2.5 %collective-permute-start.6 = (bf16[2,512,256]{2,1,0:T(8,128)(2,1)S(1)}, bf16[2,512,256]{2,1,0:T(8,128)(2,1)S(1)}, u32[]{:S(2)}, u32[]{:S(2)}) collective-permute-start(bf16[2,512,256]{2,1,0:T(8,128)(2,1)S(1)} %pad_maximum_fusion.1), channel_id=1, source_target_pairs={{0,1},{1,0},{2,3},{3,2},{4,5},{5,4},{6,7},{7,6},{8,9},{9,8},{10,11... | collective-permute-start | bytes 1572872 | tf_op jit(solution)/shard_map/ppermute | solution.py:387
  47.4 1.9 %collective-permute-start.7 = (bf16[32,256]{1,0:T(8,128)(2,1)S(1)}, bf16[32,256]{1,0:T(8,128)(2,1)S(1)}, u32[]{:S(2)}, u32[]{:S(2)}) collective-permute-start(bf16[32,256]{1,0:T(8,128)(2,1)S(1)} %get-tuple-element.37), channel_id=1, source_target_pairs={{0,8},{8,16},{16,24},{24,32},{32,40},{40,48},{48,56},{56,64},{64,7... | collective-permute-start | bytes 49160 | tf_op jit(solution)/shard_map/ppermute | solution.py:374
  49.3 8.9 %collective-permute-start.8 = (bf16[32,256]{1,0:T(8,128)(2,1)S(1)}, bf16[32,256]{1,0:T(8,128)(2,1)S(1)}, u32[]{:S(2)}, u32[]{:S(2)}) collective-permute-start(bf16[32,256]{1,0:T(8,128)(2,1)S(1)} %get-tuple-element.38), channel_id=1, source_target_pairs={{8,0},{16,8},{24,16},{32,24},{40,32},{48,40},{56,48},{64,56},{72,6... | collective-permute-start | bytes 49160 | tf_op jit(solution)/shard_map/ppermute | solution.py:375
  60.0 4.9 %collective-permute-start.11 = (bf16[512,256]{1,0:T(8,128)(2,1)S(1)}, bf16[512,256]{1,0:T(8,128)(2,1)}, u32[]{:S(2)}, u32[]{:S(2)}) collective-permute-start(bf16[512,256]{1,0:T(8,128)(2,1)S(1)} %shard_map.114.m0.up_row.refs_0_), channel_id=1, source_target_pairs={{0,4},{2,6},{4,0},{6,2},{1,5},{3,7},{5,1},{7,3},{8,12},{10,14},{12... | collective-permute-start | bytes 786440 | tf_op jit(solution)/shard_map/ppermute | solution.py:382
  64.9 6.0 %collective-permute-start.10 = (bf16[512,256]{1,0:T(8,128)(2,1)S(1)}, bf16[512,256]{1,0:T(8,128)(2,1)}, u32[]{:S(2)}, u32[]{:S(2)}) collective-permute-start(bf16[512,256]{1,0:T(8,128)(2,1)S(1)} %shard_map.114.m0.up_row.refs_0_), channel_id=1, source_target_pairs={{0,6},{2,0},{4,2},{6,4},{1,7},{3,1},{5,3},{7,5},{8,14},{10,8},{12,... | collective-permute-start | bytes 786440 | tf_op jit(solution)/shard_map/ppermute | solution.py:382
  70.9 1.9 %collective-permute-start.9 = (bf16[512,256]{1,0:T(8,128)(2,1)S(1)}, bf16[512,256]{1,0:T(8,128)(2,1)}, u32[]{:S(2)}, u32[]{:S(2)}) collective-permute-start(bf16[512,256]{1,0:T(8,128)(2,1)S(1)} %shard_map.114.m0.up_row.refs_0_), channel_id=1, source_target_pairs={{0,2},{2,4},{4,6},{6,0},{1,3},{3,5},{5,7},{7,1},{8,10},{10,12},{12... | collective-permute-start | bytes 786440 | tf_op jit(solution)/shard_map/ppermute | solution.py:382
  75.1 8.8 %all-to-all-start.1 = ((bf16[4,64,2048]{2,1,0:T(8,128)(2,1)}), bf16[4,64,2048]{2,1,0:T(8,128)(2,1)S(1)}, u32[]{:S(2)}, u32[]{:S(2)}) async-start(bf16[4,64,2048]{2,1,0:T(8,128)(2,1)} %bitcast.24), calls=%async_computation.1 | async-start | bytes 2097152 | tf_op jit(solution)/shard_map/all_to_all | solution.py:471
  85.1 1.9 %collective-permute-start.13 = (bf16[2,512,256]{2,1,0:T(8,128)(2,1)S(1)}, bf16[2,512,256]{2,1,0:T(8,128)(2,1)S(1)}, u32[]{:S(2)}, u32[]{:S(2)}) collective-permute-start(bf16[2,512,256]{2,1,0:T(8,128)(2,1)S(1)} %pad_maximum_fusion.3), channel_id=1, source_target_pairs={{0,1},{1,0},{2,3},{3,2},{4,5},{5,4},{6,7},{7,6},{8,9},{9,8},{10,11... | collective-permute-start | bytes 1572872 | tf_op jit(solution)/shard_map/ppermute | solution.py:387
  87.0 3.7 %collective-permute-done.9.m1 = bf16[512,256]{1,0:T(8,128)(2,1)} collective-permute-done((bf16[512,256]{1,0:T(8,128)(2,1)S(1)}, bf16[512,256]{1,0:T(8,128)(2,1)}, u32[]{:S(2)}, u32[]{:S(2)}) %collective-permute-start.9) | collective-permute-done | bytes 262176 | tf_op jit(solution)/shard_map/ppermute | solution.py:382
  91.8 1.9 %collective-permute-start.12 = (bf16[2,512,256]{2,1,0:T(8,128)(2,1)S(1)}, bf16[2,512,256]{2,1,0:T(8,128)(2,1)S(1)}, u32[]{:S(2)}, u32[]{:S(2)}) collective-permute-start(bf16[2,512,256]{2,1,0:T(8,128)(2,1)S(1)} %pad_maximum_fusion.2), channel_id=1, source_target_pairs={{0,1},{1,0},{2,3},{3,2},{4,5},{5,4},{6,7},{7,6},{8,9},{9,8},{10,11... | collective-permute-start | bytes 1572872 | tf_op jit(solution)/shard_map/ppermute | solution.py:387
  95.6 3.3 %shard_map.116 = (bf16[256,2304]{1,0:T(8,128)(2,1)}, bf16[512,256]{1,0:T(8,128)(2,1)S(1)}) custom-call(s32[5]{0:T(128)S(1)} %copy-done.15, bf16[256,512]{1,0:T(8,128)(2,1)S(1)} %copy-done.9, bf16[512,256]{1,0:T(8,128)(2,1)S(1)} %shard_map.114.m0.up_row.refs_0_, bf16[512,256]{1,0:T(8,128)(2,1)} %collective-permute-done.9.m1, ...), custom_call_target="tpu_custom_call" | custom-call | tf_op jit(solution)/shard_map/pallas_call | solution.py:49
  99.7 10.2 %all-to-all-start = ((bf16[8,32,2304]{2,1,0:T(8,128)(2,1)}), bf16[8,32,2304]{2,1,0:T(8,128)(2,1)S(1)}, u32[]{:S(2)}, u32[]{:S(2)}) async-start(bf16[8,32,2304]{2,1,0:T(8,128)(2,1)} %bitcast.23), calls=%async_computation | async-start | bytes 2359296 | tf_op jit(solution)/shard_map/all_to_all | solution.py:494
  110.6 3.9 %collective-permute-start.16 = (bf16[32,2048]{1,0:T(8,128)(2,1)S(1)}, bf16[32,2048]{1,0:T(8,128)(2,1)S(1)}, u32[]{:S(2)}, u32[]{:S(2)}) collective-permute-start(bf16[32,2048]{1,0:T(8,128)(2,1)S(1)} %get-tuple-element.48), channel_id=1, source_target_pairs={{0,32},{32,0},{1,33},{33,1},{2,34},{34,2},{3,35},{35,3},{4,36},{36... | collective-permute-start | bytes 393224 | tf_op jit(solution)/shard_map/ppermute | solution.py:479
  114.6 13.5 %collective-permute-done.16.received = bf16[32,2048]{1,0:T(8,128)(2,1)S(1)} collective-permute-done((bf16[32,2048]{1,0:T(8,128)(2,1)S(1)}, bf16[32,2048]{1,0:T(8,128)(2,1)S(1)}, u32[]{:S(2)}, u32[]{:S(2)}) %collective-permute-start.16) | collective-permute-done | bytes 131104 | tf_op jit(solution)/shard_map/ppermute | solution.py:479
  129.0 7.2 %all-to-all-start.2 = ((bf16[8,4,5632]{2,1,0:T(4,128)(2,1)}), bf16[8,4,5632]{2,1,0:T(4,128)(2,1)S(1)}, u32[]{:S(2)}, u32[]{:S(2)}) async-start(bf16[8,4,5632]{2,1,0:T(4,128)(2,1)} %shard_map.119), calls=%async_computation.2 | async-start | bytes 720896 | tf_op jit(solution)/shard_map/all_to_all | solution.py:501
  136.2 4.7 %collective-permute-start.15 = (bf16[16,256]{1,0:T(8,128)(2,1)S(1)}, bf16[16,256]{1,0:T(8,128)(2,1)S(1)}, u32[]{:S(2)}, u32[]{:S(2)}) collective-permute-start(bf16[16,256]{1,0:T(8,128)(2,1)S(1)} %get-tuple-element.52), channel_id=1, source_target_pairs={{8,0},{16,8},{24,16},{32,24},{40,32},{48,40},{56,48},{64,56},{72,6... | collective-permute-start | bytes 24584 | tf_op jit(solution)/shard_map/ppermute | solution.py:375
  142.8 7.8 %collective-permute-done.14.refs_2_ = bf16[16,256]{1,0:T(8,128)(2,1)S(1)} collective-permute-done((bf16[16,256]{1,0:T(8,128)(2,1)S(1)}, bf16[16,256]{1,0:T(8,128)(2,1)S(1)}, u32[]{:S(2)}, u32[]{:S(2)}) %collective-permute-start.14) | collective-permute-done | bytes 8224 | tf_op jit(solution)/shard_map/ppermute | solution.py:374
  (73 shorter events, 22.1 us)
Async XLA Ops:
  0.6 38.0 %collective-permute-start.4 = (bf16[512,256]{1,0:T(8,128)(2,1)}, bf16[512,256]{1,0:T(8,128)(2,1)S(1)}, u32[]{:S(2)}, u32[]{:S(2)}) collective-permute-start(bf16[512,256]{1,0:T(8,128)(2,1)} %m0.3), channel_id=1, source_target_pairs={{0,4},{2,6},{4,0},{6,2},{1,5},{3,7},{5,1},{7,3},{8,12},{10,14},{12... | collective-permute-start | bytes 786440 | tf_op jit(solution)/shard_map/ppermute | solution.py:382
  11.6 27.1 %collective-permute-start.3 = (bf16[512,256]{1,0:T(8,128)(2,1)}, bf16[512,256]{1,0:T(8,128)(2,1)S(1)}, u32[]{:S(2)}, u32[]{:S(2)}) collective-permute-start(bf16[512,256]{1,0:T(8,128)(2,1)} %m0.3), channel_id=1, source_target_pairs={{0,6},{2,0},{4,2},{6,4},{1,7},{3,1},{5,3},{7,5},{8,14},{10,8},{12,... | collective-permute-start | bytes 786440 | tf_op jit(solution)/shard_map/ppermute | solution.py:382
  13.5 25.2 %collective-permute-start.2 = (bf16[512,256]{1,0:T(8,128)(2,1)}, bf16[512,256]{1,0:T(8,128)(2,1)S(1)}, u32[]{:S(2)}, u32[]{:S(2)}) collective-permute-start(bf16[512,256]{1,0:T(8,128)(2,1)} %m0.3), channel_id=1, source_target_pairs={{0,2},{2,4},{4,6},{6,0},{1,3},{3,5},{5,7},{7,1},{8,10},{10,12},{12... | collective-permute-start | bytes 786440 | tf_op jit(solution)/shard_map/ppermute | solution.py:382
  19.3 11.5 %collective-permute-start = (bf16[48,256]{1,0:T(8,128)(2,1)S(1)}, bf16[48,256]{1,0:T(8,128)(2,1)S(1)}, u32[]{:S(2)}, u32[]{:S(2)}) collective-permute-start(bf16[48,256]{1,0:T(8,128)(2,1)S(1)} %get-tuple-element.28), channel_id=1, source_target_pairs={{0,8},{8,16},{16,24},{24,32},{32,40},{40,48},{48,56},{56,64},{64,7... | collective-permute-start | bytes 73736 | tf_op jit(solution)/shard_map/ppermute | solution.py:374
  22.7 8.2 %collective-permute-start.1 = (bf16[48,256]{1,0:T(8,128)(2,1)S(1)}, bf16[48,256]{1,0:T(8,128)(2,1)S(1)}, u32[]{:S(2)}, u32[]{:S(2)}) collective-permute-start(bf16[48,256]{1,0:T(8,128)(2,1)S(1)} %get-tuple-element.29), channel_id=1, source_target_pairs={{8,0},{16,8},{24,16},{32,24},{40,32},{48,40},{56,48},{64,56},{72,6... | collective-permute-start | bytes 73736 | tf_op jit(solution)/shard_map/ppermute | solution.py:375
  40.0 4.6 %collective-permute-start.5 = (bf16[2,512,256]{2,1,0:T(8,128)(2,1)S(1)}, bf16[2,512,256]{2,1,0:T(8,128)(2,1)S(1)}, u32[]{:S(2)}, u32[]{:S(2)}) collective-permute-start(bf16[2,512,256]{2,1,0:T(8,128)(2,1)S(1)} %pad_maximum_fusion), channel_id=1, source_target_pairs={{0,1},{1,0},{2,3},{3,2},{4,5},{5,4},{6,7},{7,6},{8,9},{9,8},{10,11... | collective-permute-start | bytes 1572872 | tf_op jit(solution)/shard_map/ppermute | solution.py:387
  42.0 17.7 %copy-start.5 = (bf16[2,9,256]{2,1,0:T(8,128)(2,1)S(1)}, bf16[2,9,256]{2,1,0:T(8,128)(2,1)}, u32[]{:S(2)}) copy-start(bf16[2,9,256]{2,1,0:T(8,128)(2,1)} %copy.12.refs_9_.refs_4_.conv) | copy-start | bytes 27652
  42.0 30.9 %copy-start.2 = (bf16[512,256]{1,0:T(8,128)(2,1)S(1)}, bf16[512,256]{1,0:T(8,128)(2,1)}, u32[]{:S(2)}) copy-start(bf16[512,256]{1,0:T(8,128)(2,1)} %saved.1) | copy-start | bytes 786436
  42.0 30.9 %copy-start.11 = (bf16[48,256]{1,0:T(8,128)(2,1)S(1)}, bf16[48,256]{1,0:T(8,128)(2,1)}, u32[]{:S(2)}) copy-start(bf16[48,256]{1,0:T(8,128)(2,1)} %copy-done.10) | copy-start | bytes 73732
  42.0 30.9 %copy-start.13 = (bf16[48,256]{1,0:T(8,128)(2,1)S(1)}, bf16[48,256]{1,0:T(8,128)(2,1)}, u32[]{:S(2)}) copy-start(bf16[48,256]{1,0:T(8,128)(2,1)} %copy-done.12) | copy-start | bytes 73732
  42.0 4.1 %collective-permute-start.6 = (bf16[2,512,256]{2,1,0:T(8,128)(2,1)S(1)}, bf16[2,512,256]{2,1,0:T(8,128)(2,1)S(1)}, u32[]{:S(2)}, u32[]{:S(2)}) collective-permute-start(bf16[2,512,256]{2,1,0:T(8,128)(2,1)S(1)} %pad_maximum_fusion.1), channel_id=1, source_target_pairs={{0,1},{1,0},{2,3},{3,2},{4,5},{5,4},{6,7},{7,6},{8,9},{9,8},{10,11... | collective-permute-start | bytes 1572872 | tf_op jit(solution)/shard_map/ppermute | solution.py:387
  47.4 10.8 %collective-permute-start.7 = (bf16[32,256]{1,0:T(8,128)(2,1)S(1)}, bf16[32,256]{1,0:T(8,128)(2,1)S(1)}, u32[]{:S(2)}, u32[]{:S(2)}) collective-permute-start(bf16[32,256]{1,0:T(8,128)(2,1)S(1)} %get-tuple-element.37), channel_id=1, source_target_pairs={{0,8},{8,16},{16,24},{24,32},{32,40},{40,48},{48,56},{56,64},{64,7... | collective-permute-start | bytes 49160 | tf_op jit(solution)/shard_map/ppermute | solution.py:374
  49.3 10.3 %collective-permute-start.8 = (bf16[32,256]{1,0:T(8,128)(2,1)S(1)}, bf16[32,256]{1,0:T(8,128)(2,1)S(1)}, u32[]{:S(2)}, u32[]{:S(2)}) collective-permute-start(bf16[32,256]{1,0:T(8,128)(2,1)S(1)} %get-tuple-element.38), channel_id=1, source_target_pairs={{8,0},{16,8},{24,16},{32,24},{40,32},{48,40},{56,48},{64,56},{72,6... | collective-permute-start | bytes 49160 | tf_op jit(solution)/shard_map/ppermute | solution.py:375
  60.0 23.9 %collective-permute-start.11 = (bf16[512,256]{1,0:T(8,128)(2,1)S(1)}, bf16[512,256]{1,0:T(8,128)(2,1)}, u32[]{:S(2)}, u32[]{:S(2)}) collective-permute-start(bf16[512,256]{1,0:T(8,128)(2,1)S(1)} %shard_map.114.m0.up_row.refs_0_), channel_id=1, source_target_pairs={{0,4},{2,6},{4,0},{6,2},{1,5},{3,7},{5,1},{7,3},{8,12},{10,14},{12... | collective-permute-start | bytes 786440 | tf_op jit(solution)/shard_map/ppermute | solution.py:382
  64.9 19.0 %collective-permute-start.10 = (bf16[512,256]{1,0:T(8,128)(2,1)S(1)}, bf16[512,256]{1,0:T(8,128)(2,1)}, u32[]{:S(2)}, u32[]{:S(2)}) collective-permute-start(bf16[512,256]{1,0:T(8,128)(2,1)S(1)} %shard_map.114.m0.up_row.refs_0_), channel_id=1, source_target_pairs={{0,6},{2,0},{4,2},{6,4},{1,7},{3,1},{5,3},{7,5},{8,14},{10,8},{12,... | collective-permute-start | bytes 786440 | tf_op jit(solution)/shard_map/ppermute | solution.py:382
  70.9 19.9 %collective-permute-start.9 = (bf16[512,256]{1,0:T(8,128)(2,1)S(1)}, bf16[512,256]{1,0:T(8,128)(2,1)}, u32[]{:S(2)}, u32[]{:S(2)}) collective-permute-start(bf16[512,256]{1,0:T(8,128)(2,1)S(1)} %shard_map.114.m0.up_row.refs_0_), channel_id=1, source_target_pairs={{0,2},{2,4},{4,6},{6,0},{1,3},{3,5},{5,7},{7,1},{8,10},{10,12},{12... | collective-permute-start | bytes 786440 | tf_op jit(solution)/shard_map/ppermute | solution.py:382
  75.1 24.6 %all-to-all-start.1 = ((bf16[4,64,2048]{2,1,0:T(8,128)(2,1)}), bf16[4,64,2048]{2,1,0:T(8,128)(2,1)S(1)}, u32[]{:S(2)}, u32[]{:S(2)}) async-start(bf16[4,64,2048]{2,1,0:T(8,128)(2,1)} %bitcast.24), calls=%async_computation.1 | async-start | bytes 2097152 | tf_op jit(solution)/shard_map/all_to_all | solution.py:471
  85.1 8.6 %collective-permute-start.13 = (bf16[2,512,256]{2,1,0:T(8,128)(2,1)S(1)}, bf16[2,512,256]{2,1,0:T(8,128)(2,1)S(1)}, u32[]{:S(2)}, u32[]{:S(2)}) collective-permute-start(bf16[2,512,256]{2,1,0:T(8,128)(2,1)S(1)} %pad_maximum_fusion.3), channel_id=1, source_target_pairs={{0,1},{1,0},{2,3},{3,2},{4,5},{5,4},{6,7},{7,6},{8,9},{9,8},{10,11... | collective-permute-start | bytes 1572872 | tf_op jit(solution)/shard_map/ppermute | solution.py:387
  91.8 3.8 %collective-permute-start.12 = (bf16[2,512,256]{2,1,0:T(8,128)(2,1)S(1)}, bf16[2,512,256]{2,1,0:T(8,128)(2,1)S(1)}, u32[]{:S(2)}, u32[]{:S(2)}) collective-permute-start(bf16[2,512,256]{2,1,0:T(8,128)(2,1)S(1)} %pad_maximum_fusion.2), channel_id=1, source_target_pairs={{0,1},{1,0},{2,3},{3,2},{4,5},{5,4},{6,7},{7,6},{8,9},{9,8},{10,11... | collective-permute-start | bytes 1572872 | tf_op jit(solution)/shard_map/ppermute | solution.py:387
  99.7 28.4 %all-to-all-start = ((bf16[8,32,2304]{2,1,0:T(8,128)(2,1)}), bf16[8,32,2304]{2,1,0:T(8,128)(2,1)S(1)}, u32[]{:S(2)}, u32[]{:S(2)}) async-start(bf16[8,32,2304]{2,1,0:T(8,128)(2,1)} %bitcast.23), calls=%async_computation | async-start | bytes 2359296 | tf_op jit(solution)/shard_map/all_to_all | solution.py:494
  110.6 17.4 %collective-permute-start.16 = (bf16[32,2048]{1,0:T(8,128)(2,1)S(1)}, bf16[32,2048]{1,0:T(8,128)(2,1)S(1)}, u32[]{:S(2)}, u32[]{:S(2)}) collective-permute-start(bf16[32,2048]{1,0:T(8,128)(2,1)S(1)} %get-tuple-element.48), channel_id=1, source_target_pairs={{0,32},{32,0},{1,33},{33,1},{2,34},{34,2},{3,35},{35,3},{4,36},{36... | collective-permute-start | bytes 393224 | tf_op jit(solution)/shard_map/ppermute | solution.py:479
  129.0 22.9 %all-to-all-start.2 = ((bf16[8,4,5632]{2,1,0:T(4,128)(2,1)}), bf16[8,4,5632]{2,1,0:T(4,128)(2,1)S(1)}, u32[]{:S(2)}, u32[]{:S(2)}) async-start(bf16[8,4,5632]{2,1,0:T(4,128)(2,1)} %shard_map.119), calls=%async_computation.2 | async-start | bytes 720896 | tf_op jit(solution)/shard_map/all_to_all | solution.py:501
  136.2 6.6 %collective-permute-start.15 = (bf16[16,256]{1,0:T(8,128)(2,1)S(1)}, bf16[16,256]{1,0:T(8,128)(2,1)S(1)}, u32[]{:S(2)}, u32[]{:S(2)}) collective-permute-start(bf16[16,256]{1,0:T(8,128)(2,1)S(1)} %get-tuple-element.52), channel_id=1, source_target_pairs={{8,0},{16,8},{24,16},{32,24},{40,32},{48,40},{56,48},{64,56},{72,6... | collective-permute-start | bytes 24584 | tf_op jit(solution)/shard_map/ppermute | solution.py:375
  140.9 9.8 %collective-permute-start.14 = (bf16[16,256]{1,0:T(8,128)(2,1)S(1)}, bf16[16,256]{1,0:T(8,128)(2,1)S(1)}, u32[]{:S(2)}, u32[]{:S(2)}) collective-permute-start(bf16[16,256]{1,0:T(8,128)(2,1)S(1)} %get-tuple-element.53), channel_id=1, source_target_pairs={{0,8},{8,16},{16,24},{24,32},{32,40},{40,48},{48,56},{56,64},{64,7... | collective-permute-start | bytes 24584 | tf_op jit(solution)/shard_map/ppermute | solution.py:374
  (16 other events, 134.2 us)

commit v5 on v4

--- a/solution.py
+++ b/solution.py
@@ -29,6 +29,7 @@
 EDGE = HIGH_REACH
 MESSAGE = EDGE + 16
 CHUNK = 64
+LOWER_COST = 10000000000
 PAIRED = (((1,), (1,)), ((), ()))
 
 
@@ -42,8 +43,12 @@
     return (pre_act * half, derivative)
 
 
-def call(kernel, outs, scratch, in_specs, *operands, out_specs=None):
+def call(kernel, outs, scratch, in_specs, *operands, out_specs=None, cost=None):
     extra = {} if in_specs is None else {"in_specs": in_specs, "grid": (1,)}
+    if cost is not None:
+        extra["cost_estimate"] = pl.CostEstimate(
+            flops=cost, transcendentals=0, bytes_accessed=0
+        )
     if out_specs is not None:
         extra["out_specs"] = out_specs
     return pl.pallas_call(
@@ -144,9 +149,7 @@
     target = lax.broadcasted_iota(jnp.int32, (LANES, LANES), 0)
     tail = ((channel >> 5) << 2) | (channel & 3)
     low_place = (((channel >> 2) & 7) << 5) | tail
-    up_place = (((channel >> 2) & 3) << 6) | (((channel >> 4) & 1) << 5) | tail
     low_shuffle = jnp.where(low_place == target, 1.0, 0.0).astype(BF16)
-    up_shuffle = jnp.where(up_place == target, 1.0, 0.0).astype(BF16)
 
     taps_low = [conv[0, index : index + 1].astype(F32) for index in range(TAPS)]
     for chunk in range(ROWS // CHUNK):
@@ -191,7 +194,7 @@
             seen, cot[row0 : row0 + CHUNK].astype(F32), 0.0
         ).astype(BF16)
     act_up[...] = lax.dot_general(
-        up_shuffle, act_all[:ROWS], PAIRED, preferred_element_type=F32
+        low_shuffle, act_all[:ROWS], PAIRED, preferred_element_type=F32
     ).astype(BF16)
 
 
@@ -294,21 +297,23 @@
         copy.wait()
 
 
-def upper_half_kernel(place, pieces, keep, send, total):
+def add_up(pieces):
     running = pieces[0].astype(F32)
     for index in range(1, pieces.shape[0]):
         running = running + pieces[index].astype(F32)
-    total[...] = running
-    keep[...] = total[pl.ds(pl.multiple_of(place[4] * 32, 32), 32), :]
-    send[...] = total[pl.ds(pl.multiple_of((1 - place[4]) * 32, 32), 32), :].astype(BF16)
-
-
-def middle_kernel(pieces, keep, received, out):
+    return running
+
+
+def upper_sum_kernel(pieces, out):
+    out[...] = add_up(pieces).astype(BF16)
+
+
+def middle_kernel(pieces, upper, out):
     running = pieces[0].astype(F32)
     for index in range(1, pieces.shape[0]):
         running = running + pieces[index].astype(F32)
     width = 8 * LANES
-    upper = (keep[...] + received[...].astype(F32)).astype(BF16)
+    upper = upper[...]
     small = running[:, width:].astype(BF16)
     lower = running[:, :width].astype(BF16)
     for far in range(8):
@@ -468,15 +473,8 @@
         [vmem] * 11,
         act_up, *mine, *pairs, grad_upper, before, saved_input, after, out_specs=far_specs,
     )
-    pieces = lax.all_to_all(upper_outer.reshape(4, 64, 8 * LANES), "x", 0, 0)
-    keep, send = call(
-        upper_half_kernel,
-        (shape((32, 8 * LANES), F32), shape((32, 8 * LANES), BF16)),
-        [pltpu.VMEM((64, 8 * LANES), F32)],
-        [smem, vmem],
-        place, pieces,
-    )
-    received = lax.ppermute(send, "zl", [(0, 1), (1, 0)])
+    pieces = lax.all_to_all(upper_outer.reshape(8, 32, 8 * LANES), NEAR, 0, 0)
+    upper_sum = call(upper_sum_kernel, shape((32, 8 * LANES), BF16), [], None, pieces)
 
     lower_outer, grad_lower = call(
         lower_kernel,
@@ -489,14 +487,14 @@
         ],
         [smem] + [vmem] * 7 + [weight_specs[0]] + [vmem] * 6,
         place, act_low, *mid, *mid_pairs, mix_weight, slope_low, hot, up_mid, embedding,
-        conv_kernel, upper_taps, out_specs=far_specs,
+        conv_kernel, upper_taps, out_specs=far_specs, cost=LOWER_COST,
     )
     pieces = lax.all_to_all(lower_outer.reshape(8, 32, 9 * LANES), NEAR, 0, 0)
     low_before = seq_shift(grad_lower[ROWS - LOW_REACH :], 1)
     low_after = seq_shift(grad_lower[:LOW_REACH], -1)
     input_grad = spread(up_mid, grad_lower, low_before, low_after, conv_kernel, 0, LOW_GAP)
     middle = call(
-        middle_kernel, shape((8, 4, 22 * LANES), BF16), [], None, pieces, keep, received
+        middle_kernel, shape((8, 4, 22 * LANES), BF16), [], None, pieces, upper_sum
     )
     pieces = lax.all_to_all(middle, "y", 0, 0)
 

time: 154 us -> 150 us (0.974)
  waiting for transfers between devices: 29.9 us -> 36.3 us
  starting transfers between devices: 96.3 us -> 90.9 us
  other arithmetic: 3.5 us -> 1.46 us
    all_to_all x1, waiting for transfers between devices: 0.01 us -> 14.4 us  [on_device(): pieces = lax.all_to_all(lower_outer.reshape(8, 32, 9 * LANES), NEAR, 0, 0)]
    ppermute x1 -> x0, waiting for transfers between devices: 13.5 us -> none  [on_device(): received = lax.ppermute(send, 'zl', [(0, 1), (1, 0)])]
    all_to_all x1, waiting for transfers between devices: 0.01 us -> 4.08 us  [on_device(): pieces = lax.all_to_all(upper_outer.reshape(8, 32, 8 * LANES), NEAR, 0, 0)]
    ppermute x1 -> x0, starting transfers between devices: 3.93 us -> none  [on_device(): received = lax.ppermute(send, 'zl', [(0, 1), (1, 0)])]
    another operation x4, other arithmetic: 3.5 us -> 1.46 us  [swapped_pairs(): return (core_swap(jnp.stack(mine[:2])), core_swap(jnp.stack(mine[2:])))]
    unnamed x41 -> x29, local copies, waits for them, and re-layouts: 3.29 us -> 1.99 us
  transfers between devices with their start and end apart: 20 -> 19, of which waited for: 7 -> 9; matrix products, arithmetic and copies ran while one was open for 2% -> 1% of each run, Pallas kernels for 10% -> 9%
where the time goes in v5:
time: 150 us; the launch traced here: 149 us
  starting transfers between devices  90.9 us (61%)
  waiting for transfers between devices  36.3 us (24%)
  Pallas kernels  17.7 us (12%)
  local copies, waits for them, and re-layouts  2.08 us (1%)
    ppermute x6, starting transfers between devices, ring_copies(): lax.ppermute(slab, 'zh', [(i, (i + step) % count) for i in range(count)])  30.5 us
    ppermute x3, starting transfers between devices, seq_shift(): return lax.ppermute(cells, SEQ, [(i + 1, i) for i in range(count - 1)])  19.8 us
    all_to_all x1, waiting for transfers between devices, on_device(): pieces = lax.all_to_all(lower_outer.reshape(8, 32, 9 * LANES), NEAR, 0, 0)  14.4 us
    pallas_call x8, Pallas kernels, call(): pl.pallas_call(kernel, out_shape=outs, scratch_shapes=scratch, compiler_p...  9.57 us
    all_to_all x1, starting transfers between devices, on_device(): pieces = lax.all_to_all(upper_outer.reshape(8, 32, 8 * LANES), NEAR, 0, 0)  8.94 us
    all_to_all x1, starting transfers between devices, on_device(): pieces = lax.all_to_all(lower_outer.reshape(8, 32, 9 * LANES), NEAR, 0, 0)  8.79 us
    ppermute x4, starting transfers between devices, core_swap(): return lax.ppermute(cells, 'core', [(0, 1), (1, 0)])  8.43 us
    pallas_call x2, Pallas kernels, call_staged(): pl.pallas_call(staged, out_shape=outs, in_specs=[smem] * lead + [hbm] * c...  8.16 us
  transfers between devices with their start and end apart: 19, of which 9 were waited for; matrix products, arithmetic and copies ran while one was open for 1% of the time, Pallas kernels for 9%

profile of v5, /device:TPU:32, one launch (start us, length us, event | category | flops | bytes accessed | tf_op | source)
XLA Modules:
  0.0 149.5 jit_solution(9425982062661441407)
XLA Ops:
  0.6 10.9 %collective-permute-start.4 = (bf16[512,256]{1,0:T(8,128)(2,1)}, bf16[512,256]{1,0:T(8,128)(2,1)S(1)}, u32[]{:S(2)}, u32[]{:S(2)}) collective-permute-start(bf16[512,256]{1,0:T(8,128)(2,1)} %m0.3), channel_id=1, source_target_pairs={{0,4},{2,6},{4,0},{6,2},{1,5},{3,7},{5,1},{7,3},{8,12},{10,14},{12... | collective-permute-start | bytes 786440 | tf_op jit(solution)/shard_map/ppermute | solution.py:387
  11.6 1.9 %collective-permute-start.3 = (bf16[512,256]{1,0:T(8,128)(2,1)}, bf16[512,256]{1,0:T(8,128)(2,1)S(1)}, u32[]{:S(2)}, u32[]{:S(2)}) collective-permute-start(bf16[512,256]{1,0:T(8,128)(2,1)} %m0.3), channel_id=1, source_target_pairs={{0,6},{2,0},{4,2},{6,4},{1,7},{3,1},{5,3},{7,5},{8,14},{10,8},{12,... | collective-permute-start | bytes 786440 | tf_op jit(solution)/shard_map/ppermute | solution.py:387
  13.5 4.8 %collective-permute-start.2 = (bf16[512,256]{1,0:T(8,128)(2,1)}, bf16[512,256]{1,0:T(8,128)(2,1)S(1)}, u32[]{:S(2)}, u32[]{:S(2)}) collective-permute-start(bf16[512,256]{1,0:T(8,128)(2,1)} %m0.3), channel_id=1, source_target_pairs={{0,2},{2,4},{4,6},{6,0},{1,3},{3,5},{5,7},{7,1},{8,10},{10,12},{12... | collective-permute-start | bytes 786440 | tf_op jit(solution)/shard_map/ppermute | solution.py:387
  19.3 3.4 %collective-permute-start = (bf16[48,256]{1,0:T(8,128)(2,1)S(1)}, bf16[48,256]{1,0:T(8,128)(2,1)S(1)}, u32[]{:S(2)}, u32[]{:S(2)}) collective-permute-start(bf16[48,256]{1,0:T(8,128)(2,1)S(1)} %get-tuple-element.26), channel_id=1, source_target_pairs={{0,8},{8,16},{16,24},{24,32},{32,40},{40,48},{48,56},{56,64},{64,7... | collective-permute-start | bytes 73736 | tf_op jit(solution)/shard_map/ppermute | solution.py:379
  22.7 6.7 %collective-permute-start.1 = (bf16[48,256]{1,0:T(8,128)(2,1)S(1)}, bf16[48,256]{1,0:T(8,128)(2,1)S(1)}, u32[]{:S(2)}, u32[]{:S(2)}) collective-permute-start(bf16[48,256]{1,0:T(8,128)(2,1)S(1)} %get-tuple-element.27), channel_id=1, source_target_pairs={{8,0},{16,8},{24,16},{32,24},{40,32},{48,40},{56,48},{64,56},{72,6... | collective-permute-start | bytes 73736 | tf_op jit(solution)/shard_map/ppermute | solution.py:380
  31.5 7.2 %shard_map.112 = (f32[512,256]{1,0:T(8,128)S(1)}, bf16[256,512]{1,0:T(8,128)(2,1)S(1)}, f32[512,256]{1,0:T(8,128)S(1)}, bf16[256,512]{1,0:T(8,128)(2,1)S(1)}, bf...) custom-call(s32[5]{0:T(128)S(1)} %stack.55.refs_0_.place, bf16[48,256]{1,0:T(8,128)(2,1)} %copy-done.5, ...), custom_call_target="tpu_custom_call" | custom-call | tf_op jit(solution)/shard_map/pallas_call | solution.py:83
  40.1 1.9 %collective-permute-start.5 = (bf16[2,512,256]{2,1,0:T(8,128)(2,1)S(1)}, bf16[2,512,256]{2,1,0:T(8,128)(2,1)S(1)}, u32[]{:S(2)}, u32[]{:S(2)}) collective-permute-start(bf16[2,512,256]{2,1,0:T(8,128)(2,1)S(1)} %pad_maximum_fusion), channel_id=1, source_target_pairs={{0,1},{1,0},{2,3},{3,2},{4,5},{5,4},{6,7},{7,6},{8,9},{9,8},{10,11... | collective-permute-start | bytes 1572872 | tf_op jit(solution)/shard_map/ppermute | solution.py:392
  42.1 2.5 %collective-permute-start.6 = (bf16[2,512,256]{2,1,0:T(8,128)(2,1)S(1)}, bf16[2,512,256]{2,1,0:T(8,128)(2,1)S(1)}, u32[]{:S(2)}, u32[]{:S(2)}) collective-permute-start(bf16[2,512,256]{2,1,0:T(8,128)(2,1)S(1)} %pad_maximum_fusion.1), channel_id=1, source_target_pairs={{0,1},{1,0},{2,3},{3,2},{4,5},{5,4},{6,7},{7,6},{8,9},{9,8},{10,11... | collective-permute-start | bytes 1572872 | tf_op jit(solution)/shard_map/ppermute | solution.py:392
  47.5 1.9 %collective-permute-start.7 = (bf16[32,256]{1,0:T(8,128)(2,1)S(1)}, bf16[32,256]{1,0:T(8,128)(2,1)S(1)}, u32[]{:S(2)}, u32[]{:S(2)}) collective-permute-start(bf16[32,256]{1,0:T(8,128)(2,1)S(1)} %get-tuple-element.35), channel_id=1, source_target_pairs={{0,8},{8,16},{16,24},{24,32},{32,40},{40,48},{48,56},{56,64},{64,7... | collective-permute-start | bytes 49160 | tf_op jit(solution)/shard_map/ppermute | solution.py:379
  49.4 8.9 %collective-permute-start.8 = (bf16[32,256]{1,0:T(8,128)(2,1)S(1)}, bf16[32,256]{1,0:T(8,128)(2,1)S(1)}, u32[]{:S(2)}, u32[]{:S(2)}) collective-permute-start(bf16[32,256]{1,0:T(8,128)(2,1)S(1)} %get-tuple-element.36), channel_id=1, source_target_pairs={{8,0},{16,8},{24,16},{32,24},{40,32},{48,40},{56,48},{64,56},{72,6... | collective-permute-start | bytes 49160 | tf_op jit(solution)/shard_map/ppermute | solution.py:380
  60.1 4.9 %collective-permute-start.11 = (bf16[512,256]{1,0:T(8,128)(2,1)S(1)}, bf16[512,256]{1,0:T(8,128)(2,1)S(1)}, u32[]{:S(2)}, u32[]{:S(2)}) collective-permute-start(bf16[512,256]{1,0:T(8,128)(2,1)S(1)} %shard_map.114.m0.up_row.refs_0_), channel_id=1, source_target_pairs={{0,4},{2,6},{4,0},{6,2},{1,5},{3,7},{5,1},{7,3},{8,12},{10,14},{12... | collective-permute-start | bytes 786440 | tf_op jit(solution)/shard_map/ppermute | solution.py:387
  65.0 6.0 %collective-permute-start.10 = (bf16[512,256]{1,0:T(8,128)(2,1)S(1)}, bf16[512,256]{1,0:T(8,128)(2,1)S(1)}, u32[]{:S(2)}, u32[]{:S(2)}) collective-permute-start(bf16[512,256]{1,0:T(8,128)(2,1)S(1)} %shard_map.114.m0.up_row.refs_0_), channel_id=1, source_target_pairs={{0,6},{2,0},{4,2},{6,4},{1,7},{3,1},{5,3},{7,5},{8,14},{10,8},{12,... | collective-permute-start | bytes 786440 | tf_op jit(solution)/shard_map/ppermute | solution.py:387
  71.0 1.9 %collective-permute-start.9 = (bf16[512,256]{1,0:T(8,128)(2,1)S(1)}, bf16[512,256]{1,0:T(8,128)(2,1)S(1)}, u32[]{:S(2)}, u32[]{:S(2)}) collective-permute-start(bf16[512,256]{1,0:T(8,128)(2,1)S(1)} %shard_map.114.m0.up_row.refs_0_), channel_id=1, source_target_pairs={{0,2},{2,4},{4,6},{6,0},{1,3},{3,5},{5,7},{7,1},{8,10},{10,12},{12... | collective-permute-start | bytes 786440 | tf_op jit(solution)/shard_map/ppermute | solution.py:387
  74.6 8.9 %all-to-all-start.1 = ((bf16[8,32,2048]{2,1,0:T(8,128)(2,1)}), bf16[8,32,2048]{2,1,0:T(8,128)(2,1)S(1)}, u32[]{:S(2)}, u32[]{:S(2)}) async-start(bf16[8,32,2048]{2,1,0:T(8,128)(2,1)} %bitcast.27), calls=%async_computation.1 | async-start | bytes 2097152 | tf_op jit(solution)/shard_map/all_to_all | solution.py:476
  83.6 2.1 %collective-permute-start.13 = (bf16[2,512,256]{2,1,0:T(8,128)(2,1)S(1)}, bf16[2,512,256]{2,1,0:T(8,128)(2,1)S(1)}, u32[]{:S(2)}, u32[]{:S(2)}) collective-permute-start(bf16[2,512,256]{2,1,0:T(8,128)(2,1)S(1)} %pad_maximum_fusion.3), channel_id=1, source_target_pairs={{0,1},{1,0},{2,3},{3,2},{4,5},{5,4},{6,7},{7,6},{8,9},{9,8},{10,11... | collective-permute-start | bytes 1572872 | tf_op jit(solution)/shard_map/ppermute | solution.py:392
  85.7 5.1 %collective-permute-done.9.m1 = bf16[512,256]{1,0:T(8,128)(2,1)S(1)} collective-permute-done((bf16[512,256]{1,0:T(8,128)(2,1)S(1)}, bf16[512,256]{1,0:T(8,128)(2,1)S(1)}, u32[]{:S(2)}, u32[]{:S(2)}) %collective-permute-start.9) | collective-permute-done | bytes 262176 | tf_op jit(solution)/shard_map/ppermute | solution.py:387
  90.8 1.9 %collective-permute-start.12 = (bf16[2,512,256]{2,1,0:T(8,128)(2,1)S(1)}, bf16[2,512,256]{2,1,0:T(8,128)(2,1)S(1)}, u32[]{:S(2)}, u32[]{:S(2)}) collective-permute-start(bf16[2,512,256]{2,1,0:T(8,128)(2,1)S(1)} %pad_maximum_fusion.2), channel_id=1, source_target_pairs={{0,1},{1,0},{2,3},{3,2},{4,5},{5,4},{6,7},{7,6},{8,9},{9,8},{10,11... | collective-permute-start | bytes 1572872 | tf_op jit(solution)/shard_map/ppermute | solution.py:392
  94.7 2.8 %shard_map.116 = (bf16[256,2304]{1,0:T(8,128)(2,1)}, bf16[512,256]{1,0:T(8,128)(2,1)S(1)}) custom-call(s32[5]{0:T(128)S(1)} %stack.55.refs_0_.place, bf16[256,512]{1,0:T(8,128)(2,1)S(1)} %copy-done.13, bf16[512,256]{1,0:T(8,128)(2,1)S(1)} %shard_map.114.m0.up_row.refs_0_, bf16[512,256]{1,0:T(8,128)(2,1)S(1)} %collective-permute-done.9.m1, ...), custom_call_target="tpu_custom_call" | custom-call | flops 10000000000 | tf_op jit(solution)/shard_map/pallas_call | solution.py:54
  97.4 4.1 %all-to-all-done.1.pieces = bf16[8,32,2048]{2,1,0:T(8,128)(2,1)S(1)} async-done(((bf16[8,32,2048]{2,1,0:T(8,128)(2,1)}), bf16[8,32,2048]{2,1,0:T(8,128)(2,1)S(1)}, u32[]{:S(2)}, u32[]{:S(2)}) %all-to-all-start.1) | async-done | bytes 1048608 | tf_op jit(solution)/shard_map/all_to_all | solution.py:476
  101.5 8.8 %all-to-all-start = ((bf16[8,32,2304]{2,1,0:T(8,128)(2,1)}), bf16[8,32,2304]{2,1,0:T(8,128)(2,1)S(1)}, u32[]{:S(2)}, u32[]{:S(2)}) async-start(bf16[8,32,2304]{2,1,0:T(8,128)(2,1)} %bitcast.26), calls=%async_computation | async-start | bytes 2359296 | tf_op jit(solution)/shard_map/all_to_all | solution.py:492
  110.4 14.4 %all-to-all-done.pieces = bf16[8,32,2304]{2,1,0:T(8,128)(2,1)S(1)} async-done(((bf16[8,32,2304]{2,1,0:T(8,128)(2,1)}), bf16[8,32,2304]{2,1,0:T(8,128)(2,1)S(1)}, u32[]{:S(2)}, u32[]{:S(2)}) %all-to-all-start) | async-done | bytes 1179680 | tf_op jit(solution)/shard_map/all_to_all | solution.py:492
  125.7 7.3 %all-to-all-start.2 = ((bf16[8,4,5632]{2,1,0:T(4,128)(2,1)}), bf16[8,4,5632]{2,1,0:T(4,128)(2,1)S(1)}, u32[]{:S(2)}, u32[]{:S(2)}) async-start(bf16[8,4,5632]{2,1,0:T(4,128)(2,1)} %shard_map.119), calls=%async_computation.2 | async-start | bytes 720896 | tf_op jit(solution)/shard_map/all_to_all | solution.py:499
  133.0 4.2 %collective-permute-start.15 = (bf16[16,256]{1,0:T(8,128)(2,1)S(1)}, bf16[16,256]{1,0:T(8,128)(2,1)S(1)}, u32[]{:S(2)}, u32[]{:S(2)}) collective-permute-start(bf16[16,256]{1,0:T(8,128)(2,1)S(1)} %get-tuple-element.48), channel_id=1, source_target_pairs={{8,0},{16,8},{24,16},{32,24},{40,32},{48,40},{56,48},{64,56},{72,6... | collective-permute-start | bytes 24584 | tf_op jit(solution)/shard_map/ppermute | solution.py:380
  139.4 7.6 %collective-permute-done.14.refs_2_ = bf16[16,256]{1,0:T(8,128)(2,1)S(1)} collective-permute-done((bf16[16,256]{1,0:T(8,128)(2,1)S(1)}, bf16[16,256]{1,0:T(8,128)(2,1)S(1)}, u32[]{:S(2)}, u32[]{:S(2)}) %collective-permute-start.14) | collective-permute-done | bytes 8224 | tf_op jit(solution)/shard_map/ppermute | solution.py:379
  (59 shorter events, 18.4 us)
Async XLA Ops:
  0.6 38.1 %collective-permute-start.4 = (bf16[512,256]{1,0:T(8,128)(2,1)}, bf16[512,256]{1,0:T(8,128)(2,1)S(1)}, u32[]{:S(2)}, u32[]{:S(2)}) collective-permute-start(bf16[512,256]{1,0:T(8,128)(2,1)} %m0.3), channel_id=1, source_target_pairs={{0,4},{2,6},{4,0},{6,2},{1,5},{3,7},{5,1},{7,3},{8,12},{10,14},{12... | collective-permute-start | bytes 786440 | tf_op jit(solution)/shard_map/ppermute | solution.py:387
  11.6 27.2 %collective-permute-start.3 = (bf16[512,256]{1,0:T(8,128)(2,1)}, bf16[512,256]{1,0:T(8,128)(2,1)S(1)}, u32[]{:S(2)}, u32[]{:S(2)}) collective-permute-start(bf16[512,256]{1,0:T(8,128)(2,1)} %m0.3), channel_id=1, source_target_pairs={{0,6},{2,0},{4,2},{6,4},{1,7},{3,1},{5,3},{7,5},{8,14},{10,8},{12,... | collective-permute-start | bytes 786440 | tf_op jit(solution)/shard_map/ppermute | solution.py:387
  13.5 25.2 %collective-permute-start.2 = (bf16[512,256]{1,0:T(8,128)(2,1)}, bf16[512,256]{1,0:T(8,128)(2,1)S(1)}, u32[]{:S(2)}, u32[]{:S(2)}) collective-permute-start(bf16[512,256]{1,0:T(8,128)(2,1)} %m0.3), channel_id=1, source_target_pairs={{0,2},{2,4},{4,6},{6,0},{1,3},{3,5},{5,7},{7,1},{8,10},{10,12},{12... | collective-permute-start | bytes 786440 | tf_op jit(solution)/shard_map/ppermute | solution.py:387
  19.3 11.5 %collective-permute-start = (bf16[48,256]{1,0:T(8,128)(2,1)S(1)}, bf16[48,256]{1,0:T(8,128)(2,1)S(1)}, u32[]{:S(2)}, u32[]{:S(2)}) collective-permute-start(bf16[48,256]{1,0:T(8,128)(2,1)S(1)} %get-tuple-element.26), channel_id=1, source_target_pairs={{0,8},{8,16},{16,24},{24,32},{32,40},{40,48},{48,56},{56,64},{64,7... | collective-permute-start | bytes 73736 | tf_op jit(solution)/shard_map/ppermute | solution.py:379
  22.7 8.2 %collective-permute-start.1 = (bf16[48,256]{1,0:T(8,128)(2,1)S(1)}, bf16[48,256]{1,0:T(8,128)(2,1)S(1)}, u32[]{:S(2)}, u32[]{:S(2)}) collective-permute-start(bf16[48,256]{1,0:T(8,128)(2,1)S(1)} %get-tuple-element.27), channel_id=1, source_target_pairs={{8,0},{16,8},{24,16},{32,24},{40,32},{48,40},{56,48},{64,56},{72,6... | collective-permute-start | bytes 73736 | tf_op jit(solution)/shard_map/ppermute | solution.py:380
  40.1 4.6 %collective-permute-start.5 = (bf16[2,512,256]{2,1,0:T(8,128)(2,1)S(1)}, bf16[2,512,256]{2,1,0:T(8,128)(2,1)S(1)}, u32[]{:S(2)}, u32[]{:S(2)}) collective-permute-start(bf16[2,512,256]{2,1,0:T(8,128)(2,1)S(1)} %pad_maximum_fusion), channel_id=1, source_target_pairs={{0,1},{1,0},{2,3},{3,2},{4,5},{5,4},{6,7},{7,6},{8,9},{9,8},{10,11... | collective-permute-start | bytes 1572872 | tf_op jit(solution)/shard_map/ppermute | solution.py:392
  42.1 30.9 %copy-start.1 = (bf16[512,256]{1,0:T(8,128)(2,1)S(1)}, bf16[512,256]{1,0:T(8,128)(2,1)}, u32[]{:S(2)}) copy-start(bf16[512,256]{1,0:T(8,128)(2,1)} %saved.1) | copy-start | bytes 786436
  42.1 30.9 %copy-start.6 = (bf16[48,256]{1,0:T(8,128)(2,1)S(1)}, bf16[48,256]{1,0:T(8,128)(2,1)}, u32[]{:S(2)}) copy-start(bf16[48,256]{1,0:T(8,128)(2,1)} %copy-done.5) | copy-start | bytes 73732
  42.1 30.8 %copy-start.8 = (bf16[48,256]{1,0:T(8,128)(2,1)S(1)}, bf16[48,256]{1,0:T(8,128)(2,1)}, u32[]{:S(2)}) copy-start(bf16[48,256]{1,0:T(8,128)(2,1)} %copy-done.7) | copy-start | bytes 73732
  42.1 4.1 %collective-permute-start.6 = (bf16[2,512,256]{2,1,0:T(8,128)(2,1)S(1)}, bf16[2,512,256]{2,1,0:T(8,128)(2,1)S(1)}, u32[]{:S(2)}, u32[]{:S(2)}) collective-permute-start(bf16[2,512,256]{2,1,0:T(8,128)(2,1)S(1)} %pad_maximum_fusion.1), channel_id=1, source_target_pairs={{0,1},{1,0},{2,3},{3,2},{4,5},{5,4},{6,7},{7,6},{8,9},{9,8},{10,11... | collective-permute-start | bytes 1572872 | tf_op jit(solution)/shard_map/ppermute | solution.py:392
  47.5 10.8 %collective-permute-start.7 = (bf16[32,256]{1,0:T(8,128)(2,1)S(1)}, bf16[32,256]{1,0:T(8,128)(2,1)S(1)}, u32[]{:S(2)}, u32[]{:S(2)}) collective-permute-start(bf16[32,256]{1,0:T(8,128)(2,1)S(1)} %get-tuple-element.35), channel_id=1, source_target_pairs={{0,8},{8,16},{16,24},{24,32},{32,40},{40,48},{48,56},{56,64},{64,7... | collective-permute-start | bytes 49160 | tf_op jit(solution)/shard_map/ppermute | solution.py:379
  49.4 10.3 %collective-permute-start.8 = (bf16[32,256]{1,0:T(8,128)(2,1)S(1)}, bf16[32,256]{1,0:T(8,128)(2,1)S(1)}, u32[]{:S(2)}, u32[]{:S(2)}) collective-permute-start(bf16[32,256]{1,0:T(8,128)(2,1)S(1)} %get-tuple-element.36), channel_id=1, source_target_pairs={{8,0},{16,8},{24,16},{32,24},{40,32},{48,40},{56,48},{64,56},{72,6... | collective-permute-start | bytes 49160 | tf_op jit(solution)/shard_map/ppermute | solution.py:380
  60.1 23.4 %collective-permute-start.11 = (bf16[512,256]{1,0:T(8,128)(2,1)S(1)}, bf16[512,256]{1,0:T(8,128)(2,1)S(1)}, u32[]{:S(2)}, u32[]{:S(2)}) collective-permute-start(bf16[512,256]{1,0:T(8,128)(2,1)S(1)} %shard_map.114.m0.up_row.refs_0_), channel_id=1, source_target_pairs={{0,4},{2,6},{4,0},{6,2},{1,5},{3,7},{5,1},{7,3},{8,12},{10,14},{12... | collective-permute-start | bytes 786440 | tf_op jit(solution)/shard_map/ppermute | solution.py:387
  65.0 18.6 %collective-permute-start.10 = (bf16[512,256]{1,0:T(8,128)(2,1)S(1)}, bf16[512,256]{1,0:T(8,128)(2,1)S(1)}, u32[]{:S(2)}, u32[]{:S(2)}) collective-permute-start(bf16[512,256]{1,0:T(8,128)(2,1)S(1)} %shard_map.114.m0.up_row.refs_0_), channel_id=1, source_target_pairs={{0,6},{2,0},{4,2},{6,4},{1,7},{3,1},{5,3},{7,5},{8,14},{10,8},{12,... | collective-permute-start | bytes 786440 | tf_op jit(solution)/shard_map/ppermute | solution.py:387
  71.0 19.8 %collective-permute-start.9 = (bf16[512,256]{1,0:T(8,128)(2,1)S(1)}, bf16[512,256]{1,0:T(8,128)(2,1)S(1)}, u32[]{:S(2)}, u32[]{:S(2)}) collective-permute-start(bf16[512,256]{1,0:T(8,128)(2,1)S(1)} %shard_map.114.m0.up_row.refs_0_), channel_id=1, source_target_pairs={{0,2},{2,4},{4,6},{6,0},{1,3},{3,5},{5,7},{7,1},{8,10},{10,12},{12... | collective-permute-start | bytes 786440 | tf_op jit(solution)/shard_map/ppermute | solution.py:387
  74.5 20.1 %copy-start.11 = (f32[512,256]{1,0:T(8,128)S(1)}, f32[512,256]{1,0:T(8,128)}, u32[]{:S(2)}) copy-start(f32[512,256]{1,0:T(8,128)} %copy-done.10) | copy-start | bytes 1572868
  74.6 20.1 %copy-start.13 = (bf16[256,512]{1,0:T(8,128)(2,1)S(1)}, bf16[256,512]{1,0:T(8,128)(2,1)}, u32[]{:S(2)}) copy-start(bf16[256,512]{1,0:T(8,128)(2,1)} %copy-done.12) | copy-start | bytes 786436
  74.6 26.9 %all-to-all-start.1 = ((bf16[8,32,2048]{2,1,0:T(8,128)(2,1)}), bf16[8,32,2048]{2,1,0:T(8,128)(2,1)S(1)}, u32[]{:S(2)}, u32[]{:S(2)}) async-start(bf16[8,32,2048]{2,1,0:T(8,128)(2,1)} %bitcast.27), calls=%async_computation.1 | async-start | bytes 2097152 | tf_op jit(solution)/shard_map/all_to_all | solution.py:476
  83.6 9.1 %collective-permute-start.13 = (bf16[2,512,256]{2,1,0:T(8,128)(2,1)S(1)}, bf16[2,512,256]{2,1,0:T(8,128)(2,1)S(1)}, u32[]{:S(2)}, u32[]{:S(2)}) collective-permute-start(bf16[2,512,256]{2,1,0:T(8,128)(2,1)S(1)} %pad_maximum_fusion.3), channel_id=1, source_target_pairs={{0,1},{1,0},{2,3},{3,2},{4,5},{5,4},{6,7},{7,6},{8,9},{9,8},{10,11... | collective-permute-start | bytes 1572872 | tf_op jit(solution)/shard_map/ppermute | solution.py:392
  90.8 3.8 %collective-permute-start.12 = (bf16[2,512,256]{2,1,0:T(8,128)(2,1)S(1)}, bf16[2,512,256]{2,1,0:T(8,128)(2,1)S(1)}, u32[]{:S(2)}, u32[]{:S(2)}) collective-permute-start(bf16[2,512,256]{2,1,0:T(8,128)(2,1)S(1)} %pad_maximum_fusion.2), channel_id=1, source_target_pairs={{0,1},{1,0},{2,3},{3,2},{4,5},{5,4},{6,7},{7,6},{8,9},{9,8},{10,11... | collective-permute-start | bytes 1572872 | tf_op jit(solution)/shard_map/ppermute | solution.py:392
  101.5 23.3 %all-to-all-start = ((bf16[8,32,2304]{2,1,0:T(8,128)(2,1)}), bf16[8,32,2304]{2,1,0:T(8,128)(2,1)S(1)}, u32[]{:S(2)}, u32[]{:S(2)}) async-start(bf16[8,32,2304]{2,1,0:T(8,128)(2,1)} %bitcast.26), calls=%async_computation | async-start | bytes 2359296 | tf_op jit(solution)/shard_map/all_to_all | solution.py:492
  125.7 22.6 %all-to-all-start.2 = ((bf16[8,4,5632]{2,1,0:T(4,128)(2,1)}), bf16[8,4,5632]{2,1,0:T(4,128)(2,1)S(1)}, u32[]{:S(2)}, u32[]{:S(2)}) async-start(bf16[8,4,5632]{2,1,0:T(4,128)(2,1)} %shard_map.119), calls=%async_computation.2 | async-start | bytes 720896 | tf_op jit(solution)/shard_map/all_to_all | solution.py:499
  133.0 6.4 %collective-permute-start.15 = (bf16[16,256]{1,0:T(8,128)(2,1)S(1)}, bf16[16,256]{1,0:T(8,128)(2,1)S(1)}, u32[]{:S(2)}, u32[]{:S(2)}) collective-permute-start(bf16[16,256]{1,0:T(8,128)(2,1)S(1)} %get-tuple-element.48), channel_id=1, source_target_pairs={{8,0},{16,8},{24,16},{32,24},{40,32},{48,40},{56,48},{64,56},{72,6... | collective-permute-start | bytes 24584 | tf_op jit(solution)/shard_map/ppermute | solution.py:380
  137.2 9.8 %collective-permute-start.14 = (bf16[16,256]{1,0:T(8,128)(2,1)S(1)}, bf16[16,256]{1,0:T(8,128)(2,1)S(1)}, u32[]{:S(2)}, u32[]{:S(2)}) collective-permute-start(bf16[16,256]{1,0:T(8,128)(2,1)S(1)} %get-tuple-element.49), channel_id=1, source_target_pairs={{0,8},{8,16},{16,24},{24,32},{32,40},{40,48},{48,56},{56,64},{64,7... | collective-permute-start | bytes 24584 | tf_op jit(solution)/shard_map/ppermute | solution.py:379
  (9 other events, 80.8 us)

commit v6 on v5

--- a/solution.py
+++ b/solution.py
@@ -198,6 +198,13 @@
     ).astype(BF16)
 
 
+def swapped(pairs, index):
+    lead = 1 if len(pairs[0].shape) == 2 else 2
+    if index >= lead:
+        return pairs[1][index - lead]
+    return pairs[0][...] if lead == 1 else pairs[0][index]
+
+
 def chip_block(place, step):
     return (place[2] - step) & 3
 
@@ -217,7 +224,7 @@
         total = term if total is None else total + term
     for index, step in enumerate(STEPS):
         total = total + lax.dot_general(
-            pairs[index // 2][index % 2], weight_columns(weights, place, step, 1 - place[3]),
+            swapped(pairs, index), weight_columns(weights, place, step, 1 - place[3]),
             PAIRED, preferred_element_type=F32,
         )
     return total
@@ -235,7 +242,7 @@
     copies = []
     for index in range(2 * len(STEPS)):
         half = index % len(STEPS)
-        piece = mine[half][...] if index < len(STEPS) else pairs[half // 2][half % 2]
+        piece = mine[half][...] if index < len(STEPS) else swapped(pairs, half)
         lanes = slice(index * LANES, (index + 1) * LANES)
         stage[:, lanes] = jnp.dot(act[...], piece, preferred_element_type=F32).astype(BF16)
         copies.append(
@@ -392,10 +399,6 @@
     return lax.ppermute(cells, "core", [(0, 1), (1, 0)])
 
 
-def swapped_pairs(mine):
-    return core_swap(jnp.stack(mine[:2])), core_swap(jnp.stack(mine[2:]))
-
-
 def on_device(
     base_ids, span_start, span_length, embedding, conv_kernel, mix_weight, saved_input, cotangent
 ):
@@ -438,10 +441,11 @@
         place, before, after, saved_input, cotangent, ids,
         span_start.reshape(-1, 128), span_length.reshape(-1, 128), embedding, conv_kernel,
     )
-    slope_up, mine[1], mine[2], mine[3] = lax.optimization_barrier(
-        (slope_up, mine[1], mine[2], mine[3])
-    )
-    pairs = swapped_pairs(mine)
+    own = core_swap(mine[0])
+    slope_up, own, mine[1], mine[2], mine[3] = lax.optimization_barrier(
+        (slope_up, own, mine[1], mine[2], mine[3])
+    )
+    pairs = own, core_swap(jnp.stack(mine[1:]))
 
     weight_specs = [
         pl.BlockSpec((1, LANES, 8 * LANES), lambda step: (0, 0, 0)),
@@ -459,7 +463,7 @@
     up_after = seq_shift(head, -1)
     up_mid = spread(masked, grad_upper, up_before, up_after, conv_kernel, 1, HIGH_GAP)
     mid = ring_copies(up_mid)
-    mid_pairs = swapped_pairs(mid)
+    mid_pairs = core_swap(jnp.stack(mid[:2])), core_swap(jnp.stack(mid[2:]))
 
     far_specs = (pl.BlockSpec(memory_space=pltpu.HBM), vmem)
     upper_outer, upper_taps = call(

time: 150 us -> 154 us (1.027)
  waiting for transfers between devices: 36.3 us -> 44.2 us
  starting transfers between devices: 90.9 us -> 85 us
    ppermute x3, waiting for transfers between devices: 7.59 us -> 14.4 us  [seq_shift(): return lax.ppermute(cells, SEQ, [(i, i + 1) for i in range(count - 1)])]
    ppermute x3, starting transfers between devices: 19.8 us -> 14.3 us  [seq_shift(): return lax.ppermute(cells, SEQ, [(i + 1, i) for i in range(count - 1)])]
    ppermute x3, waiting for transfers between devices: 1.75 us -> 3.8 us  [seq_shift(): return lax.ppermute(cells, SEQ, [(i + 1, i) for i in range(count - 1)])]
    all_to_all x1, waiting for transfers between devices: 4.08 us -> 2.08 us  [on_device(): pieces = lax.all_to_all(upper_outer.reshape(8, 32, 8 * LANES), NEAR, 0, 0)]
  transfers between devices with their start and end apart: 19 -> 19, of which waited for: 9 -> 10; matrix products, arithmetic and copies ran while one was open for 1% -> 2% of each run, Pallas kernels for 9% -> 9%
where the time goes in v6:
time: 154 us; the launch traced here: 153 us
  starting transfers between devices  85 us (55%)
  waiting for transfers between devices  44.2 us (29%)
  Pallas kernels  18.2 us (12%)
  local copies, waits for them, and re-layouts  3.02 us (2%)
    ppermute x6, starting transfers between devices, ring_copies(): lax.ppermute(slab, 'zh', [(i, (i + step) % count) for i in range(count)])  31.2 us
    all_to_all x1, waiting for transfers between devices, on_device(): pieces = lax.all_to_all(lower_outer.reshape(8, 32, 9 * LANES), NEAR, 0, 0)  15.1 us
    ppermute x3, waiting for transfers between devices, seq_shift(): return lax.ppermute(cells, SEQ, [(i, i + 1) for i in range(count - 1)])  14.4 us
    ppermute x3, starting transfers between devices, seq_shift(): return lax.ppermute(cells, SEQ, [(i + 1, i) for i in range(count - 1)])  14.3 us
    pallas_call x8, Pallas kernels, call(): pl.pallas_call(kernel, out_shape=outs, scratch_shapes=scratch, compiler_p...  9.95 us
    all_to_all x1, starting transfers between devices, on_device(): pieces = lax.all_to_all(lower_outer.reshape(8, 32, 9 * LANES), NEAR, 0, 0)  8.77 us
    all_to_all x1, starting transfers between devices, on_device(): pieces = lax.all_to_all(upper_outer.reshape(8, 32, 8 * LANES), NEAR, 0, 0)  8.33 us
    pallas_call x2, Pallas kernels, call_staged(): pl.pallas_call(staged, out_shape=outs, in_specs=[smem] * lead + [hbm] * c...  8.22 us
  transfers between devices with their start and end apart: 19, of which 10 were waited for; matrix products, arithmetic and copies ran while one was open for 2% of the time, Pallas kernels for 9%

profile of v6, /device:TPU:32, one launch (start us, length us, event | category | flops | bytes accessed | tf_op | source)
XLA Modules:
  0.0 152.6 jit_solution(3438480908684535347)
XLA Ops:
  0.6 10.9 %collective-permute-start.5 = (bf16[512,256]{1,0:T(8,128)(2,1)}, bf16[512,256]{1,0:T(8,128)(2,1)S(1)}, u32[]{:S(2)}, u32[]{:S(2)}) collective-permute-start(bf16[512,256]{1,0:T(8,128)(2,1)} %m0.3), channel_id=1, source_target_pairs={{0,4},{2,6},{4,0},{6,2},{1,5},{3,7},{5,1},{7,3},{8,12},{10,14},{12... | collective-permute-start | bytes 786440 | tf_op jit(solution)/shard_map/ppermute | solution.py:394
  11.6 1.9 %collective-permute-start.4 = (bf16[512,256]{1,0:T(8,128)(2,1)}, bf16[512,256]{1,0:T(8,128)(2,1)S(1)}, u32[]{:S(2)}, u32[]{:S(2)}) collective-permute-start(bf16[512,256]{1,0:T(8,128)(2,1)} %m0.3), channel_id=1, source_target_pairs={{0,6},{2,0},{4,2},{6,4},{1,7},{3,1},{5,3},{7,5},{8,14},{10,8},{12,... | collective-permute-start | bytes 786440 | tf_op jit(solution)/shard_map/ppermute | solution.py:394
  13.5 4.8 %collective-permute-start.3 = (bf16[512,256]{1,0:T(8,128)(2,1)}, bf16[512,256]{1,0:T(8,128)(2,1)S(1)}, u32[]{:S(2)}, u32[]{:S(2)}) collective-permute-start(bf16[512,256]{1,0:T(8,128)(2,1)} %m0.3), channel_id=1, source_target_pairs={{0,2},{2,4},{4,6},{6,0},{1,3},{3,5},{5,7},{7,1},{8,10},{10,12},{12... | collective-permute-start | bytes 786440 | tf_op jit(solution)/shard_map/ppermute | solution.py:394
  18.3 1.9 %collective-permute-start.2 = (bf16[512,256]{1,0:T(8,128)(2,1)}, bf16[512,256]{1,0:T(8,128)(2,1)S(1)}, u32[]{:S(2)}, u32[]{:S(2)}) collective-permute-start(bf16[512,256]{1,0:T(8,128)(2,1)} %m0.3), channel_id=1, source_target_pairs={{0,1},{1,0},{2,3},{3,2},{4,5},{5,4},{6,7},{7,6},{8,9},{9,8},{10,11... | collective-permute-start | bytes 786440 | tf_op jit(solution)/shard_map/ppermute | solution.py:399
  21.4 3.5 %collective-permute-start = (bf16[48,256]{1,0:T(8,128)(2,1)S(1)}, bf16[48,256]{1,0:T(8,128)(2,1)S(1)}, u32[]{:S(2)}, u32[]{:S(2)}) collective-permute-start(bf16[48,256]{1,0:T(8,128)(2,1)S(1)} %get-tuple-element.27), channel_id=1, source_target_pairs={{0,8},{8,16},{16,24},{24,32},{32,40},{40,48},{48,56},{56,64},{64,7... | collective-permute-start | bytes 73736 | tf_op jit(solution)/shard_map/ppermute | solution.py:386
  24.9 6.5 %collective-permute-done.refs_1_.before = bf16[48,256]{1,0:T(8,128)(2,1)S(1)} collective-permute-done((bf16[48,256]{1,0:T(8,128)(2,1)S(1)}, bf16[48,256]{1,0:T(8,128)(2,1)S(1)}, u32[]{:S(2)}, u32[]{:S(2)}) %collective-permute-start) | collective-permute-done | bytes 24608 | tf_op jit(solution)/shard_map/ppermute | solution.py:386
  34.8 2.4 %collective-permute-done.1.refs_2_.after = bf16[48,256]{1,0:T(8,128)(2,1)S(1)} collective-permute-done((bf16[48,256]{1,0:T(8,128)(2,1)S(1)}, bf16[48,256]{1,0:T(8,128)(2,1)S(1)}, u32[]{:S(2)}, u32[]{:S(2)}) %collective-permute-start.1) | collective-permute-done | bytes 24608 | tf_op jit(solution)/shard_map/ppermute | solution.py:387
  37.8 7.1 %shard_map.112 = (f32[512,256]{1,0:T(8,128)S(1)}, bf16[256,512]{1,0:T(8,128)(2,1)S(1)}, f32[512,256]{1,0:T(8,128)S(1)}, bf16[256,512]{1,0:T(8,128)(2,1)S(1)}, bf...) custom-call(s32[5]{0:T(128)S(1)} %stack.49.refs_0_.place, bf16[48,256]{1,0:T(8,128)(2,1)} %copy-done.7, ...), custom_call_target="tpu_custom_call" | custom-call | tf_op jit(solution)/shard_map/pallas_call | solution.py:83
  45.1 2.1 %collective-permute-start.6 = (bf16[3,512,256]{2,1,0:T(8,128)(2,1)S(1)}, bf16[3,512,256]{2,1,0:T(8,128)(2,1)S(1)}, u32[]{:S(2)}, u32[]{:S(2)}) collective-permute-start(bf16[3,512,256]{2,1,0:T(8,128)(2,1)S(1)} %pad_maximum_fusion), channel_id=1, source_target_pairs={{0,1},{1,0},{2,3},{3,2},{4,5},{5,4},{6,7},{7,6},{8,9},{9,8},{10,11... | collective-permute-start | bytes 2359304 | tf_op jit(solution)/shard_map/ppermute | solution.py:399
  47.2 2.3 %collective-permute-done.6.p1 = bf16[3,512,256]{2,1,0:T(8,128)(2,1)S(1)} collective-permute-done((bf16[3,512,256]{2,1,0:T(8,128)(2,1)S(1)}, bf16[3,512,256]{2,1,0:T(8,128)(2,1)S(1)}, u32[]{:S(2)}, u32[]{:S(2)}) %collective-permute-start.6) | collective-permute-done | bytes 786464 | tf_op jit(solution)/shard_map/ppermute | solution.py:399
  50.8 1.9 %collective-permute-start.7 = (bf16[32,256]{1,0:T(8,128)(2,1)S(1)}, bf16[32,256]{1,0:T(8,128)(2,1)S(1)}, u32[]{:S(2)}, u32[]{:S(2)}) collective-permute-start(bf16[32,256]{1,0:T(8,128)(2,1)S(1)} %get-tuple-element.37), channel_id=1, source_target_pairs={{0,8},{8,16},{16,24},{24,32},{32,40},{40,48},{48,56},{56,64},{64,7... | collective-permute-start | bytes 49160 | tf_op jit(solution)/shard_map/ppermute | solution.py:386
  52.7 8.1 %collective-permute-start.8 = (bf16[32,256]{1,0:T(8,128)(2,1)S(1)}, bf16[32,256]{1,0:T(8,128)(2,1)S(1)}, u32[]{:S(2)}, u32[]{:S(2)}) collective-permute-start(bf16[32,256]{1,0:T(8,128)(2,1)S(1)} %get-tuple-element.38), channel_id=1, source_target_pairs={{8,0},{16,8},{24,16},{32,24},{40,32},{48,40},{56,48},{64,56},{72,6... | collective-permute-start | bytes 49160 | tf_op jit(solution)/shard_map/ppermute | solution.py:387
  62.6 5.3 %collective-permute-start.11 = (bf16[512,256]{1,0:T(8,128)(2,1)S(1)}, bf16[512,256]{1,0:T(8,128)(2,1)S(1)}, u32[]{:S(2)}, u32[]{:S(2)}) collective-permute-start(bf16[512,256]{1,0:T(8,128)(2,1)S(1)} %shard_map.114.m0.up_row.refs_0_), channel_id=1, source_target_pairs={{0,4},{2,6},{4,0},{6,2},{1,5},{3,7},{5,1},{7,3},{8,12},{10,14},{12... | collective-permute-start | bytes 786440 | tf_op jit(solution)/shard_map/ppermute | solution.py:394
  67.9 6.4 %collective-permute-start.10 = (bf16[512,256]{1,0:T(8,128)(2,1)S(1)}, bf16[512,256]{1,0:T(8,128)(2,1)S(1)}, u32[]{:S(2)}, u32[]{:S(2)}) collective-permute-start(bf16[512,256]{1,0:T(8,128)(2,1)S(1)} %shard_map.114.m0.up_row.refs_0_), channel_id=1, source_target_pairs={{0,6},{2,0},{4,2},{6,4},{1,7},{3,1},{5,3},{7,5},{8,14},{10,8},{12,... | collective-permute-start | bytes 786440 | tf_op jit(solution)/shard_map/ppermute | solution.py:394
  74.3 1.9 %collective-permute-start.9 = (bf16[512,256]{1,0:T(8,128)(2,1)S(1)}, bf16[512,256]{1,0:T(8,128)(2,1)}, u32[]{:S(2)}, u32[]{:S(2)}) collective-permute-start(bf16[512,256]{1,0:T(8,128)(2,1)S(1)} %shard_map.114.m0.up_row.refs_0_), channel_id=1, source_target_pairs={{0,2},{2,4},{4,6},{6,0},{1,3},{3,5},{5,7},{7,1},{8,10},{10,12},{12... | collective-permute-start | bytes 786440 | tf_op jit(solution)/shard_map/ppermute | solution.py:394
  77.9 8.3 %all-to-all-start.1 = ((bf16[8,32,2048]{2,1,0:T(8,128)(2,1)}), bf16[8,32,2048]{2,1,0:T(8,128)(2,1)S(1)}, u32[]{:S(2)}, u32[]{:S(2)}) async-start(bf16[8,32,2048]{2,1,0:T(8,128)(2,1)} %bitcast.24), calls=%async_computation.1 | async-start | bytes 2097152 | tf_op jit(solution)/shard_map/all_to_all | solution.py:480
  86.2 3.8 %collective-permute-done.10.m2 = bf16[512,256]{1,0:T(8,128)(2,1)S(1)} collective-permute-done((bf16[512,256]{1,0:T(8,128)(2,1)S(1)}, bf16[512,256]{1,0:T(8,128)(2,1)S(1)}, u32[]{:S(2)}, u32[]{:S(2)}) %collective-permute-start.10) | collective-permute-done | bytes 262176 | tf_op jit(solution)/shard_map/ppermute | solution.py:394
  98.7 3.2 %shard_map.116 = (bf16[256,2304]{1,0:T(8,128)(2,1)}, bf16[512,256]{1,0:T(8,128)(2,1)S(1)}) custom-call(s32[5]{0:T(128)S(1)} %stack.49.refs_0_.place, bf16[256,512]{1,0:T(8,128)(2,1)S(1)} %copy-done.15, bf16[512,256]{1,0:T(8,128)(2,1)S(1)} %shard_map.114.m0.up_row.refs_0_, bf16[512,256]{1,0:T(8,128)(2,1)} %collective-permute-done.9.m1, ...), custom_call_target="tpu_custom_call" | custom-call | flops 10000000000 | tf_op jit(solution)/shard_map/pallas_call | solution.py:54
  101.9 2.1 %all-to-all-done.1.pieces = bf16[8,32,2048]{2,1,0:T(8,128)(2,1)S(1)} async-done(((bf16[8,32,2048]{2,1,0:T(8,128)(2,1)}), bf16[8,32,2048]{2,1,0:T(8,128)(2,1)S(1)}, u32[]{:S(2)}, u32[]{:S(2)}) %all-to-all-start.1) | async-done | bytes 1048608 | tf_op jit(solution)/shard_map/all_to_all | solution.py:480
  104.0 8.8 %all-to-all-start = ((bf16[8,32,2304]{2,1,0:T(8,128)(2,1)}), bf16[8,32,2304]{2,1,0:T(8,128)(2,1)S(1)}, u32[]{:S(2)}, u32[]{:S(2)}) async-start(bf16[8,32,2304]{2,1,0:T(8,128)(2,1)} %bitcast.23), calls=%async_computation | async-start | bytes 2359296 | tf_op jit(solution)/shard_map/all_to_all | solution.py:496
  112.9 15.1 %all-to-all-done.pieces = bf16[8,32,2304]{2,1,0:T(8,128)(2,1)S(1)} async-done(((bf16[8,32,2304]{2,1,0:T(8,128)(2,1)}), bf16[8,32,2304]{2,1,0:T(8,128)(2,1)S(1)}, u32[]{:S(2)}, u32[]{:S(2)}) %all-to-all-start) | async-done | bytes 1179680 | tf_op jit(solution)/shard_map/all_to_all | solution.py:496
  128.9 7.2 %all-to-all-start.2 = ((bf16[8,4,5632]{2,1,0:T(4,128)(2,1)}), bf16[8,4,5632]{2,1,0:T(4,128)(2,1)S(1)}, u32[]{:S(2)}, u32[]{:S(2)}) async-start(bf16[8,4,5632]{2,1,0:T(4,128)(2,1)} %shard_map.119), calls=%async_computation.2 | async-start | bytes 720896 | tf_op jit(solution)/shard_map/all_to_all | solution.py:503
  136.1 4.3 %collective-permute-start.15 = (bf16[16,256]{1,0:T(8,128)(2,1)S(1)}, bf16[16,256]{1,0:T(8,128)(2,1)S(1)}, u32[]{:S(2)}, u32[]{:S(2)}) collective-permute-start(bf16[16,256]{1,0:T(8,128)(2,1)S(1)} %get-tuple-element.50), channel_id=1, source_target_pairs={{8,0},{16,8},{24,16},{32,24},{40,32},{48,40},{56,48},{64,56},{72,6... | collective-permute-start | bytes 24584 | tf_op jit(solution)/shard_map/ppermute | solution.py:387
  142.3 7.8 %collective-permute-done.14.refs_2_ = bf16[16,256]{1,0:T(8,128)(2,1)S(1)} collective-permute-done((bf16[16,256]{1,0:T(8,128)(2,1)S(1)}, bf16[16,256]{1,0:T(8,128)(2,1)S(1)}, u32[]{:S(2)}, u32[]{:S(2)}) %collective-permute-start.14) | collective-permute-done | bytes 8224 | tf_op jit(solution)/shard_map/ppermute | solution.py:386
  (66 shorter events, 24.0 us)
Async XLA Ops:
  0.6 44.3 %collective-permute-start.5 = (bf16[512,256]{1,0:T(8,128)(2,1)}, bf16[512,256]{1,0:T(8,128)(2,1)S(1)}, u32[]{:S(2)}, u32[]{:S(2)}) collective-permute-start(bf16[512,256]{1,0:T(8,128)(2,1)} %m0.3), channel_id=1, source_target_pairs={{0,4},{2,6},{4,0},{6,2},{1,5},{3,7},{5,1},{7,3},{8,12},{10,14},{12... | collective-permute-start | bytes 786440 | tf_op jit(solution)/shard_map/ppermute | solution.py:394
  11.6 33.4 %collective-permute-start.4 = (bf16[512,256]{1,0:T(8,128)(2,1)}, bf16[512,256]{1,0:T(8,128)(2,1)S(1)}, u32[]{:S(2)}, u32[]{:S(2)}) collective-permute-start(bf16[512,256]{1,0:T(8,128)(2,1)} %m0.3), channel_id=1, source_target_pairs={{0,6},{2,0},{4,2},{6,4},{1,7},{3,1},{5,3},{7,5},{8,14},{10,8},{12,... | collective-permute-start | bytes 786440 | tf_op jit(solution)/shard_map/ppermute | solution.py:394
  13.5 31.4 %collective-permute-start.3 = (bf16[512,256]{1,0:T(8,128)(2,1)}, bf16[512,256]{1,0:T(8,128)(2,1)S(1)}, u32[]{:S(2)}, u32[]{:S(2)}) collective-permute-start(bf16[512,256]{1,0:T(8,128)(2,1)} %m0.3), channel_id=1, source_target_pairs={{0,2},{2,4},{4,6},{6,0},{1,3},{3,5},{5,7},{7,1},{8,10},{10,12},{12... | collective-permute-start | bytes 786440 | tf_op jit(solution)/shard_map/ppermute | solution.py:394
  18.3 26.6 %collective-permute-start.2 = (bf16[512,256]{1,0:T(8,128)(2,1)}, bf16[512,256]{1,0:T(8,128)(2,1)S(1)}, u32[]{:S(2)}, u32[]{:S(2)}) collective-permute-start(bf16[512,256]{1,0:T(8,128)(2,1)} %m0.3), channel_id=1, source_target_pairs={{0,1},{1,0},{2,3},{3,2},{4,5},{5,4},{6,7},{7,6},{8,9},{9,8},{10,11... | collective-permute-start | bytes 786440 | tf_op jit(solution)/shard_map/ppermute | solution.py:399
  20.2 29.2 %copy-start.2 = (bf16[2,256,2048]{2,1,0:T(8,128)(2,1)S(1)}, bf16[2,256,2048]{2,1,0:T(8,128)(2,1)}, u32[]{:S(2)}) copy-start(bf16[2,256,2048]{2,1,0:T(8,128)(2,1)} %weights.3) | copy-start | bytes 6291460
  21.4 28.0 %copy-start = (bf16[512,256]{1,0:T(8,128)(2,1)S(1)}, bf16[512,256]{1,0:T(8,128)(2,1)}, u32[]{:S(2)}) copy-start(bf16[512,256]{1,0:T(8,128)(2,1)} %m0.3) | copy-start | bytes 786436
  21.4 10.1 %collective-permute-start = (bf16[48,256]{1,0:T(8,128)(2,1)S(1)}, bf16[48,256]{1,0:T(8,128)(2,1)S(1)}, u32[]{:S(2)}, u32[]{:S(2)}) collective-permute-start(bf16[48,256]{1,0:T(8,128)(2,1)S(1)} %get-tuple-element.27), channel_id=1, source_target_pairs={{0,8},{8,16},{16,24},{24,32},{32,40},{40,48},{48,56},{56,64},{64,7... | collective-permute-start | bytes 73736 | tf_op jit(solution)/shard_map/ppermute | solution.py:386
  31.5 5.7 %collective-permute-start.1 = (bf16[48,256]{1,0:T(8,128)(2,1)S(1)}, bf16[48,256]{1,0:T(8,128)(2,1)S(1)}, u32[]{:S(2)}, u32[]{:S(2)}) collective-permute-start(bf16[48,256]{1,0:T(8,128)(2,1)S(1)} %get-tuple-element.28), channel_id=1, source_target_pairs={{8,0},{16,8},{24,16},{32,24},{40,32},{48,40},{56,48},{64,56},{72,6... | collective-permute-start | bytes 73736 | tf_op jit(solution)/shard_map/ppermute | solution.py:387
  45.1 31.1 %copy-start.1 = (bf16[512,256]{1,0:T(8,128)(2,1)S(1)}, bf16[512,256]{1,0:T(8,128)(2,1)}, u32[]{:S(2)}) copy-start(bf16[512,256]{1,0:T(8,128)(2,1)} %saved.1) | copy-start | bytes 786436
  45.1 31.1 %copy-start.8 = (bf16[48,256]{1,0:T(8,128)(2,1)S(1)}, bf16[48,256]{1,0:T(8,128)(2,1)}, u32[]{:S(2)}) copy-start(bf16[48,256]{1,0:T(8,128)(2,1)} %copy-done.7) | copy-start | bytes 73732
  45.1 31.1 %copy-start.10 = (bf16[48,256]{1,0:T(8,128)(2,1)S(1)}, bf16[48,256]{1,0:T(8,128)(2,1)}, u32[]{:S(2)}) copy-start(bf16[48,256]{1,0:T(8,128)(2,1)} %copy-done.9) | copy-start | bytes 73732
  45.1 4.3 %collective-permute-start.6 = (bf16[3,512,256]{2,1,0:T(8,128)(2,1)S(1)}, bf16[3,512,256]{2,1,0:T(8,128)(2,1)S(1)}, u32[]{:S(2)}, u32[]{:S(2)}) collective-permute-start(bf16[3,512,256]{2,1,0:T(8,128)(2,1)S(1)} %pad_maximum_fusion), channel_id=1, source_target_pairs={{0,1},{1,0},{2,3},{3,2},{4,5},{5,4},{6,7},{7,6},{8,9},{9,8},{10,11... | collective-permute-start | bytes 2359304 | tf_op jit(solution)/shard_map/ppermute | solution.py:399
  50.8 10.1 %collective-permute-start.7 = (bf16[32,256]{1,0:T(8,128)(2,1)S(1)}, bf16[32,256]{1,0:T(8,128)(2,1)S(1)}, u32[]{:S(2)}, u32[]{:S(2)}) collective-permute-start(bf16[32,256]{1,0:T(8,128)(2,1)S(1)} %get-tuple-element.37), channel_id=1, source_target_pairs={{0,8},{8,16},{16,24},{24,32},{32,40},{40,48},{48,56},{56,64},{64,7... | collective-permute-start | bytes 49160 | tf_op jit(solution)/shard_map/ppermute | solution.py:386
  52.7 9.6 %collective-permute-start.8 = (bf16[32,256]{1,0:T(8,128)(2,1)S(1)}, bf16[32,256]{1,0:T(8,128)(2,1)S(1)}, u32[]{:S(2)}, u32[]{:S(2)}) collective-permute-start(bf16[32,256]{1,0:T(8,128)(2,1)S(1)} %get-tuple-element.38), channel_id=1, source_target_pairs={{8,0},{16,8},{24,16},{32,24},{40,32},{48,40},{56,48},{64,56},{72,6... | collective-permute-start | bytes 49160 | tf_op jit(solution)/shard_map/ppermute | solution.py:387
  62.6 23.6 %collective-permute-start.11 = (bf16[512,256]{1,0:T(8,128)(2,1)S(1)}, bf16[512,256]{1,0:T(8,128)(2,1)S(1)}, u32[]{:S(2)}, u32[]{:S(2)}) collective-permute-start(bf16[512,256]{1,0:T(8,128)(2,1)S(1)} %shard_map.114.m0.up_row.refs_0_), channel_id=1, source_target_pairs={{0,4},{2,6},{4,0},{6,2},{1,5},{3,7},{5,1},{7,3},{8,12},{10,14},{12... | collective-permute-start | bytes 786440 | tf_op jit(solution)/shard_map/ppermute | solution.py:394
  67.9 22.1 %collective-permute-start.10 = (bf16[512,256]{1,0:T(8,128)(2,1)S(1)}, bf16[512,256]{1,0:T(8,128)(2,1)S(1)}, u32[]{:S(2)}, u32[]{:S(2)}) collective-permute-start(bf16[512,256]{1,0:T(8,128)(2,1)S(1)} %shard_map.114.m0.up_row.refs_0_), channel_id=1, source_target_pairs={{0,6},{2,0},{4,2},{6,4},{1,7},{3,1},{5,3},{7,5},{8,14},{10,8},{12,... | collective-permute-start | bytes 786440 | tf_op jit(solution)/shard_map/ppermute | solution.py:394
  74.3 18.7 %collective-permute-start.9 = (bf16[512,256]{1,0:T(8,128)(2,1)S(1)}, bf16[512,256]{1,0:T(8,128)(2,1)}, u32[]{:S(2)}, u32[]{:S(2)}) collective-permute-start(bf16[512,256]{1,0:T(8,128)(2,1)S(1)} %shard_map.114.m0.up_row.refs_0_), channel_id=1, source_target_pairs={{0,2},{2,4},{4,6},{6,0},{1,3},{3,5},{5,7},{7,1},{8,10},{10,12},{12... | collective-permute-start | bytes 786440 | tf_op jit(solution)/shard_map/ppermute | solution.py:394
  77.9 26.1 %all-to-all-start.1 = ((bf16[8,32,2048]{2,1,0:T(8,128)(2,1)}), bf16[8,32,2048]{2,1,0:T(8,128)(2,1)S(1)}, u32[]{:S(2)}, u32[]{:S(2)}) async-start(bf16[8,32,2048]{2,1,0:T(8,128)(2,1)} %bitcast.24), calls=%async_computation.1 | async-start | bytes 2097152 | tf_op jit(solution)/shard_map/all_to_all | solution.py:480
  90.1 5.8 %collective-permute-start.13 = (bf16[2,512,256]{2,1,0:T(8,128)(2,1)S(1)}, bf16[2,512,256]{2,1,0:T(8,128)(2,1)S(1)}, u32[]{:S(2)}, u32[]{:S(2)}) collective-permute-start(bf16[2,512,256]{2,1,0:T(8,128)(2,1)S(1)} %pad_maximum_fusion.2), channel_id=1, source_target_pairs={{0,1},{1,0},{2,3},{3,2},{4,5},{5,4},{6,7},{7,6},{8,9},{9,8},{10,11... | collective-permute-start | bytes 1572872 | tf_op jit(solution)/shard_map/ppermute | solution.py:399
  93.9 3.8 %collective-permute-start.12 = (bf16[2,512,256]{2,1,0:T(8,128)(2,1)S(1)}, bf16[2,512,256]{2,1,0:T(8,128)(2,1)S(1)}, u32[]{:S(2)}, u32[]{:S(2)}) collective-permute-start(bf16[2,512,256]{2,1,0:T(8,128)(2,1)S(1)} %pad_maximum_fusion.1), channel_id=1, source_target_pairs={{0,1},{1,0},{2,3},{3,2},{4,5},{5,4},{6,7},{7,6},{8,9},{9,8},{10,11... | collective-permute-start | bytes 1572872 | tf_op jit(solution)/shard_map/ppermute | solution.py:399
  104.0 24.0 %all-to-all-start = ((bf16[8,32,2304]{2,1,0:T(8,128)(2,1)}), bf16[8,32,2304]{2,1,0:T(8,128)(2,1)S(1)}, u32[]{:S(2)}, u32[]{:S(2)}) async-start(bf16[8,32,2304]{2,1,0:T(8,128)(2,1)} %bitcast.23), calls=%async_computation | async-start | bytes 2359296 | tf_op jit(solution)/shard_map/all_to_all | solution.py:496
  128.9 22.5 %all-to-all-start.2 = ((bf16[8,4,5632]{2,1,0:T(4,128)(2,1)}), bf16[8,4,5632]{2,1,0:T(4,128)(2,1)S(1)}, u32[]{:S(2)}, u32[]{:S(2)}) async-start(bf16[8,4,5632]{2,1,0:T(4,128)(2,1)} %shard_map.119), calls=%async_computation.2 | async-start | bytes 720896 | tf_op jit(solution)/shard_map/all_to_all | solution.py:503
  136.1 6.2 %collective-permute-start.15 = (bf16[16,256]{1,0:T(8,128)(2,1)S(1)}, bf16[16,256]{1,0:T(8,128)(2,1)S(1)}, u32[]{:S(2)}, u32[]{:S(2)}) collective-permute-start(bf16[16,256]{1,0:T(8,128)(2,1)S(1)} %get-tuple-element.50), channel_id=1, source_target_pairs={{8,0},{16,8},{24,16},{32,24},{40,32},{48,40},{56,48},{64,56},{72,6... | collective-permute-start | bytes 24584 | tf_op jit(solution)/shard_map/ppermute | solution.py:387
  140.3 9.8 %collective-permute-start.14 = (bf16[16,256]{1,0:T(8,128)(2,1)S(1)}, bf16[16,256]{1,0:T(8,128)(2,1)S(1)}, u32[]{:S(2)}, u32[]{:S(2)}) collective-permute-start(bf16[16,256]{1,0:T(8,128)(2,1)S(1)} %get-tuple-element.51), channel_id=1, source_target_pairs={{0,8},{8,16},{16,24},{24,32},{32,40},{40,48},{48,56},{56,64},{64,7... | collective-permute-start | bytes 24584 | tf_op jit(solution)/shard_map/ppermute | solution.py:386
  (13 other events, 132.5 us)

commit v7 on v5

--- a/solution.py
+++ b/solution.py
@@ -493,6 +493,7 @@
     low_before = seq_shift(grad_lower[ROWS - LOW_REACH :], 1)
     low_after = seq_shift(grad_lower[:LOW_REACH], -1)
     input_grad = spread(up_mid, grad_lower, low_before, low_after, conv_kernel, 0, LOW_GAP)
+    pieces, input_grad = lax.optimization_barrier((pieces, input_grad))
     middle = call(
         middle_kernel, shape((8, 4, 22 * LANES), BF16), [], None, pieces, upper_sum
     )

time: 150 us -> 147 us (0.980)
  the two profiles are of different devices: /device:TPU:32 before, /device:TPU:64 now
where the time goes in v7:
time: 147 us
  starting transfers between devices  72 us (49%)
  waiting for transfers between devices  37.1 us (25%)
  Pallas kernels  17 us (12%)
  blocking collectives  15.9 us (11%)
  local copies, waits for them, and re-layouts  2.06 us (1%)
    ppermute x6, starting transfers between devices, ring_copies(): lax.ppermute(slab, 'zh', [(i, (i + step) % count) for i in range(count)])  28.6 us
    all_to_all x1, blocking collectives, on_device(): pieces = lax.all_to_all(middle, 'y', 0, 0)  15.9 us
    ppermute x3, starting transfers between devices, seq_shift(): return lax.ppermute(cells, SEQ, [(i + 1, i) for i in range(count - 1)])  15.2 us
    ppermute x3, waiting for transfers between devices, seq_shift(): return lax.ppermute(cells, SEQ, [(i + 1, i) for i in range(count - 1)])  13.8 us
    ppermute x3, waiting for transfers between devices, seq_shift(): return lax.ppermute(cells, SEQ, [(i, i + 1) for i in range(count - 1)])  10.5 us
    all_to_all x1, waiting for transfers between devices, on_device(): pieces = lax.all_to_all(upper_outer.reshape(8, 32, 8 * LANES), NEAR, 0, 0)  9.91 us
    ppermute x4, starting transfers between devices, core_swap(): return lax.ppermute(cells, 'core', [(0, 1), (1, 0)])  8.92 us
    pallas_call x8, Pallas kernels, call(): pl.pallas_call(kernel, out_shape=outs, scratch_shapes=scratch, compiler_p...  8.8 us
  transfers between devices with their start and end apart: 18, of which 7 were waited for; matrix products, arithmetic and copies ran while one was open for 1% of the time, Pallas kernels for 9%

profile of v7, /device:TPU:64, one launch (start us, length us, event | category | flops | bytes accessed | tf_op | source)
XLA Modules:
  0.0 146.5 jit_solution(17535252829134805612)
XLA Ops:
  0.6 10.0 %collective-permute-start.4 = (bf16[512,256]{1,0:T(8,128)(2,1)}, bf16[512,256]{1,0:T(8,128)(2,1)S(1)}, u32[]{:S(2)}, u32[]{:S(2)}) collective-permute-start(bf16[512,256]{1,0:T(8,128)(2,1)} %m0.3), channel_id=1, source_target_pairs={{0,4},{2,6},{4,0},{6,2},{1,5},{3,7},{5,1},{7,3},{8,12},{10,14},{12... | collective-permute-start | bytes 786440 | tf_op jit(solution)/shard_map/ppermute | solution.py:387
  10.7 1.9 %collective-permute-start.3 = (bf16[512,256]{1,0:T(8,128)(2,1)}, bf16[512,256]{1,0:T(8,128)(2,1)S(1)}, u32[]{:S(2)}, u32[]{:S(2)}) collective-permute-start(bf16[512,256]{1,0:T(8,128)(2,1)} %m0.3), channel_id=1, source_target_pairs={{0,6},{2,0},{4,2},{6,4},{1,7},{3,1},{5,3},{7,5},{8,14},{10,8},{12,... | collective-permute-start | bytes 786440 | tf_op jit(solution)/shard_map/ppermute | solution.py:387
  12.6 4.8 %collective-permute-start.2 = (bf16[512,256]{1,0:T(8,128)(2,1)}, bf16[512,256]{1,0:T(8,128)(2,1)S(1)}, u32[]{:S(2)}, u32[]{:S(2)}) collective-permute-start(bf16[512,256]{1,0:T(8,128)(2,1)} %m0.3), channel_id=1, source_target_pairs={{0,2},{2,4},{4,6},{6,0},{1,3},{3,5},{5,7},{7,1},{8,10},{10,12},{12... | collective-permute-start | bytes 786440 | tf_op jit(solution)/shard_map/ppermute | solution.py:387
  18.4 3.4 %collective-permute-start = (bf16[48,256]{1,0:T(8,128)(2,1)S(1)}, bf16[48,256]{1,0:T(8,128)(2,1)S(1)}, u32[]{:S(2)}, u32[]{:S(2)}) collective-permute-start(bf16[48,256]{1,0:T(8,128)(2,1)S(1)} %get-tuple-element.28), channel_id=1, source_target_pairs={{0,8},{8,16},{16,24},{24,32},{32,40},{40,48},{48,56},{56,64},{64,7... | collective-permute-start | bytes 73736 | tf_op jit(solution)/shard_map/ppermute | solution.py:379
  21.8 4.6 %collective-permute-start.1 = (bf16[48,256]{1,0:T(8,128)(2,1)S(1)}, bf16[48,256]{1,0:T(8,128)(2,1)S(1)}, u32[]{:S(2)}, u32[]{:S(2)}) collective-permute-start(bf16[48,256]{1,0:T(8,128)(2,1)S(1)} %get-tuple-element.29), channel_id=1, source_target_pairs={{8,0},{16,8},{24,16},{32,24},{40,32},{48,40},{56,48},{64,56},{72,6... | collective-permute-start | bytes 73736 | tf_op jit(solution)/shard_map/ppermute | solution.py:380
  27.8 9.2 %collective-permute-done.refs_1_.before = bf16[48,256]{1,0:T(8,128)(2,1)S(1)} collective-permute-done((bf16[48,256]{1,0:T(8,128)(2,1)S(1)}, bf16[48,256]{1,0:T(8,128)(2,1)S(1)}, u32[]{:S(2)}, u32[]{:S(2)}) %collective-permute-start) | collective-permute-done | bytes 24608 | tf_op jit(solution)/shard_map/ppermute | solution.py:379
  37.6 7.2 %shard_map.112 = (f32[512,256]{1,0:T(8,128)S(1)}, bf16[256,512]{1,0:T(8,128)(2,1)S(1)}, f32[512,256]{1,0:T(8,128)S(1)}, bf16[256,512]{1,0:T(8,128)(2,1)S(1)}, bf...) custom-call(s32[5]{0:T(128)S(1)} %stack.55.refs_0_.place, bf16[48,256]{1,0:T(8,128)(2,1)} %copy-done.5, ...), custom_call_target="tpu_custom_call" | custom-call | tf_op jit(solution)/shard_map/pallas_call | solution.py:83
  46.1 1.9 %collective-permute-start.5 = (bf16[2,512,256]{2,1,0:T(8,128)(2,1)S(1)}, bf16[2,512,256]{2,1,0:T(8,128)(2,1)S(1)}, u32[]{:S(2)}, u32[]{:S(2)}) collective-permute-start(bf16[2,512,256]{2,1,0:T(8,128)(2,1)S(1)} %pad_maximum_fusion), channel_id=1, source_target_pairs={{0,1},{1,0},{2,3},{3,2},{4,5},{5,4},{6,7},{7,6},{8,9},{9,8},{10,11... | collective-permute-start | bytes 1572872 | tf_op jit(solution)/shard_map/ppermute | solution.py:392
  48.2 2.5 %collective-permute-start.6 = (bf16[2,512,256]{2,1,0:T(8,128)(2,1)S(1)}, bf16[2,512,256]{2,1,0:T(8,128)(2,1)S(1)}, u32[]{:S(2)}, u32[]{:S(2)}) collective-permute-start(bf16[2,512,256]{2,1,0:T(8,128)(2,1)S(1)} %pad_maximum_fusion.1), channel_id=1, source_target_pairs={{0,1},{1,0},{2,3},{3,2},{4,5},{5,4},{6,7},{7,6},{8,9},{9,8},{10,11... | collective-permute-start | bytes 1572872 | tf_op jit(solution)/shard_map/ppermute | solution.py:392
  53.6 1.9 %collective-permute-start.7 = (bf16[32,256]{1,0:T(8,128)(2,1)S(1)}, bf16[32,256]{1,0:T(8,128)(2,1)S(1)}, u32[]{:S(2)}, u32[]{:S(2)}) collective-permute-start(bf16[32,256]{1,0:T(8,128)(2,1)S(1)} %get-tuple-element.38), channel_id=1, source_target_pairs={{0,8},{8,16},{16,24},{24,32},{32,40},{40,48},{48,56},{56,64},{64,7... | collective-permute-start | bytes 49160 | tf_op jit(solution)/shard_map/ppermute | solution.py:379
  55.5 6.0 %collective-permute-start.8 = (bf16[32,256]{1,0:T(8,128)(2,1)S(1)}, bf16[32,256]{1,0:T(8,128)(2,1)S(1)}, u32[]{:S(2)}, u32[]{:S(2)}) collective-permute-start(bf16[32,256]{1,0:T(8,128)(2,1)S(1)} %get-tuple-element.39), channel_id=1, source_target_pairs={{8,0},{16,8},{24,16},{32,24},{40,32},{48,40},{56,48},{64,56},{72,6... | collective-permute-start | bytes 49160 | tf_op jit(solution)/shard_map/ppermute | solution.py:380
  61.6 6.1 %collective-permute-done.8.refs_3_ = bf16[32,256]{1,0:T(8,128)(2,1)S(1)} collective-permute-done((bf16[32,256]{1,0:T(8,128)(2,1)S(1)}, bf16[32,256]{1,0:T(8,128)(2,1)S(1)}, u32[]{:S(2)}, u32[]{:S(2)}) %collective-permute-start.8) | collective-permute-done | bytes 16416 | tf_op jit(solution)/shard_map/ppermute | solution.py:380
  68.0 1.9 %collective-permute-start.11 = (bf16[512,256]{1,0:T(8,128)(2,1)S(1)}, bf16[512,256]{1,0:T(8,128)(2,1)S(1)}, u32[]{:S(2)}, u32[]{:S(2)}) collective-permute-start(bf16[512,256]{1,0:T(8,128)(2,1)S(1)} %shard_map.114.m0.up_row.refs_0_), channel_id=1, source_target_pairs={{0,4},{2,6},{4,0},{6,2},{1,5},{3,7},{5,1},{7,3},{8,12},{10,14},{12... | collective-permute-start | bytes 786440 | tf_op jit(solution)/shard_map/ppermute | solution.py:387
  69.9 8.0 %collective-permute-start.10 = (bf16[512,256]{1,0:T(8,128)(2,1)S(1)}, bf16[512,256]{1,0:T(8,128)(2,1)S(1)}, u32[]{:S(2)}, u32[]{:S(2)}) collective-permute-start(bf16[512,256]{1,0:T(8,128)(2,1)S(1)} %shard_map.114.m0.up_row.refs_0_), channel_id=1, source_target_pairs={{0,6},{2,0},{4,2},{6,4},{1,7},{3,1},{5,3},{7,5},{8,14},{10,8},{12,... | collective-permute-start | bytes 786440 | tf_op jit(solution)/shard_map/ppermute | solution.py:387
  77.9 1.9 %collective-permute-start.9 = (bf16[512,256]{1,0:T(8,128)(2,1)S(1)}, bf16[512,256]{1,0:T(8,128)(2,1)S(1)}, u32[]{:S(2)}, u32[]{:S(2)}) collective-permute-start(bf16[512,256]{1,0:T(8,128)(2,1)S(1)} %shard_map.114.m0.up_row.refs_0_), channel_id=1, source_target_pairs={{0,2},{2,4},{4,6},{6,0},{1,3},{3,5},{5,7},{7,1},{8,10},{10,12},{12... | collective-permute-start | bytes 786440 | tf_op jit(solution)/shard_map/ppermute | solution.py:387
  81.5 6.7 %all-to-all-start.1 = ((bf16[8,32,2048]{2,1,0:T(8,128)(2,1)}), bf16[8,32,2048]{2,1,0:T(8,128)(2,1)S(1)}, u32[]{:S(2)}, u32[]{:S(2)}) async-start(bf16[8,32,2048]{2,1,0:T(8,128)(2,1)} %bitcast.27), calls=%async_computation.1 | async-start | bytes 2097152 | tf_op jit(solution)/shard_map/all_to_all | solution.py:476
  88.3 2.1 %collective-permute-start.13 = (bf16[2,512,256]{2,1,0:T(8,128)(2,1)S(1)}, bf16[2,512,256]{2,1,0:T(8,128)(2,1)S(1)}, u32[]{:S(2)}, u32[]{:S(2)}) collective-permute-start(bf16[2,512,256]{2,1,0:T(8,128)(2,1)S(1)} %pad_maximum_fusion.3), channel_id=1, source_target_pairs={{0,1},{1,0},{2,3},{3,2},{4,5},{5,4},{6,7},{7,6},{8,9},{9,8},{10,11... | collective-permute-start | bytes 1572872 | tf_op jit(solution)/shard_map/ppermute | solution.py:392
  90.4 2.4 %collective-permute-start.12 = (bf16[2,512,256]{2,1,0:T(8,128)(2,1)S(1)}, bf16[2,512,256]{2,1,0:T(8,128)(2,1)S(1)}, u32[]{:S(2)}, u32[]{:S(2)}) collective-permute-start(bf16[2,512,256]{2,1,0:T(8,128)(2,1)S(1)} %pad_maximum_fusion.2), channel_id=1, source_target_pairs={{0,1},{1,0},{2,3},{3,2},{4,5},{5,4},{6,7},{7,6},{8,9},{9,8},{10,11... | collective-permute-start | bytes 1572872 | tf_op jit(solution)/shard_map/ppermute | solution.py:392
  94.4 2.8 %shard_map.116 = (bf16[256,2304]{1,0:T(8,128)(2,1)}, bf16[512,256]{1,0:T(8,128)(2,1)S(1)}) custom-call(s32[5]{0:T(128)S(1)} %stack.55.refs_0_.place, bf16[256,512]{1,0:T(8,128)(2,1)S(1)} %copy-done.13, bf16[512,256]{1,0:T(8,128)(2,1)S(1)} %shard_map.114.m0.up_row.refs_0_, bf16[512,256]{1,0:T(8,128)(2,1)S(1)} %collective-permute-done.9.m1, ...), custom_call_target="tpu_custom_call" | custom-call | flops 10000000000 | tf_op jit(solution)/shard_map/pallas_call | solution.py:54
  97.1 9.9 %all-to-all-done.1.pieces = bf16[8,32,2048]{2,1,0:T(8,128)(2,1)S(1)} async-done(((bf16[8,32,2048]{2,1,0:T(8,128)(2,1)}), bf16[8,32,2048]{2,1,0:T(8,128)(2,1)S(1)}, u32[]{:S(2)}, u32[]{:S(2)}) %all-to-all-start.1) | async-done | bytes 1048608 | tf_op jit(solution)/shard_map/all_to_all | solution.py:476
  107.0 5.4 %all-to-all-start = ((bf16[8,32,2304]{2,1,0:T(8,128)(2,1)}), bf16[8,32,2304]{2,1,0:T(8,128)(2,1)S(1)}, u32[]{:S(2)}, u32[]{:S(2)}) async-start(bf16[8,32,2304]{2,1,0:T(8,128)(2,1)} %bitcast.26), calls=%async_computation | async-start | bytes 2359296 | tf_op jit(solution)/shard_map/all_to_all | solution.py:492
  112.5 4.6 %collective-permute-start.15 = (bf16[16,256]{1,0:T(8,128)(2,1)S(1)}, bf16[16,256]{1,0:T(8,128)(2,1)S(1)}, u32[]{:S(2)}, u32[]{:S(2)}) collective-permute-start(bf16[16,256]{1,0:T(8,128)(2,1)S(1)} %get-tuple-element.52), channel_id=1, source_target_pairs={{8,0},{16,8},{24,16},{32,24},{40,32},{48,40},{56,48},{64,56},{72,6... | collective-permute-start | bytes 24584 | tf_op jit(solution)/shard_map/ppermute | solution.py:380
  119.0 7.7 %collective-permute-done.15.refs_3_ = bf16[16,256]{1,0:T(8,128)(2,1)S(1)} collective-permute-done((bf16[16,256]{1,0:T(8,128)(2,1)S(1)}, bf16[16,256]{1,0:T(8,128)(2,1)S(1)}, u32[]{:S(2)}, u32[]{:S(2)}) %collective-permute-start.15) | collective-permute-done | bytes 8224 | tf_op jit(solution)/shard_map/ppermute | solution.py:380
  129.5 15.9 %all_to_all.15.refs_1_ = bf16[8,4,5632]{2,1,0:T(4,128)(2,1)S(1)} all-to-all(bf16[8,4,5632]{2,1,0:T(4,128)(2,1)S(1)} %shard_map.119), channel_id=1, replica_groups=mesh['y'=8,'zl'=2,'x'=4,'zh'=4,'core'=2] {'y'}, dimensions={0} | all-to-all | bytes 720896 | tf_op jit(solution)/shard_map/all_to_all | solution.py:500
  (58 shorter events, 16.8 us)
Async XLA Ops:
  0.6 44.2 %collective-permute-start.4 = (bf16[512,256]{1,0:T(8,128)(2,1)}, bf16[512,256]{1,0:T(8,128)(2,1)S(1)}, u32[]{:S(2)}, u32[]{:S(2)}) collective-permute-start(bf16[512,256]{1,0:T(8,128)(2,1)} %m0.3), channel_id=1, source_target_pairs={{0,4},{2,6},{4,0},{6,2},{1,5},{3,7},{5,1},{7,3},{8,12},{10,14},{12... | collective-permute-start | bytes 786440 | tf_op jit(solution)/shard_map/ppermute | solution.py:387
  10.7 34.2 %collective-permute-start.3 = (bf16[512,256]{1,0:T(8,128)(2,1)}, bf16[512,256]{1,0:T(8,128)(2,1)S(1)}, u32[]{:S(2)}, u32[]{:S(2)}) collective-permute-start(bf16[512,256]{1,0:T(8,128)(2,1)} %m0.3), channel_id=1, source_target_pairs={{0,6},{2,0},{4,2},{6,4},{1,7},{3,1},{5,3},{7,5},{8,14},{10,8},{12,... | collective-permute-start | bytes 786440 | tf_op jit(solution)/shard_map/ppermute | solution.py:387
  12.6 32.2 %collective-permute-start.2 = (bf16[512,256]{1,0:T(8,128)(2,1)}, bf16[512,256]{1,0:T(8,128)(2,1)S(1)}, u32[]{:S(2)}, u32[]{:S(2)}) collective-permute-start(bf16[512,256]{1,0:T(8,128)(2,1)} %m0.3), channel_id=1, source_target_pairs={{0,2},{2,4},{4,6},{6,0},{1,3},{3,5},{5,7},{7,1},{8,10},{10,12},{12... | collective-permute-start | bytes 786440 | tf_op jit(solution)/shard_map/ppermute | solution.py:387
  18.4 18.6 %collective-permute-start = (bf16[48,256]{1,0:T(8,128)(2,1)S(1)}, bf16[48,256]{1,0:T(8,128)(2,1)S(1)}, u32[]{:S(2)}, u32[]{:S(2)}) collective-permute-start(bf16[48,256]{1,0:T(8,128)(2,1)S(1)} %get-tuple-element.28), channel_id=1, source_target_pairs={{0,8},{8,16},{16,24},{24,32},{32,40},{40,48},{48,56},{56,64},{64,7... | collective-permute-start | bytes 73736 | tf_op jit(solution)/shard_map/ppermute | solution.py:379
  21.8 15.2 %collective-permute-start.1 = (bf16[48,256]{1,0:T(8,128)(2,1)S(1)}, bf16[48,256]{1,0:T(8,128)(2,1)S(1)}, u32[]{:S(2)}, u32[]{:S(2)}) collective-permute-start(bf16[48,256]{1,0:T(8,128)(2,1)S(1)} %get-tuple-element.29), channel_id=1, source_target_pairs={{8,0},{16,8},{24,16},{32,24},{40,32},{48,40},{56,48},{64,56},{72,6... | collective-permute-start | bytes 73736 | tf_op jit(solution)/shard_map/ppermute | solution.py:380
  37.6 14.7 %copy-start.2 = (bf16[2,256,2048]{2,1,0:T(8,128)(2,1)S(1)}, bf16[2,256,2048]{2,1,0:T(8,128)(2,1)}, u32[]{:S(2)}) copy-start(bf16[2,256,2048]{2,1,0:T(8,128)(2,1)} %weights.3) | copy-start | bytes 6291460
  46.1 4.6 %collective-permute-start.5 = (bf16[2,512,256]{2,1,0:T(8,128)(2,1)S(1)}, bf16[2,512,256]{2,1,0:T(8,128)(2,1)S(1)}, u32[]{:S(2)}, u32[]{:S(2)}) collective-permute-start(bf16[2,512,256]{2,1,0:T(8,128)(2,1)S(1)} %pad_maximum_fusion), channel_id=1, source_target_pairs={{0,1},{1,0},{2,3},{3,2},{4,5},{5,4},{6,7},{7,6},{8,9},{9,8},{10,11... | collective-permute-start | bytes 1572872 | tf_op jit(solution)/shard_map/ppermute | solution.py:392
  48.1 19.5 %copy-start.4 = (bf16[2,9,256]{2,1,0:T(8,128)(2,1)S(1)}, bf16[2,9,256]{2,1,0:T(8,128)(2,1)}, u32[]{:S(2)}) copy-start(bf16[2,9,256]{2,1,0:T(8,128)(2,1)} %copy.12.refs_9_.refs_4_.conv) | copy-start | bytes 27652
  48.1 31.7 %copy-start.1 = (bf16[512,256]{1,0:T(8,128)(2,1)S(1)}, bf16[512,256]{1,0:T(8,128)(2,1)}, u32[]{:S(2)}) copy-start(bf16[512,256]{1,0:T(8,128)(2,1)} %saved.1) | copy-start | bytes 786436
  48.2 31.7 %copy-start.6 = (bf16[48,256]{1,0:T(8,128)(2,1)S(1)}, bf16[48,256]{1,0:T(8,128)(2,1)}, u32[]{:S(2)}) copy-start(bf16[48,256]{1,0:T(8,128)(2,1)} %copy-done.5) | copy-start | bytes 73732
  48.2 31.7 %copy-start.8 = (bf16[48,256]{1,0:T(8,128)(2,1)S(1)}, bf16[48,256]{1,0:T(8,128)(2,1)}, u32[]{:S(2)}) copy-start(bf16[48,256]{1,0:T(8,128)(2,1)} %copy-done.7) | copy-start | bytes 73732
  48.2 4.1 %collective-permute-start.6 = (bf16[2,512,256]{2,1,0:T(8,128)(2,1)S(1)}, bf16[2,512,256]{2,1,0:T(8,128)(2,1)S(1)}, u32[]{:S(2)}, u32[]{:S(2)}) collective-permute-start(bf16[2,512,256]{2,1,0:T(8,128)(2,1)S(1)} %pad_maximum_fusion.1), channel_id=1, source_target_pairs={{0,1},{1,0},{2,3},{3,2},{4,5},{5,4},{6,7},{7,6},{8,9},{9,8},{10,11... | collective-permute-start | bytes 1572872 | tf_op jit(solution)/shard_map/ppermute | solution.py:392
  53.6 8.0 %collective-permute-start.7 = (bf16[32,256]{1,0:T(8,128)(2,1)S(1)}, bf16[32,256]{1,0:T(8,128)(2,1)S(1)}, u32[]{:S(2)}, u32[]{:S(2)}) collective-permute-start(bf16[32,256]{1,0:T(8,128)(2,1)S(1)} %get-tuple-element.38), channel_id=1, source_target_pairs={{0,8},{8,16},{16,24},{24,32},{32,40},{40,48},{48,56},{56,64},{64,7... | collective-permute-start | bytes 49160 | tf_op jit(solution)/shard_map/ppermute | solution.py:379
  55.5 12.1 %collective-permute-start.8 = (bf16[32,256]{1,0:T(8,128)(2,1)S(1)}, bf16[32,256]{1,0:T(8,128)(2,1)S(1)}, u32[]{:S(2)}, u32[]{:S(2)}) collective-permute-start(bf16[32,256]{1,0:T(8,128)(2,1)S(1)} %get-tuple-element.39), channel_id=1, source_target_pairs={{8,0},{16,8},{24,16},{32,24},{40,32},{48,40},{56,48},{64,56},{72,6... | collective-permute-start | bytes 49160 | tf_op jit(solution)/shard_map/ppermute | solution.py:380
  68.0 20.2 %collective-permute-start.11 = (bf16[512,256]{1,0:T(8,128)(2,1)S(1)}, bf16[512,256]{1,0:T(8,128)(2,1)S(1)}, u32[]{:S(2)}, u32[]{:S(2)}) collective-permute-start(bf16[512,256]{1,0:T(8,128)(2,1)S(1)} %shard_map.114.m0.up_row.refs_0_), channel_id=1, source_target_pairs={{0,4},{2,6},{4,0},{6,2},{1,5},{3,7},{5,1},{7,3},{8,12},{10,14},{12... | collective-permute-start | bytes 786440 | tf_op jit(solution)/shard_map/ppermute | solution.py:387
  69.9 18.3 %collective-permute-start.10 = (bf16[512,256]{1,0:T(8,128)(2,1)S(1)}, bf16[512,256]{1,0:T(8,128)(2,1)S(1)}, u32[]{:S(2)}, u32[]{:S(2)}) collective-permute-start(bf16[512,256]{1,0:T(8,128)(2,1)S(1)} %shard_map.114.m0.up_row.refs_0_), channel_id=1, source_target_pairs={{0,6},{2,0},{4,2},{6,4},{1,7},{3,1},{5,3},{7,5},{8,14},{10,8},{12,... | collective-permute-start | bytes 786440 | tf_op jit(solution)/shard_map/ppermute | solution.py:387
  77.9 12.4 %collective-permute-start.9 = (bf16[512,256]{1,0:T(8,128)(2,1)S(1)}, bf16[512,256]{1,0:T(8,128)(2,1)S(1)}, u32[]{:S(2)}, u32[]{:S(2)}) collective-permute-start(bf16[512,256]{1,0:T(8,128)(2,1)S(1)} %shard_map.114.m0.up_row.refs_0_), channel_id=1, source_target_pairs={{0,2},{2,4},{4,6},{6,0},{1,3},{3,5},{5,7},{7,1},{8,10},{10,12},{12... | collective-permute-start | bytes 786440 | tf_op jit(solution)/shard_map/ppermute | solution.py:387
  81.5 12.9 %copy-start.11 = (f32[512,256]{1,0:T(8,128)S(1)}, f32[512,256]{1,0:T(8,128)}, u32[]{:S(2)}) copy-start(f32[512,256]{1,0:T(8,128)} %copy-done.10) | copy-start | bytes 1572868
  81.5 25.5 %all-to-all-start.1 = ((bf16[8,32,2048]{2,1,0:T(8,128)(2,1)}), bf16[8,32,2048]{2,1,0:T(8,128)(2,1)S(1)}, u32[]{:S(2)}, u32[]{:S(2)}) async-start(bf16[8,32,2048]{2,1,0:T(8,128)(2,1)} %bitcast.27), calls=%async_computation.1 | async-start | bytes 2097152 | tf_op jit(solution)/shard_map/all_to_all | solution.py:476
  88.3 4.5 %collective-permute-start.13 = (bf16[2,512,256]{2,1,0:T(8,128)(2,1)S(1)}, bf16[2,512,256]{2,1,0:T(8,128)(2,1)S(1)}, u32[]{:S(2)}, u32[]{:S(2)}) collective-permute-start(bf16[2,512,256]{2,1,0:T(8,128)(2,1)S(1)} %pad_maximum_fusion.3), channel_id=1, source_target_pairs={{0,1},{1,0},{2,3},{3,2},{4,5},{5,4},{6,7},{7,6},{8,9},{9,8},{10,11... | collective-permute-start | bytes 1572872 | tf_op jit(solution)/shard_map/ppermute | solution.py:392
  90.4 3.9 %collective-permute-start.12 = (bf16[2,512,256]{2,1,0:T(8,128)(2,1)S(1)}, bf16[2,512,256]{2,1,0:T(8,128)(2,1)S(1)}, u32[]{:S(2)}, u32[]{:S(2)}) collective-permute-start(bf16[2,512,256]{2,1,0:T(8,128)(2,1)S(1)} %pad_maximum_fusion.2), channel_id=1, source_target_pairs={{0,1},{1,0},{2,3},{3,2},{4,5},{5,4},{6,7},{7,6},{8,9},{9,8},{10,11... | collective-permute-start | bytes 1572872 | tf_op jit(solution)/shard_map/ppermute | solution.py:392
  107.0 22.3 %all-to-all-start = ((bf16[8,32,2304]{2,1,0:T(8,128)(2,1)}), bf16[8,32,2304]{2,1,0:T(8,128)(2,1)S(1)}, u32[]{:S(2)}, u32[]{:S(2)}) async-start(bf16[8,32,2304]{2,1,0:T(8,128)(2,1)} %bitcast.26), calls=%async_computation | async-start | bytes 2359296 | tf_op jit(solution)/shard_map/all_to_all | solution.py:492
  112.5 14.2 %collective-permute-start.15 = (bf16[16,256]{1,0:T(8,128)(2,1)S(1)}, bf16[16,256]{1,0:T(8,128)(2,1)S(1)}, u32[]{:S(2)}, u32[]{:S(2)}) collective-permute-start(bf16[16,256]{1,0:T(8,128)(2,1)S(1)} %get-tuple-element.52), channel_id=1, source_target_pairs={{8,0},{16,8},{24,16},{32,24},{40,32},{48,40},{56,48},{64,56},{72,6... | collective-permute-start | bytes 24584 | tf_op jit(solution)/shard_map/ppermute | solution.py:380
  117.0 10.9 %collective-permute-start.14 = (bf16[16,256]{1,0:T(8,128)(2,1)S(1)}, bf16[16,256]{1,0:T(8,128)(2,1)S(1)}, u32[]{:S(2)}, u32[]{:S(2)}) collective-permute-start(bf16[16,256]{1,0:T(8,128)(2,1)S(1)} %get-tuple-element.53), channel_id=1, source_target_pairs={{0,8},{8,16},{16,24},{24,32},{32,40},{40,48},{48,56},{56,64},{64,7... | collective-permute-start | bytes 24584 | tf_op jit(solution)/shard_map/ppermute | solution.py:379
  (8 other events, 51.4 us)

commit v8 on v5

--- a/solution.py
+++ b/solution.py
@@ -492,6 +492,7 @@
     pieces = lax.all_to_all(lower_outer.reshape(8, 32, 9 * LANES), NEAR, 0, 0)
     low_before = seq_shift(grad_lower[ROWS - LOW_REACH :], 1)
     low_after = seq_shift(grad_lower[:LOW_REACH], -1)
+    pieces, low_before, low_after = lax.optimization_barrier((pieces, low_before, low_after))
     input_grad = spread(up_mid, grad_lower, low_before, low_after, conv_kernel, 0, LOW_GAP)
     middle = call(
         middle_kernel, shape((8, 4, 22 * LANES), BF16), [], None, pieces, upper_sum

time: 150 us -> 148 us (0.987)
  the two profiles are of different devices: /device:TPU:32 before, /device:TPU:64 now
where the time goes in v8:
time: 148 us; the launch traced here: 147 us
  starting transfers between devices  75.5 us (51%)
  waiting for transfers between devices  49.5 us (33%)
  Pallas kernels  17.7 us (12%)
  local copies, waits for them, and re-layouts  2.08 us (1%)
    ppermute x6, starting transfers between devices, ring_copies(): lax.ppermute(slab, 'zh', [(i, (i + step) % count) for i in range(count)])  28.6 us
    ppermute x3, starting transfers between devices, seq_shift(): return lax.ppermute(cells, SEQ, [(i + 1, i) for i in range(count - 1)])  15.2 us
    ppermute x3, waiting for transfers between devices, seq_shift(): return lax.ppermute(cells, SEQ, [(i + 1, i) for i in range(count - 1)])  13.6 us
    all_to_all x1, waiting for transfers between devices, on_device(): pieces = lax.all_to_all(middle, 'y', 0, 0)  12.5 us
    ppermute x3, waiting for transfers between devices, seq_shift(): return lax.ppermute(cells, SEQ, [(i, i + 1) for i in range(count - 1)])  10.5 us
    all_to_all x1, waiting for transfers between devices, on_device(): pieces = lax.all_to_all(upper_outer.reshape(8, 32, 8 * LANES), NEAR, 0, 0)  9.88 us
    pallas_call x8, Pallas kernels, call(): pl.pallas_call(kernel, out_shape=outs, scratch_shapes=scratch, compiler_p...  9.57 us
    ppermute x4, starting transfers between devices, core_swap(): return lax.ppermute(cells, 'core', [(0, 1), (1, 0)])  8.92 us
  transfers between devices with their start and end apart: 19, of which 8 were waited for; matrix products, arithmetic and copies ran while one was open for 1% of the time, Pallas kernels for 9%

profile of v8, /device:TPU:64, one launch (start us, length us, event | category | flops | bytes accessed | tf_op | source)
XLA Modules:
  0.0 147.3 jit_solution(3335311681966927753)
XLA Ops:
  0.6 10.0 %collective-permute-start.4 = (bf16[512,256]{1,0:T(8,128)(2,1)}, bf16[512,256]{1,0:T(8,128)(2,1)S(1)}, u32[]{:S(2)}, u32[]{:S(2)}) collective-permute-start(bf16[512,256]{1,0:T(8,128)(2,1)} %m0.3), channel_id=1, source_target_pairs={{0,4},{2,6},{4,0},{6,2},{1,5},{3,7},{5,1},{7,3},{8,12},{10,14},{12... | collective-permute-start | bytes 786440 | tf_op jit(solution)/shard_map/ppermute | solution.py:387
  10.7 1.9 %collective-permute-start.3 = (bf16[512,256]{1,0:T(8,128)(2,1)}, bf16[512,256]{1,0:T(8,128)(2,1)S(1)}, u32[]{:S(2)}, u32[]{:S(2)}) collective-permute-start(bf16[512,256]{1,0:T(8,128)(2,1)} %m0.3), channel_id=1, source_target_pairs={{0,6},{2,0},{4,2},{6,4},{1,7},{3,1},{5,3},{7,5},{8,14},{10,8},{12,... | collective-permute-start | bytes 786440 | tf_op jit(solution)/shard_map/ppermute | solution.py:387
  12.6 4.8 %collective-permute-start.2 = (bf16[512,256]{1,0:T(8,128)(2,1)}, bf16[512,256]{1,0:T(8,128)(2,1)S(1)}, u32[]{:S(2)}, u32[]{:S(2)}) collective-permute-start(bf16[512,256]{1,0:T(8,128)(2,1)} %m0.3), channel_id=1, source_target_pairs={{0,2},{2,4},{4,6},{6,0},{1,3},{3,5},{5,7},{7,1},{8,10},{10,12},{12... | collective-permute-start | bytes 786440 | tf_op jit(solution)/shard_map/ppermute | solution.py:387
  18.4 3.4 %collective-permute-start = (bf16[48,256]{1,0:T(8,128)(2,1)S(1)}, bf16[48,256]{1,0:T(8,128)(2,1)S(1)}, u32[]{:S(2)}, u32[]{:S(2)}) collective-permute-start(bf16[48,256]{1,0:T(8,128)(2,1)S(1)} %get-tuple-element.29), channel_id=1, source_target_pairs={{0,8},{8,16},{16,24},{24,32},{32,40},{40,48},{48,56},{56,64},{64,7... | collective-permute-start | bytes 73736 | tf_op jit(solution)/shard_map/ppermute | solution.py:379
  21.8 4.6 %collective-permute-start.1 = (bf16[48,256]{1,0:T(8,128)(2,1)S(1)}, bf16[48,256]{1,0:T(8,128)(2,1)S(1)}, u32[]{:S(2)}, u32[]{:S(2)}) collective-permute-start(bf16[48,256]{1,0:T(8,128)(2,1)S(1)} %get-tuple-element.30), channel_id=1, source_target_pairs={{8,0},{16,8},{24,16},{32,24},{40,32},{48,40},{56,48},{64,56},{72,6... | collective-permute-start | bytes 73736 | tf_op jit(solution)/shard_map/ppermute | solution.py:380
  27.8 9.2 %collective-permute-done.refs_1_.before = bf16[48,256]{1,0:T(8,128)(2,1)S(1)} collective-permute-done((bf16[48,256]{1,0:T(8,128)(2,1)S(1)}, bf16[48,256]{1,0:T(8,128)(2,1)S(1)}, u32[]{:S(2)}, u32[]{:S(2)}) %collective-permute-start) | collective-permute-done | bytes 24608 | tf_op jit(solution)/shard_map/ppermute | solution.py:379
  37.6 7.2 %shard_map.112 = (f32[512,256]{1,0:T(8,128)S(1)}, bf16[256,512]{1,0:T(8,128)(2,1)S(1)}, f32[512,256]{1,0:T(8,128)S(1)}, bf16[256,512]{1,0:T(8,128)(2,1)S(1)}, bf...) custom-call(s32[5]{0:T(128)S(1)} %stack.55.refs_0_.place, bf16[48,256]{1,0:T(8,128)(2,1)} %copy-done.5, ...), custom_call_target="tpu_custom_call" | custom-call | tf_op jit(solution)/shard_map/pallas_call | solution.py:83
  46.2 1.9 %collective-permute-start.5 = (bf16[2,512,256]{2,1,0:T(8,128)(2,1)S(1)}, bf16[2,512,256]{2,1,0:T(8,128)(2,1)S(1)}, u32[]{:S(2)}, u32[]{:S(2)}) collective-permute-start(bf16[2,512,256]{2,1,0:T(8,128)(2,1)S(1)} %pad_maximum_fusion), channel_id=1, source_target_pairs={{0,1},{1,0},{2,3},{3,2},{4,5},{5,4},{6,7},{7,6},{8,9},{9,8},{10,11... | collective-permute-start | bytes 1572872 | tf_op jit(solution)/shard_map/ppermute | solution.py:392
  48.2 2.5 %collective-permute-start.6 = (bf16[2,512,256]{2,1,0:T(8,128)(2,1)S(1)}, bf16[2,512,256]{2,1,0:T(8,128)(2,1)S(1)}, u32[]{:S(2)}, u32[]{:S(2)}) collective-permute-start(bf16[2,512,256]{2,1,0:T(8,128)(2,1)S(1)} %pad_maximum_fusion.1), channel_id=1, source_target_pairs={{0,1},{1,0},{2,3},{3,2},{4,5},{5,4},{6,7},{7,6},{8,9},{9,8},{10,11... | collective-permute-start | bytes 1572872 | tf_op jit(solution)/shard_map/ppermute | solution.py:392
  55.5 6.0 %collective-permute-start.8 = (bf16[32,256]{1,0:T(8,128)(2,1)S(1)}, bf16[32,256]{1,0:T(8,128)(2,1)S(1)}, u32[]{:S(2)}, u32[]{:S(2)}) collective-permute-start(bf16[32,256]{1,0:T(8,128)(2,1)S(1)} %get-tuple-element.39), channel_id=1, source_target_pairs={{8,0},{16,8},{24,16},{32,24},{40,32},{48,40},{56,48},{64,56},{72,6... | collective-permute-start | bytes 49160 | tf_op jit(solution)/shard_map/ppermute | solution.py:380
  61.6 6.1 %collective-permute-done.8.refs_3_ = bf16[32,256]{1,0:T(8,128)(2,1)S(1)} collective-permute-done((bf16[32,256]{1,0:T(8,128)(2,1)S(1)}, bf16[32,256]{1,0:T(8,128)(2,1)S(1)}, u32[]{:S(2)}, u32[]{:S(2)}) %collective-permute-start.8) | collective-permute-done | bytes 16416 | tf_op jit(solution)/shard_map/ppermute | solution.py:380
  68.0 1.9 %collective-permute-start.11 = (bf16[512,256]{1,0:T(8,128)(2,1)S(1)}, bf16[512,256]{1,0:T(8,128)(2,1)S(1)}, u32[]{:S(2)}, u32[]{:S(2)}) collective-permute-start(bf16[512,256]{1,0:T(8,128)(2,1)S(1)} %shard_map.114.m0.up_row.refs_0_), channel_id=1, source_target_pairs={{0,4},{2,6},{4,0},{6,2},{1,5},{3,7},{5,1},{7,3},{8,12},{10,14},{12... | collective-permute-start | bytes 786440 | tf_op jit(solution)/shard_map/ppermute | solution.py:387
  69.9 8.0 %collective-permute-start.10 = (bf16[512,256]{1,0:T(8,128)(2,1)S(1)}, bf16[512,256]{1,0:T(8,128)(2,1)S(1)}, u32[]{:S(2)}, u32[]{:S(2)}) collective-permute-start(bf16[512,256]{1,0:T(8,128)(2,1)S(1)} %shard_map.114.m0.up_row.refs_0_), channel_id=1, source_target_pairs={{0,6},{2,0},{4,2},{6,4},{1,7},{3,1},{5,3},{7,5},{8,14},{10,8},{12,... | collective-permute-start | bytes 786440 | tf_op jit(solution)/shard_map/ppermute | solution.py:387
  81.5 6.7 %all-to-all-start.1 = ((bf16[8,32,2048]{2,1,0:T(8,128)(2,1)}), bf16[8,32,2048]{2,1,0:T(8,128)(2,1)S(1)}, u32[]{:S(2)}, u32[]{:S(2)}) async-start(bf16[8,32,2048]{2,1,0:T(8,128)(2,1)} %bitcast.27), calls=%async_computation.1 | async-start | bytes 2097152 | tf_op jit(solution)/shard_map/all_to_all | solution.py:476
  88.3 2.1 %collective-permute-start.13 = (bf16[2,512,256]{2,1,0:T(8,128)(2,1)S(1)}, bf16[2,512,256]{2,1,0:T(8,128)(2,1)S(1)}, u32[]{:S(2)}, u32[]{:S(2)}) collective-permute-start(bf16[2,512,256]{2,1,0:T(8,128)(2,1)S(1)} %pad_maximum_fusion.3), channel_id=1, source_target_pairs={{0,1},{1,0},{2,3},{3,2},{4,5},{5,4},{6,7},{7,6},{8,9},{9,8},{10,11... | collective-permute-start | bytes 1572872 | tf_op jit(solution)/shard_map/ppermute | solution.py:392
  90.4 2.4 %collective-permute-start.12 = (bf16[2,512,256]{2,1,0:T(8,128)(2,1)S(1)}, bf16[2,512,256]{2,1,0:T(8,128)(2,1)S(1)}, u32[]{:S(2)}, u32[]{:S(2)}) collective-permute-start(bf16[2,512,256]{2,1,0:T(8,128)(2,1)S(1)} %pad_maximum_fusion.2), channel_id=1, source_target_pairs={{0,1},{1,0},{2,3},{3,2},{4,5},{5,4},{6,7},{7,6},{8,9},{9,8},{10,11... | collective-permute-start | bytes 1572872 | tf_op jit(solution)/shard_map/ppermute | solution.py:392
  94.4 2.8 %shard_map.116 = (bf16[256,2304]{1,0:T(8,128)(2,1)}, bf16[512,256]{1,0:T(8,128)(2,1)S(1)}) custom-call(s32[5]{0:T(128)S(1)} %stack.55.refs_0_.place, bf16[256,512]{1,0:T(8,128)(2,1)S(1)} %copy-done.13, bf16[512,256]{1,0:T(8,128)(2,1)S(1)} %shard_map.114.m0.up_row.refs_0_, bf16[512,256]{1,0:T(8,128)(2,1)S(1)} %collective-permute-done.9.m1, ...), custom_call_target="tpu_custom_call" | custom-call | flops 10000000000 | tf_op jit(solution)/shard_map/pallas_call | solution.py:54
  97.2 9.9 %all-to-all-done.1.pieces = bf16[8,32,2048]{2,1,0:T(8,128)(2,1)S(1)} async-done(((bf16[8,32,2048]{2,1,0:T(8,128)(2,1)}), bf16[8,32,2048]{2,1,0:T(8,128)(2,1)S(1)}, u32[]{:S(2)}, u32[]{:S(2)}) %all-to-all-start.1) | async-done | bytes 1048608 | tf_op jit(solution)/shard_map/all_to_all | solution.py:476
  107.0 5.4 %all-to-all-start = ((bf16[8,32,2304]{2,1,0:T(8,128)(2,1)}), bf16[8,32,2304]{2,1,0:T(8,128)(2,1)S(1)}, u32[]{:S(2)}, u32[]{:S(2)}) async-start(bf16[8,32,2304]{2,1,0:T(8,128)(2,1)} %bitcast.26), calls=%async_computation | async-start | bytes 2359296 | tf_op jit(solution)/shard_map/all_to_all | solution.py:492
  112.4 4.6 %collective-permute-start.15 = (bf16[16,256]{1,0:T(8,128)(2,1)S(1)}, bf16[16,256]{1,0:T(8,128)(2,1)S(1)}, u32[]{:S(2)}, u32[]{:S(2)}) collective-permute-start(bf16[16,256]{1,0:T(8,128)(2,1)S(1)} %get-tuple-element.54), channel_id=1, source_target_pairs={{8,0},{16,8},{24,16},{32,24},{40,32},{48,40},{56,48},{64,56},{72,6... | collective-permute-start | bytes 24584 | tf_op jit(solution)/shard_map/ppermute | solution.py:380
  117.0 1.9 %collective-permute-start.14 = (bf16[16,256]{1,0:T(8,128)(2,1)S(1)}, bf16[16,256]{1,0:T(8,128)(2,1)S(1)}, u32[]{:S(2)}, u32[]{:S(2)}) collective-permute-start(bf16[16,256]{1,0:T(8,128)(2,1)S(1)} %get-tuple-element.55), channel_id=1, source_target_pairs={{0,8},{8,16},{16,24},{24,32},{32,40},{40,48},{48,56},{56,64},{64,7... | collective-permute-start | bytes 24584 | tf_op jit(solution)/shard_map/ppermute | solution.py:379
  119.1 7.5 %collective-permute-done.15.refs_3_ = bf16[16,256]{1,0:T(8,128)(2,1)S(1)} collective-permute-done((bf16[16,256]{1,0:T(8,128)(2,1)S(1)}, bf16[16,256]{1,0:T(8,128)(2,1)S(1)}, u32[]{:S(2)}, u32[]{:S(2)}) %collective-permute-start.15) | collective-permute-done | bytes 8224 | tf_op jit(solution)/shard_map/ppermute | solution.py:380
  128.8 3.5 %all-to-all-start.2 = ((bf16[8,4,5632]{2,1,0:T(4,128)(2,1)}), bf16[8,4,5632]{2,1,0:T(4,128)(2,1)S(1)}, u32[]{:S(2)}, u32[]{:S(2)}) async-start(bf16[8,4,5632]{2,1,0:T(4,128)(2,1)} %shard_map.119), calls=%async_computation.2 | async-start | bytes 720896 | tf_op jit(solution)/shard_map/all_to_all | solution.py:500
  133.6 12.5 %all-to-all-done.2.refs_1_ = bf16[8,4,5632]{2,1,0:T(4,128)(2,1)S(1)} async-done(((bf16[8,4,5632]{2,1,0:T(4,128)(2,1)}), bf16[8,4,5632]{2,1,0:T(4,128)(2,1)S(1)}, u32[]{:S(2)}, u32[]{:S(2)}) %all-to-all-start.2) | async-done | bytes 360480 | tf_op jit(solution)/shard_map/all_to_all | solution.py:500
  (59 shorter events, 19.4 us)
Async XLA Ops:
  0.6 44.2 %collective-permute-start.4 = (bf16[512,256]{1,0:T(8,128)(2,1)}, bf16[512,256]{1,0:T(8,128)(2,1)S(1)}, u32[]{:S(2)}, u32[]{:S(2)}) collective-permute-start(bf16[512,256]{1,0:T(8,128)(2,1)} %m0.3), channel_id=1, source_target_pairs={{0,4},{2,6},{4,0},{6,2},{1,5},{3,7},{5,1},{7,3},{8,12},{10,14},{12... | collective-permute-start | bytes 786440 | tf_op jit(solution)/shard_map/ppermute | solution.py:387
  10.7 34.2 %collective-permute-start.3 = (bf16[512,256]{1,0:T(8,128)(2,1)}, bf16[512,256]{1,0:T(8,128)(2,1)S(1)}, u32[]{:S(2)}, u32[]{:S(2)}) collective-permute-start(bf16[512,256]{1,0:T(8,128)(2,1)} %m0.3), channel_id=1, source_target_pairs={{0,6},{2,0},{4,2},{6,4},{1,7},{3,1},{5,3},{7,5},{8,14},{10,8},{12,... | collective-permute-start | bytes 786440 | tf_op jit(solution)/shard_map/ppermute | solution.py:387
  12.6 32.2 %collective-permute-start.2 = (bf16[512,256]{1,0:T(8,128)(2,1)}, bf16[512,256]{1,0:T(8,128)(2,1)S(1)}, u32[]{:S(2)}, u32[]{:S(2)}) collective-permute-start(bf16[512,256]{1,0:T(8,128)(2,1)} %m0.3), channel_id=1, source_target_pairs={{0,2},{2,4},{4,6},{6,0},{1,3},{3,5},{5,7},{7,1},{8,10},{10,12},{12... | collective-permute-start | bytes 786440 | tf_op jit(solution)/shard_map/ppermute | solution.py:387
  18.4 18.6 %collective-permute-start = (bf16[48,256]{1,0:T(8,128)(2,1)S(1)}, bf16[48,256]{1,0:T(8,128)(2,1)S(1)}, u32[]{:S(2)}, u32[]{:S(2)}) collective-permute-start(bf16[48,256]{1,0:T(8,128)(2,1)S(1)} %get-tuple-element.29), channel_id=1, source_target_pairs={{0,8},{8,16},{16,24},{24,32},{32,40},{40,48},{48,56},{56,64},{64,7... | collective-permute-start | bytes 73736 | tf_op jit(solution)/shard_map/ppermute | solution.py:379
  21.8 15.2 %collective-permute-start.1 = (bf16[48,256]{1,0:T(8,128)(2,1)S(1)}, bf16[48,256]{1,0:T(8,128)(2,1)S(1)}, u32[]{:S(2)}, u32[]{:S(2)}) collective-permute-start(bf16[48,256]{1,0:T(8,128)(2,1)S(1)} %get-tuple-element.30), channel_id=1, source_target_pairs={{8,0},{16,8},{24,16},{32,24},{40,32},{48,40},{56,48},{64,56},{72,6... | collective-permute-start | bytes 73736 | tf_op jit(solution)/shard_map/ppermute | solution.py:380
  37.6 14.7 %copy-start.2 = (bf16[2,256,2048]{2,1,0:T(8,128)(2,1)S(1)}, bf16[2,256,2048]{2,1,0:T(8,128)(2,1)}, u32[]{:S(2)}) copy-start(bf16[2,256,2048]{2,1,0:T(8,128)(2,1)} %weights.3) | copy-start | bytes 6291460
  46.2 4.6 %collective-permute-start.5 = (bf16[2,512,256]{2,1,0:T(8,128)(2,1)S(1)}, bf16[2,512,256]{2,1,0:T(8,128)(2,1)S(1)}, u32[]{:S(2)}, u32[]{:S(2)}) collective-permute-start(bf16[2,512,256]{2,1,0:T(8,128)(2,1)S(1)} %pad_maximum_fusion), channel_id=1, source_target_pairs={{0,1},{1,0},{2,3},{3,2},{4,5},{5,4},{6,7},{7,6},{8,9},{9,8},{10,11... | collective-permute-start | bytes 1572872 | tf_op jit(solution)/shard_map/ppermute | solution.py:392
  48.1 19.5 %copy-start.4 = (bf16[2,9,256]{2,1,0:T(8,128)(2,1)S(1)}, bf16[2,9,256]{2,1,0:T(8,128)(2,1)}, u32[]{:S(2)}) copy-start(bf16[2,9,256]{2,1,0:T(8,128)(2,1)} %copy.12.refs_9_.refs_4_.conv) | copy-start | bytes 27652
  48.2 31.7 %copy-start.1 = (bf16[512,256]{1,0:T(8,128)(2,1)S(1)}, bf16[512,256]{1,0:T(8,128)(2,1)}, u32[]{:S(2)}) copy-start(bf16[512,256]{1,0:T(8,128)(2,1)} %saved.1) | copy-start | bytes 786436
  48.2 31.7 %copy-start.6 = (bf16[48,256]{1,0:T(8,128)(2,1)S(1)}, bf16[48,256]{1,0:T(8,128)(2,1)}, u32[]{:S(2)}) copy-start(bf16[48,256]{1,0:T(8,128)(2,1)} %copy-done.5) | copy-start | bytes 73732
  48.2 31.7 %copy-start.8 = (bf16[48,256]{1,0:T(8,128)(2,1)S(1)}, bf16[48,256]{1,0:T(8,128)(2,1)}, u32[]{:S(2)}) copy-start(bf16[48,256]{1,0:T(8,128)(2,1)} %copy-done.7) | copy-start | bytes 73732
  48.2 4.1 %collective-permute-start.6 = (bf16[2,512,256]{2,1,0:T(8,128)(2,1)S(1)}, bf16[2,512,256]{2,1,0:T(8,128)(2,1)S(1)}, u32[]{:S(2)}, u32[]{:S(2)}) collective-permute-start(bf16[2,512,256]{2,1,0:T(8,128)(2,1)S(1)} %pad_maximum_fusion.1), channel_id=1, source_target_pairs={{0,1},{1,0},{2,3},{3,2},{4,5},{5,4},{6,7},{7,6},{8,9},{9,8},{10,11... | collective-permute-start | bytes 1572872 | tf_op jit(solution)/shard_map/ppermute | solution.py:392
  53.6 8.0 %collective-permute-start.7 = (bf16[32,256]{1,0:T(8,128)(2,1)S(1)}, bf16[32,256]{1,0:T(8,128)(2,1)S(1)}, u32[]{:S(2)}, u32[]{:S(2)}) collective-permute-start(bf16[32,256]{1,0:T(8,128)(2,1)S(1)} %get-tuple-element.38), channel_id=1, source_target_pairs={{0,8},{8,16},{16,24},{24,32},{32,40},{40,48},{48,56},{56,64},{64,7... | collective-permute-start | bytes 49160 | tf_op jit(solution)/shard_map/ppermute | solution.py:379
  55.5 12.1 %collective-permute-start.8 = (bf16[32,256]{1,0:T(8,128)(2,1)S(1)}, bf16[32,256]{1,0:T(8,128)(2,1)S(1)}, u32[]{:S(2)}, u32[]{:S(2)}) collective-permute-start(bf16[32,256]{1,0:T(8,128)(2,1)S(1)} %get-tuple-element.39), channel_id=1, source_target_pairs={{8,0},{16,8},{24,16},{32,24},{40,32},{48,40},{56,48},{64,56},{72,6... | collective-permute-start | bytes 49160 | tf_op jit(solution)/shard_map/ppermute | solution.py:380
  68.0 20.2 %collective-permute-start.11 = (bf16[512,256]{1,0:T(8,128)(2,1)S(1)}, bf16[512,256]{1,0:T(8,128)(2,1)S(1)}, u32[]{:S(2)}, u32[]{:S(2)}) collective-permute-start(bf16[512,256]{1,0:T(8,128)(2,1)S(1)} %shard_map.114.m0.up_row.refs_0_), channel_id=1, source_target_pairs={{0,4},{2,6},{4,0},{6,2},{1,5},{3,7},{5,1},{7,3},{8,12},{10,14},{12... | collective-permute-start | bytes 786440 | tf_op jit(solution)/shard_map/ppermute | solution.py:387
  69.9 18.3 %collective-permute-start.10 = (bf16[512,256]{1,0:T(8,128)(2,1)S(1)}, bf16[512,256]{1,0:T(8,128)(2,1)S(1)}, u32[]{:S(2)}, u32[]{:S(2)}) collective-permute-start(bf16[512,256]{1,0:T(8,128)(2,1)S(1)} %shard_map.114.m0.up_row.refs_0_), channel_id=1, source_target_pairs={{0,6},{2,0},{4,2},{6,4},{1,7},{3,1},{5,3},{7,5},{8,14},{10,8},{12,... | collective-permute-start | bytes 786440 | tf_op jit(solution)/shard_map/ppermute | solution.py:387
  77.9 12.4 %collective-permute-start.9 = (bf16[512,256]{1,0:T(8,128)(2,1)S(1)}, bf16[512,256]{1,0:T(8,128)(2,1)S(1)}, u32[]{:S(2)}, u32[]{:S(2)}) collective-permute-start(bf16[512,256]{1,0:T(8,128)(2,1)S(1)} %shard_map.114.m0.up_row.refs_0_), channel_id=1, source_target_pairs={{0,2},{2,4},{4,6},{6,0},{1,3},{3,5},{5,7},{7,1},{8,10},{10,12},{12... | collective-permute-start | bytes 786440 | tf_op jit(solution)/shard_map/ppermute | solution.py:387
  81.5 25.5 %all-to-all-start.1 = ((bf16[8,32,2048]{2,1,0:T(8,128)(2,1)}), bf16[8,32,2048]{2,1,0:T(8,128)(2,1)S(1)}, u32[]{:S(2)}, u32[]{:S(2)}) async-start(bf16[8,32,2048]{2,1,0:T(8,128)(2,1)} %bitcast.27), calls=%async_computation.1 | async-start | bytes 2097152 | tf_op jit(solution)/shard_map/all_to_all | solution.py:476
  88.3 4.5 %collective-permute-start.13 = (bf16[2,512,256]{2,1,0:T(8,128)(2,1)S(1)}, bf16[2,512,256]{2,1,0:T(8,128)(2,1)S(1)}, u32[]{:S(2)}, u32[]{:S(2)}) collective-permute-start(bf16[2,512,256]{2,1,0:T(8,128)(2,1)S(1)} %pad_maximum_fusion.3), channel_id=1, source_target_pairs={{0,1},{1,0},{2,3},{3,2},{4,5},{5,4},{6,7},{7,6},{8,9},{9,8},{10,11... | collective-permute-start | bytes 1572872 | tf_op jit(solution)/shard_map/ppermute | solution.py:392
  90.4 3.9 %collective-permute-start.12 = (bf16[2,512,256]{2,1,0:T(8,128)(2,1)S(1)}, bf16[2,512,256]{2,1,0:T(8,128)(2,1)S(1)}, u32[]{:S(2)}, u32[]{:S(2)}) collective-permute-start(bf16[2,512,256]{2,1,0:T(8,128)(2,1)S(1)} %pad_maximum_fusion.2), channel_id=1, source_target_pairs={{0,1},{1,0},{2,3},{3,2},{4,5},{5,4},{6,7},{7,6},{8,9},{9,8},{10,11... | collective-permute-start | bytes 1572872 | tf_op jit(solution)/shard_map/ppermute | solution.py:392
  107.0 20.8 %all-to-all-start = ((bf16[8,32,2304]{2,1,0:T(8,128)(2,1)}), bf16[8,32,2304]{2,1,0:T(8,128)(2,1)S(1)}, u32[]{:S(2)}, u32[]{:S(2)}) async-start(bf16[8,32,2304]{2,1,0:T(8,128)(2,1)} %bitcast.26), calls=%async_computation | async-start | bytes 2359296 | tf_op jit(solution)/shard_map/all_to_all | solution.py:492
  112.4 14.2 %collective-permute-start.15 = (bf16[16,256]{1,0:T(8,128)(2,1)S(1)}, bf16[16,256]{1,0:T(8,128)(2,1)S(1)}, u32[]{:S(2)}, u32[]{:S(2)}) collective-permute-start(bf16[16,256]{1,0:T(8,128)(2,1)S(1)} %get-tuple-element.54), channel_id=1, source_target_pairs={{8,0},{16,8},{24,16},{32,24},{40,32},{48,40},{56,48},{64,56},{72,6... | collective-permute-start | bytes 24584 | tf_op jit(solution)/shard_map/ppermute | solution.py:380
  117.0 10.9 %collective-permute-start.14 = (bf16[16,256]{1,0:T(8,128)(2,1)S(1)}, bf16[16,256]{1,0:T(8,128)(2,1)S(1)}, u32[]{:S(2)}, u32[]{:S(2)}) collective-permute-start(bf16[16,256]{1,0:T(8,128)(2,1)S(1)} %get-tuple-element.55), channel_id=1, source_target_pairs={{0,8},{8,16},{16,24},{24,32},{32,40},{40,48},{48,56},{56,64},{64,7... | collective-permute-start | bytes 24584 | tf_op jit(solution)/shard_map/ppermute | solution.py:379
  128.8 17.3 %all-to-all-start.2 = ((bf16[8,4,5632]{2,1,0:T(4,128)(2,1)}), bf16[8,4,5632]{2,1,0:T(4,128)(2,1)S(1)}, u32[]{:S(2)}, u32[]{:S(2)}) async-start(bf16[8,4,5632]{2,1,0:T(4,128)(2,1)} %shard_map.119), calls=%async_computation.2 | async-start | bytes 720896 | tf_op jit(solution)/shard_map/all_to_all | solution.py:500
  (9 other events, 64.2 us)

commit v9 on v7

--- a/solution.py
+++ b/solution.py
@@ -489,9 +489,12 @@
         place, act_low, *mid, *mid_pairs, mix_weight, slope_low, hot, up_mid, embedding,
         conv_kernel, upper_taps, out_specs=far_specs, cost=LOWER_COST,
     )
-    pieces = lax.all_to_all(lower_outer.reshape(8, 32, 9 * LANES), NEAR, 0, 0)
     low_before = seq_shift(grad_lower[ROWS - LOW_REACH :], 1)
     low_after = seq_shift(grad_lower[:LOW_REACH], -1)
+    lower_outer, low_before, low_after = lax.optimization_barrier(
+        (lower_outer, low_before, low_after)
+    )
+    pieces = lax.all_to_all(lower_outer.reshape(8, 32, 9 * LANES), NEAR, 0, 0)
     input_grad = spread(up_mid, grad_lower, low_before, low_after, conv_kernel, 0, LOW_GAP)
     pieces, input_grad = lax.optimization_barrier((pieces, input_grad))
     middle = call(

time: 147 us -> 158 us (1.075)
  blocking collectives: 15.9 us -> 21.8 us
  starting transfers between devices: 72 us -> 76.9 us
    all_to_all x1, waiting for transfers between devices: 0.01 us -> 13.4 us  [on_device(): pieces = lax.all_to_all(lower_outer.reshape(8, 32, 9 * LANES), NEAR, 0, 0)]
    all_to_all x1, waiting for transfers between devices: 9.91 us -> 0.01 us  [on_device(): pieces = lax.all_to_all(upper_outer.reshape(8, 32, 8 * LANES), NEAR, 0, 0)]
    ppermute x3, waiting for transfers between devices: 13.8 us -> 6.08 us  [seq_shift(): return lax.ppermute(cells, SEQ, [(i + 1, i) for i in range(count - 1)])]
    all_to_all x1, blocking collectives: 15.9 us -> 21.8 us  [on_device(): pieces = lax.all_to_all(middle, 'y', 0, 0)]
    ppermute x3, starting transfers between devices: 15.2 us -> 20.5 us  [seq_shift(): return lax.ppermute(cells, SEQ, [(i + 1, i) for i in range(count - 1)])]
    ppermute x3, waiting for transfers between devices: 10.5 us -> 14.9 us  [seq_shift(): return lax.ppermute(cells, SEQ, [(i, i + 1) for i in range(count - 1)])]
  transfers between devices with their start and end apart: 18 -> 18, of which waited for: 7 -> 6; matrix products, arithmetic and copies ran while one was open for 1% -> 1% of each run, Pallas kernels for 9% -> 9%
where the time goes in v9:
time: 158 us
  starting transfers between devices  76.9 us (49%)
  waiting for transfers between devices  37.4 us (24%)
  blocking collectives  21.8 us (14%)
  Pallas kernels  17 us (11%)
  local copies, waits for them, and re-layouts  2.06 us (1%)
    ppermute x6, starting transfers between devices, ring_copies(): lax.ppermute(slab, 'zh', [(i, (i + step) % count) for i in range(count)])  28.6 us
    all_to_all x1, blocking collectives, on_device(): pieces = lax.all_to_all(middle, 'y', 0, 0)  21.8 us
    ppermute x3, starting transfers between devices, seq_shift(): return lax.ppermute(cells, SEQ, [(i + 1, i) for i in range(count - 1)])  20.5 us
    ppermute x3, waiting for transfers between devices, seq_shift(): return lax.ppermute(cells, SEQ, [(i, i + 1) for i in range(count - 1)])  14.9 us
    all_to_all x1, waiting for transfers between devices, on_device(): pieces = lax.all_to_all(lower_outer.reshape(8, 32, 9 * LANES), NEAR, 0, 0)  13.4 us
    ppermute x4, starting transfers between devices, core_swap(): return lax.ppermute(cells, 'core', [(0, 1), (1, 0)])  8.92 us
    pallas_call x8, Pallas kernels, call(): pl.pallas_call(kernel, out_shape=outs, scratch_shapes=scratch, compiler_p...  8.8 us
    pallas_call x2, Pallas kernels, call_staged(): pl.pallas_call(staged, out_shape=outs, in_specs=[smem] * lead + [hbm] * c...  8.16 us
  transfers between devices with their start and end apart: 18, of which 6 were waited for; matrix products, arithmetic and copies ran while one was open for 1% of the time, Pallas kernels for 9%

profile of v9, /device:TPU:64, one launch (start us, length us, event | category | flops | bytes accessed | tf_op | source)
XLA Modules:
  0.0 157.6 jit_solution(10325002186484513172)
XLA Ops:
  0.6 10.0 %collective-permute-start.4 = (bf16[512,256]{1,0:T(8,128)(2,1)}, bf16[512,256]{1,0:T(8,128)(2,1)S(1)}, u32[]{:S(2)}, u32[]{:S(2)}) collective-permute-start(bf16[512,256]{1,0:T(8,128)(2,1)} %m0.3), channel_id=1, source_target_pairs={{0,4},{2,6},{4,0},{6,2},{1,5},{3,7},{5,1},{7,3},{8,12},{10,14},{12... | collective-permute-start | bytes 786440 | tf_op jit(solution)/shard_map/ppermute | solution.py:387
  10.7 1.9 %collective-permute-start.3 = (bf16[512,256]{1,0:T(8,128)(2,1)}, bf16[512,256]{1,0:T(8,128)(2,1)S(1)}, u32[]{:S(2)}, u32[]{:S(2)}) collective-permute-start(bf16[512,256]{1,0:T(8,128)(2,1)} %m0.3), channel_id=1, source_target_pairs={{0,6},{2,0},{4,2},{6,4},{1,7},{3,1},{5,3},{7,5},{8,14},{10,8},{12,... | collective-permute-start | bytes 786440 | tf_op jit(solution)/shard_map/ppermute | solution.py:387
  12.6 4.8 %collective-permute-start.2 = (bf16[512,256]{1,0:T(8,128)(2,1)}, bf16[512,256]{1,0:T(8,128)(2,1)S(1)}, u32[]{:S(2)}, u32[]{:S(2)}) collective-permute-start(bf16[512,256]{1,0:T(8,128)(2,1)} %m0.3), channel_id=1, source_target_pairs={{0,2},{2,4},{4,6},{6,0},{1,3},{3,5},{5,7},{7,1},{8,10},{10,12},{12... | collective-permute-start | bytes 786440 | tf_op jit(solution)/shard_map/ppermute | solution.py:387
  18.4 3.4 %collective-permute-start = (bf16[48,256]{1,0:T(8,128)(2,1)S(1)}, bf16[48,256]{1,0:T(8,128)(2,1)S(1)}, u32[]{:S(2)}, u32[]{:S(2)}) collective-permute-start(bf16[48,256]{1,0:T(8,128)(2,1)S(1)} %get-tuple-element.31), channel_id=1, source_target_pairs={{0,8},{8,16},{16,24},{24,32},{32,40},{40,48},{48,56},{56,64},{64,7... | collective-permute-start | bytes 73736 | tf_op jit(solution)/shard_map/ppermute | solution.py:379
  21.8 4.6 %collective-permute-start.1 = (bf16[48,256]{1,0:T(8,128)(2,1)S(1)}, bf16[48,256]{1,0:T(8,128)(2,1)S(1)}, u32[]{:S(2)}, u32[]{:S(2)}) collective-permute-start(bf16[48,256]{1,0:T(8,128)(2,1)S(1)} %get-tuple-element.32), channel_id=1, source_target_pairs={{8,0},{16,8},{24,16},{32,24},{40,32},{48,40},{56,48},{64,56},{72,6... | collective-permute-start | bytes 73736 | tf_op jit(solution)/shard_map/ppermute | solution.py:380
  27.8 9.2 %collective-permute-done.refs_1_.before = bf16[48,256]{1,0:T(8,128)(2,1)S(1)} collective-permute-done((bf16[48,256]{1,0:T(8,128)(2,1)S(1)}, bf16[48,256]{1,0:T(8,128)(2,1)S(1)}, u32[]{:S(2)}, u32[]{:S(2)}) %collective-permute-start) | collective-permute-done | bytes 24608 | tf_op jit(solution)/shard_map/ppermute | solution.py:379
  37.6 7.2 %shard_map.112 = (f32[512,256]{1,0:T(8,128)S(1)}, bf16[256,512]{1,0:T(8,128)(2,1)S(1)}, f32[512,256]{1,0:T(8,128)S(1)}, bf16[256,512]{1,0:T(8,128)(2,1)S(1)}, bf...) custom-call(s32[5]{0:T(128)S(1)} %stack.55.refs_0_.place, bf16[48,256]{1,0:T(8,128)(2,1)} %copy-done.5, ...), custom_call_target="tpu_custom_call" | custom-call | tf_op jit(solution)/shard_map/pallas_call | solution.py:83
  46.1 1.9 %collective-permute-start.5 = (bf16[2,512,256]{2,1,0:T(8,128)(2,1)S(1)}, bf16[2,512,256]{2,1,0:T(8,128)(2,1)S(1)}, u32[]{:S(2)}, u32[]{:S(2)}) collective-permute-start(bf16[2,512,256]{2,1,0:T(8,128)(2,1)S(1)} %pad_maximum_fusion), channel_id=1, source_target_pairs={{0,1},{1,0},{2,3},{3,2},{4,5},{5,4},{6,7},{7,6},{8,9},{9,8},{10,11... | collective-permute-start | bytes 1572872 | tf_op jit(solution)/shard_map/ppermute | solution.py:392
  48.2 2.5 %collective-permute-start.6 = (bf16[2,512,256]{2,1,0:T(8,128)(2,1)S(1)}, bf16[2,512,256]{2,1,0:T(8,128)(2,1)S(1)}, u32[]{:S(2)}, u32[]{:S(2)}) collective-permute-start(bf16[2,512,256]{2,1,0:T(8,128)(2,1)S(1)} %pad_maximum_fusion.1), channel_id=1, source_target_pairs={{0,1},{1,0},{2,3},{3,2},{4,5},{5,4},{6,7},{7,6},{8,9},{9,8},{10,11... | collective-permute-start | bytes 1572872 | tf_op jit(solution)/shard_map/ppermute | solution.py:392
  55.5 6.0 %collective-permute-start.8 = (bf16[32,256]{1,0:T(8,128)(2,1)S(1)}, bf16[32,256]{1,0:T(8,128)(2,1)S(1)}, u32[]{:S(2)}, u32[]{:S(2)}) collective-permute-start(bf16[32,256]{1,0:T(8,128)(2,1)S(1)} %get-tuple-element.42), channel_id=1, source_target_pairs={{8,0},{16,8},{24,16},{32,24},{40,32},{48,40},{56,48},{64,56},{72,6... | collective-permute-start | bytes 49160 | tf_op jit(solution)/shard_map/ppermute | solution.py:380
  61.6 6.1 %collective-permute-done.8.refs_3_ = bf16[32,256]{1,0:T(8,128)(2,1)S(1)} collective-permute-done((bf16[32,256]{1,0:T(8,128)(2,1)S(1)}, bf16[32,256]{1,0:T(8,128)(2,1)S(1)}, u32[]{:S(2)}, u32[]{:S(2)}) %collective-permute-start.8) | collective-permute-done | bytes 16416 | tf_op jit(solution)/shard_map/ppermute | solution.py:380
  68.0 1.9 %collective-permute-start.11 = (bf16[512,256]{1,0:T(8,128)(2,1)S(1)}, bf16[512,256]{1,0:T(8,128)(2,1)S(1)}, u32[]{:S(2)}, u32[]{:S(2)}) collective-permute-start(bf16[512,256]{1,0:T(8,128)(2,1)S(1)} %shard_map.114.m0.up_row.refs_0_), channel_id=1, source_target_pairs={{0,4},{2,6},{4,0},{6,2},{1,5},{3,7},{5,1},{7,3},{8,12},{10,14},{12... | collective-permute-start | bytes 786440 | tf_op jit(solution)/shard_map/ppermute | solution.py:387
  69.9 8.0 %collective-permute-start.10 = (bf16[512,256]{1,0:T(8,128)(2,1)S(1)}, bf16[512,256]{1,0:T(8,128)(2,1)S(1)}, u32[]{:S(2)}, u32[]{:S(2)}) collective-permute-start(bf16[512,256]{1,0:T(8,128)(2,1)S(1)} %shard_map.114.m0.up_row.refs_0_), channel_id=1, source_target_pairs={{0,6},{2,0},{4,2},{6,4},{1,7},{3,1},{5,3},{7,5},{8,14},{10,8},{12,... | collective-permute-start | bytes 786440 | tf_op jit(solution)/shard_map/ppermute | solution.py:387
  77.9 1.9 %collective-permute-start.9 = (bf16[512,256]{1,0:T(8,128)(2,1)S(1)}, bf16[512,256]{1,0:T(8,128)(2,1)S(1)}, u32[]{:S(2)}, u32[]{:S(2)}) collective-permute-start(bf16[512,256]{1,0:T(8,128)(2,1)S(1)} %shard_map.114.m0.up_row.refs_0_), channel_id=1, source_target_pairs={{0,2},{2,4},{4,6},{6,0},{1,3},{3,5},{5,7},{7,1},{8,10},{10,12},{12... | collective-permute-start | bytes 786440 | tf_op jit(solution)/shard_map/ppermute | solution.py:387
  81.5 6.7 %all-to-all-start.1 = ((bf16[8,32,2048]{2,1,0:T(8,128)(2,1)}), bf16[8,32,2048]{2,1,0:T(8,128)(2,1)S(1)}, u32[]{:S(2)}, u32[]{:S(2)}) async-start(bf16[8,32,2048]{2,1,0:T(8,128)(2,1)} %bitcast.27), calls=%async_computation.1 | async-start | bytes 2097152 | tf_op jit(solution)/shard_map/all_to_all | solution.py:476
  88.3 2.1 %collective-permute-start.13 = (bf16[2,512,256]{2,1,0:T(8,128)(2,1)S(1)}, bf16[2,512,256]{2,1,0:T(8,128)(2,1)S(1)}, u32[]{:S(2)}, u32[]{:S(2)}) collective-permute-start(bf16[2,512,256]{2,1,0:T(8,128)(2,1)S(1)} %pad_maximum_fusion.3), channel_id=1, source_target_pairs={{0,1},{1,0},{2,3},{3,2},{4,5},{5,4},{6,7},{7,6},{8,9},{9,8},{10,11... | collective-permute-start | bytes 1572872 | tf_op jit(solution)/shard_map/ppermute | solution.py:392
  90.4 2.4 %collective-permute-start.12 = (bf16[2,512,256]{2,1,0:T(8,128)(2,1)S(1)}, bf16[2,512,256]{2,1,0:T(8,128)(2,1)S(1)}, u32[]{:S(2)}, u32[]{:S(2)}) collective-permute-start(bf16[2,512,256]{2,1,0:T(8,128)(2,1)S(1)} %pad_maximum_fusion.2), channel_id=1, source_target_pairs={{0,1},{1,0},{2,3},{3,2},{4,5},{5,4},{6,7},{7,6},{8,9},{9,8},{10,11... | collective-permute-start | bytes 1572872 | tf_op jit(solution)/shard_map/ppermute | solution.py:392
  94.4 2.8 %shard_map.116 = (bf16[256,2304]{1,0:T(8,128)(2,1)}, bf16[512,256]{1,0:T(8,128)(2,1)S(1)}) custom-call(s32[5]{0:T(128)S(1)} %stack.55.refs_0_.place, bf16[256,512]{1,0:T(8,128)(2,1)S(1)} %copy-done.13, bf16[512,256]{1,0:T(8,128)(2,1)S(1)} %shard_map.114.m0.up_row.refs_0_, bf16[512,256]{1,0:T(8,128)(2,1)S(1)} %collective-permute-done.9.m1, ...), custom_call_target="tpu_custom_call" | custom-call | flops 10000000000 | tf_op jit(solution)/shard_map/pallas_call | solution.py:54
  97.1 9.9 %collective-permute-start.15 = (bf16[16,256]{1,0:T(8,128)(2,1)S(1)}, bf16[16,256]{1,0:T(8,128)(2,1)S(1)}, u32[]{:S(2)}, u32[]{:S(2)}) collective-permute-start(bf16[16,256]{1,0:T(8,128)(2,1)S(1)} %get-tuple-element.58), channel_id=1, source_target_pairs={{8,0},{16,8},{24,16},{32,24},{40,32},{48,40},{56,48},{64,56},{72,6... | collective-permute-start | bytes 24584 | tf_op jit(solution)/shard_map/ppermute | solution.py:380
  107.1 1.9 %collective-permute-start.14 = (bf16[16,256]{1,0:T(8,128)(2,1)S(1)}, bf16[16,256]{1,0:T(8,128)(2,1)S(1)}, u32[]{:S(2)}, u32[]{:S(2)}) collective-permute-start(bf16[16,256]{1,0:T(8,128)(2,1)S(1)} %get-tuple-element.59), channel_id=1, source_target_pairs={{0,8},{8,16},{16,24},{24,32},{32,40},{40,48},{48,56},{56,64},{64,7... | collective-permute-start | bytes 24584 | tf_op jit(solution)/shard_map/ppermute | solution.py:379
  109.0 5.7 %collective-permute-done.14.refs_2_ = bf16[16,256]{1,0:T(8,128)(2,1)S(1)} collective-permute-done((bf16[16,256]{1,0:T(8,128)(2,1)S(1)}, bf16[16,256]{1,0:T(8,128)(2,1)S(1)}, u32[]{:S(2)}, u32[]{:S(2)}) %collective-permute-start.14) | collective-permute-done | bytes 8224 | tf_op jit(solution)/shard_map/ppermute | solution.py:379
  114.7 4.9 %all-to-all-start = ((bf16[8,32,2304]{2,1,0:T(8,128)(2,1)}), bf16[8,32,2304]{2,1,0:T(8,128)(2,1)S(1)}, u32[]{:S(2)}, u32[]{:S(2)}) async-start(bf16[8,32,2304]{2,1,0:T(8,128)(2,1)} %bitcast.26), calls=%async_computation | async-start | bytes 2359296 | tf_op jit(solution)/shard_map/all_to_all | solution.py:497
  121.0 13.4 %all-to-all-done.pieces = bf16[8,32,2304]{2,1,0:T(8,128)(2,1)S(1)} async-done(((bf16[8,32,2304]{2,1,0:T(8,128)(2,1)}), bf16[8,32,2304]{2,1,0:T(8,128)(2,1)S(1)}, u32[]{:S(2)}, u32[]{:S(2)}) %all-to-all-start) | async-done | bytes 1179680 | tf_op jit(solution)/shard_map/all_to_all | solution.py:497
  134.6 21.8 %all_to_all.15.refs_1_ = bf16[8,4,5632]{2,1,0:T(4,128)(2,1)S(1)} all-to-all(bf16[8,4,5632]{2,1,0:T(4,128)(2,1)S(1)} %shard_map.119), channel_id=1, replica_groups=mesh['y'=8,'zl'=2,'x'=4,'zh'=4,'core'=2] {'y'}, dimensions={0} | all-to-all | bytes 720896 | tf_op jit(solution)/shard_map/all_to_all | solution.py:503
  (58 shorter events, 15.5 us)
Async XLA Ops:
  0.6 44.2 %collective-permute-start.4 = (bf16[512,256]{1,0:T(8,128)(2,1)}, bf16[512,256]{1,0:T(8,128)(2,1)S(1)}, u32[]{:S(2)}, u32[]{:S(2)}) collective-permute-start(bf16[512,256]{1,0:T(8,128)(2,1)} %m0.3), channel_id=1, source_target_pairs={{0,4},{2,6},{4,0},{6,2},{1,5},{3,7},{5,1},{7,3},{8,12},{10,14},{12... | collective-permute-start | bytes 786440 | tf_op jit(solution)/shard_map/ppermute | solution.py:387
  10.7 34.2 %collective-permute-start.3 = (bf16[512,256]{1,0:T(8,128)(2,1)}, bf16[512,256]{1,0:T(8,128)(2,1)S(1)}, u32[]{:S(2)}, u32[]{:S(2)}) collective-permute-start(bf16[512,256]{1,0:T(8,128)(2,1)} %m0.3), channel_id=1, source_target_pairs={{0,6},{2,0},{4,2},{6,4},{1,7},{3,1},{5,3},{7,5},{8,14},{10,8},{12,... | collective-permute-start | bytes 786440 | tf_op jit(solution)/shard_map/ppermute | solution.py:387
  12.6 32.2 %collective-permute-start.2 = (bf16[512,256]{1,0:T(8,128)(2,1)}, bf16[512,256]{1,0:T(8,128)(2,1)S(1)}, u32[]{:S(2)}, u32[]{:S(2)}) collective-permute-start(bf16[512,256]{1,0:T(8,128)(2,1)} %m0.3), channel_id=1, source_target_pairs={{0,2},{2,4},{4,6},{6,0},{1,3},{3,5},{5,7},{7,1},{8,10},{10,12},{12... | collective-permute-start | bytes 786440 | tf_op jit(solution)/shard_map/ppermute | solution.py:387
  18.4 18.6 %collective-permute-start = (bf16[48,256]{1,0:T(8,128)(2,1)S(1)}, bf16[48,256]{1,0:T(8,128)(2,1)S(1)}, u32[]{:S(2)}, u32[]{:S(2)}) collective-permute-start(bf16[48,256]{1,0:T(8,128)(2,1)S(1)} %get-tuple-element.31), channel_id=1, source_target_pairs={{0,8},{8,16},{16,24},{24,32},{32,40},{40,48},{48,56},{56,64},{64,7... | collective-permute-start | bytes 73736 | tf_op jit(solution)/shard_map/ppermute | solution.py:379
  21.8 15.2 %collective-permute-start.1 = (bf16[48,256]{1,0:T(8,128)(2,1)S(1)}, bf16[48,256]{1,0:T(8,128)(2,1)S(1)}, u32[]{:S(2)}, u32[]{:S(2)}) collective-permute-start(bf16[48,256]{1,0:T(8,128)(2,1)S(1)} %get-tuple-element.32), channel_id=1, source_target_pairs={{8,0},{16,8},{24,16},{32,24},{40,32},{48,40},{56,48},{64,56},{72,6... | collective-permute-start | bytes 73736 | tf_op jit(solution)/shard_map/ppermute | solution.py:380
  37.6 14.7 %copy-start.2 = (bf16[2,256,2048]{2,1,0:T(8,128)(2,1)S(1)}, bf16[2,256,2048]{2,1,0:T(8,128)(2,1)}, u32[]{:S(2)}) copy-start(bf16[2,256,2048]{2,1,0:T(8,128)(2,1)} %weights.3) | copy-start | bytes 6291460
  46.1 4.6 %collective-permute-start.5 = (bf16[2,512,256]{2,1,0:T(8,128)(2,1)S(1)}, bf16[2,512,256]{2,1,0:T(8,128)(2,1)S(1)}, u32[]{:S(2)}, u32[]{:S(2)}) collective-permute-start(bf16[2,512,256]{2,1,0:T(8,128)(2,1)S(1)} %pad_maximum_fusion), channel_id=1, source_target_pairs={{0,1},{1,0},{2,3},{3,2},{4,5},{5,4},{6,7},{7,6},{8,9},{9,8},{10,11... | collective-permute-start | bytes 1572872 | tf_op jit(solution)/shard_map/ppermute | solution.py:392
  48.1 19.5 %copy-start.4 = (bf16[2,9,256]{2,1,0:T(8,128)(2,1)S(1)}, bf16[2,9,256]{2,1,0:T(8,128)(2,1)}, u32[]{:S(2)}) copy-start(bf16[2,9,256]{2,1,0:T(8,128)(2,1)} %copy.12.refs_9_.refs_4_.conv) | copy-start | bytes 27652
  48.1 31.7 %copy-start.1 = (bf16[512,256]{1,0:T(8,128)(2,1)S(1)}, bf16[512,256]{1,0:T(8,128)(2,1)}, u32[]{:S(2)}) copy-start(bf16[512,256]{1,0:T(8,128)(2,1)} %saved.1) | copy-start | bytes 786436
  48.2 31.7 %copy-start.6 = (bf16[48,256]{1,0:T(8,128)(2,1)S(1)}, bf16[48,256]{1,0:T(8,128)(2,1)}, u32[]{:S(2)}) copy-start(bf16[48,256]{1,0:T(8,128)(2,1)} %copy-done.5) | copy-start | bytes 73732
  48.2 31.7 %copy-start.8 = (bf16[48,256]{1,0:T(8,128)(2,1)S(1)}, bf16[48,256]{1,0:T(8,128)(2,1)}, u32[]{:S(2)}) copy-start(bf16[48,256]{1,0:T(8,128)(2,1)} %copy-done.7) | copy-start | bytes 73732
  48.2 4.1 %collective-permute-start.6 = (bf16[2,512,256]{2,1,0:T(8,128)(2,1)S(1)}, bf16[2,512,256]{2,1,0:T(8,128)(2,1)S(1)}, u32[]{:S(2)}, u32[]{:S(2)}) collective-permute-start(bf16[2,512,256]{2,1,0:T(8,128)(2,1)S(1)} %pad_maximum_fusion.1), channel_id=1, source_target_pairs={{0,1},{1,0},{2,3},{3,2},{4,5},{5,4},{6,7},{7,6},{8,9},{9,8},{10,11... | collective-permute-start | bytes 1572872 | tf_op jit(solution)/shard_map/ppermute | solution.py:392
  53.6 8.0 %collective-permute-start.7 = (bf16[32,256]{1,0:T(8,128)(2,1)S(1)}, bf16[32,256]{1,0:T(8,128)(2,1)S(1)}, u32[]{:S(2)}, u32[]{:S(2)}) collective-permute-start(bf16[32,256]{1,0:T(8,128)(2,1)S(1)} %get-tuple-element.41), channel_id=1, source_target_pairs={{0,8},{8,16},{16,24},{24,32},{32,40},{40,48},{48,56},{56,64},{64,7... | collective-permute-start | bytes 49160 | tf_op jit(solution)/shard_map/ppermute | solution.py:379
  55.5 12.1 %collective-permute-start.8 = (bf16[32,256]{1,0:T(8,128)(2,1)S(1)}, bf16[32,256]{1,0:T(8,128)(2,1)S(1)}, u32[]{:S(2)}, u32[]{:S(2)}) collective-permute-start(bf16[32,256]{1,0:T(8,128)(2,1)S(1)} %get-tuple-element.42), channel_id=1, source_target_pairs={{8,0},{16,8},{24,16},{32,24},{40,32},{48,40},{56,48},{64,56},{72,6... | collective-permute-start | bytes 49160 | tf_op jit(solution)/shard_map/ppermute | solution.py:380
  68.0 20.2 %collective-permute-start.11 = (bf16[512,256]{1,0:T(8,128)(2,1)S(1)}, bf16[512,256]{1,0:T(8,128)(2,1)S(1)}, u32[]{:S(2)}, u32[]{:S(2)}) collective-permute-start(bf16[512,256]{1,0:T(8,128)(2,1)S(1)} %shard_map.114.m0.up_row.refs_0_), channel_id=1, source_target_pairs={{0,4},{2,6},{4,0},{6,2},{1,5},{3,7},{5,1},{7,3},{8,12},{10,14},{12... | collective-permute-start | bytes 786440 | tf_op jit(solution)/shard_map/ppermute | solution.py:387
  69.9 18.3 %collective-permute-start.10 = (bf16[512,256]{1,0:T(8,128)(2,1)S(1)}, bf16[512,256]{1,0:T(8,128)(2,1)S(1)}, u32[]{:S(2)}, u32[]{:S(2)}) collective-permute-start(bf16[512,256]{1,0:T(8,128)(2,1)S(1)} %shard_map.114.m0.up_row.refs_0_), channel_id=1, source_target_pairs={{0,6},{2,0},{4,2},{6,4},{1,7},{3,1},{5,3},{7,5},{8,14},{10,8},{12,... | collective-permute-start | bytes 786440 | tf_op jit(solution)/shard_map/ppermute | solution.py:387
  77.9 12.4 %collective-permute-start.9 = (bf16[512,256]{1,0:T(8,128)(2,1)S(1)}, bf16[512,256]{1,0:T(8,128)(2,1)S(1)}, u32[]{:S(2)}, u32[]{:S(2)}) collective-permute-start(bf16[512,256]{1,0:T(8,128)(2,1)S(1)} %shard_map.114.m0.up_row.refs_0_), channel_id=1, source_target_pairs={{0,2},{2,4},{4,6},{6,0},{1,3},{3,5},{5,7},{7,1},{8,10},{10,12},{12... | collective-permute-start | bytes 786440 | tf_op jit(solution)/shard_map/ppermute | solution.py:387
  81.5 12.9 %copy-start.11 = (f32[512,256]{1,0:T(8,128)S(1)}, f32[512,256]{1,0:T(8,128)}, u32[]{:S(2)}) copy-start(f32[512,256]{1,0:T(8,128)} %copy-done.10) | copy-start | bytes 1572868
  81.5 33.2 %all-to-all-start.1 = ((bf16[8,32,2048]{2,1,0:T(8,128)(2,1)}), bf16[8,32,2048]{2,1,0:T(8,128)(2,1)S(1)}, u32[]{:S(2)}, u32[]{:S(2)}) async-start(bf16[8,32,2048]{2,1,0:T(8,128)(2,1)} %bitcast.27), calls=%async_computation.1 | async-start | bytes 2097152 | tf_op jit(solution)/shard_map/all_to_all | solution.py:476
  88.3 4.5 %collective-permute-start.13 = (bf16[2,512,256]{2,1,0:T(8,128)(2,1)S(1)}, bf16[2,512,256]{2,1,0:T(8,128)(2,1)S(1)}, u32[]{:S(2)}, u32[]{:S(2)}) collective-permute-start(bf16[2,512,256]{2,1,0:T(8,128)(2,1)S(1)} %pad_maximum_fusion.3), channel_id=1, source_target_pairs={{0,1},{1,0},{2,3},{3,2},{4,5},{5,4},{6,7},{7,6},{8,9},{9,8},{10,11... | collective-permute-start | bytes 1572872 | tf_op jit(solution)/shard_map/ppermute | solution.py:392
  90.4 3.9 %collective-permute-start.12 = (bf16[2,512,256]{2,1,0:T(8,128)(2,1)S(1)}, bf16[2,512,256]{2,1,0:T(8,128)(2,1)S(1)}, u32[]{:S(2)}, u32[]{:S(2)}) collective-permute-start(bf16[2,512,256]{2,1,0:T(8,128)(2,1)S(1)} %pad_maximum_fusion.2), channel_id=1, source_target_pairs={{0,1},{1,0},{2,3},{3,2},{4,5},{5,4},{6,7},{7,6},{8,9},{9,8},{10,11... | collective-permute-start | bytes 1572872 | tf_op jit(solution)/shard_map/ppermute | solution.py:392
  97.1 11.9 %collective-permute-start.15 = (bf16[16,256]{1,0:T(8,128)(2,1)S(1)}, bf16[16,256]{1,0:T(8,128)(2,1)S(1)}, u32[]{:S(2)}, u32[]{:S(2)}) collective-permute-start(bf16[16,256]{1,0:T(8,128)(2,1)S(1)} %get-tuple-element.58), channel_id=1, source_target_pairs={{8,0},{16,8},{24,16},{32,24},{40,32},{48,40},{56,48},{64,56},{72,6... | collective-permute-start | bytes 24584 | tf_op jit(solution)/shard_map/ppermute | solution.py:380
  107.1 7.7 %collective-permute-start.14 = (bf16[16,256]{1,0:T(8,128)(2,1)S(1)}, bf16[16,256]{1,0:T(8,128)(2,1)S(1)}, u32[]{:S(2)}, u32[]{:S(2)}) collective-permute-start(bf16[16,256]{1,0:T(8,128)(2,1)S(1)} %get-tuple-element.59), channel_id=1, source_target_pairs={{0,8},{8,16},{16,24},{24,32},{32,40},{40,48},{48,56},{56,64},{64,7... | collective-permute-start | bytes 24584 | tf_op jit(solution)/shard_map/ppermute | solution.py:379
  114.7 19.7 %all-to-all-start = ((bf16[8,32,2304]{2,1,0:T(8,128)(2,1)}), bf16[8,32,2304]{2,1,0:T(8,128)(2,1)S(1)}, u32[]{:S(2)}, u32[]{:S(2)}) async-start(bf16[8,32,2304]{2,1,0:T(8,128)(2,1)} %bitcast.26), calls=%async_computation | async-start | bytes 2359296 | tf_op jit(solution)/shard_map/all_to_all | solution.py:497
  (8 other events, 51.4 us)
